TPU v7x, 32 devices: a whole 2x2x4 slice. The times are simulated.
32 devices in a mesh: dp: 8 (over z, y), seq: 4 (over x, core).
Axes of the slice: x: 2, y: 2, z: 4, core: 2. Of those that a mesh axis runs over, the one named last changes fastest.
Arguments:
- pixels: bfloat16 [32, 256, 768], P('dp', 'seq'), may hold values from -6 to 6
- block_mask: int32 [32, 256], P('dp', 'seq'), may hold values from 0 to 1, as said below
- targets: bfloat16 [32, 256, 768], P('dp', 'seq'), may hold values from -6 to 6
- square_weights: float32 [3, 768, 768], P(None, 'dp'), may hold values from -0.21875 to 0.21875
- joint_weights: float32 [768, 2304], P('dp'), may hold values from -0.21875 to 0.21875
- expand_weights: float32 [768, 3072], P('dp'), may hold values from -0.21875 to 0.21875
- reduce_weights: float32 [3072, 768], P('dp'), may hold values from -0.109375 to 0.109375
- vectors: float32 [20, 768], P(None, 'dp'), may hold values from -8 to 8, as said below
- square_moment: float32 [3, 768, 768], P(None, 'dp'), may hold values from -6.1035156e-05 to 6.1035156e-05
- joint_moment: float32 [768, 2304], P('dp'), may hold values from -6.1035156e-05 to 6.1035156e-05
- expand_moment: float32 [768, 3072], P('dp'), may hold values from -6.1035156e-05 to 6.1035156e-05
- reduce_moment: float32 [3072, 768], P('dp'), may hold values from -6.1035156e-05 to 6.1035156e-05
- vector_moment: float32 [20, 768], P(None, 'dp'), may hold values from -0.00018310547 to 0.00018310547
- square_variance: float32 [3, 768, 768], P(None, 'dp'), may hold values from 1.2087666e-12 to 4.8350664e-12
- joint_variance: float32 [768, 2304], P('dp'), may hold values from 1.2087666e-12 to 4.8350664e-12
- expand_variance: float32 [768, 3072], P('dp'), may hold values from 1.2087666e-12 to 4.8350664e-12
- reduce_variance: float32 [3072, 768], P('dp'), may hold values from 1.2087666e-12 to 4.8350664e-12
- vector_variance: float32 [20, 768], P(None, 'dp'), may hold values from 1.0878899e-11 to 4.3515597e-11
Outputs:
- masked_loss: float32 [], replicated
- gradient_norm: float32 [], replicated
- moment_square: float32 [3, 768, 768], P(None, 'dp')
- variance_square: float32 [3, 768, 768], P(None, 'dp')
- master_square: float32 [3, 768, 768], P(None, 'dp')
- moment_joint: float32 [768, 2304], P('dp')
- variance_joint: float32 [768, 2304], P('dp')
- master_joint: float32 [768, 2304], P('dp')
- moment_expand: float32 [768, 3072], P('dp')
- variance_expand: float32 [768, 3072], P('dp')
- master_expand: float32 [768, 3072], P('dp')
- moment_reduce: float32 [3072, 768], P('dp')
- variance_reduce: float32 [3072, 768], P('dp')
- master_reduce: float32 [3072, 768], P('dp')
- moment_vector: float32 [20, 768], P(None, 'dp')
- variance_vector: float32 [20, 768], P(None, 'dp')
- master_vector: float32 [20, 768], P(None, 'dp')
Inputs may be any that keep to these rules, and one draw needn't show every extreme that they name: `block_mask`: 1 marks a masked patch; patches are masked in whole 2 x 2 blocks of the 14 x 14 grid; the class and padding slots are 0. `vectors`: gains and layer scales are positive.
All inputs are finite; a program needn't handle non-finite values.
Results may differ from a plain program's by a relative error of at most 0.011.
Values may be sent and summed in bfloat16 or wider, within the bound.
No kernel may reach another device: no remote copies, remote signals or barrier semaphores. Data moves between devices by JAX's collectives and lax.ppermute only.
A program may use at most 128 MiB of HBM per device.

v0:
```python
from functools import partial
import math

import jax
import jax.numpy as jnp
from jax import lax
from jax.sharding import PartitionSpec as P

HEADS = 12
GRID = 14
MICRO = 2
IMG_MB = 2


norm_eps = 1e-06
beta_one = 0.9
beta_two = 0.999
adam_eps = 1e-08
adam_step = 10.0
matrix_rate = 0.05
vector_rate = 0.3
weight_decay = 0.05
clip_limit = 0.1


def positions(slot_float, features):
    column = jnp.arange(features)
    frequency = jnp.exp((2 * (column // 2)).astype(jnp.float32) * (-math.log(10000.0) / features))
    angle = slot_float[:, None] * frequency[None, :]
    return jnp.where(column % 2 == 0, jnp.sin(angle), jnp.cos(angle))


def layer_norm(stream, gain, shift):
    centred = stream - jnp.mean(stream, -1, keepdims=True)
    inverse = lax.rsqrt(jnp.mean(centred * centred, -1, keepdims=True) + norm_eps)
    normed = centred * inverse
    return (normed * gain + shift, normed, inverse)


def norm_back(upstream, normed, inverse, gain):
    scaled = upstream * gain
    moved = inverse * (
        scaled
        - jnp.mean(scaled, -1, keepdims=True)
        - normed * jnp.mean(scaled * normed, -1, keepdims=True)
    )
    return (moved, jnp.sum(upstream * normed, 0), jnp.sum(upstream, 0))


def dense(left, right):
    return jnp.dot(left, right, preferred_element_type=jnp.float32)


def dense_back(upstream, weight):
    return lax.dot_general(
        upstream, weight, (((1,), (1,)), ((), ())), preferred_element_type=jnp.float32
    )


def weight_grad(inputs, upstream):
    return lax.dot_general(
        inputs, upstream, (((0,), (0,)), ((), ())), preferred_element_type=jnp.float32
    )


def smooth_terms(residual):
    return jnp.where(jnp.abs(residual) < 2.0, 0.25 * residual * residual, jnp.abs(residual) - 1.0)


def adam(weight, moment, variance, grad, rate, decay):
    moment_new = beta_one * moment + (1.0 - beta_one) * grad
    variance_new = beta_two * variance + (1.0 - beta_two) * grad * grad
    corrected = (
        moment_new
        / (1.0 - beta_one**adam_step)
        / (jnp.sqrt(variance_new / (1.0 - beta_two**adam_step)) + adam_eps)
    )
    return (moment_new, variance_new, weight - rate * (corrected + decay * weight))


def fetch(shards):
    square_low, joint_low, expand_low, reduce_low, vector_low = shards
    return (
        lax.all_gather(square_low, "dp", axis=1, tiled=True),
        lax.all_gather(joint_low, "dp", axis=0, tiled=True),
        lax.all_gather(expand_low, "dp", axis=0, tiled=True),
        lax.all_gather(reduce_low, "dp", axis=0, tiled=True),
        lax.all_gather(vector_low, "dp", axis=1, tiled=True),
    )


def reduce_grads(grads):
    square_grad, joint_grad, expand_grad, reduce_grad, vector_grad = grads
    square_grad, joint_grad, expand_grad, reduce_grad, vector_grad = (
        lax.psum_scatter(square_grad, "dp", scatter_dimension=1, tiled=True),
        lax.psum_scatter(joint_grad, "dp", scatter_dimension=0, tiled=True),
        lax.psum_scatter(expand_grad, "dp", scatter_dimension=0, tiled=True),
        lax.psum_scatter(reduce_grad, "dp", scatter_dimension=0, tiled=True),
        lax.psum_scatter(vector_grad, "dp", scatter_dimension=1, tiled=True),
    )
    return lax.psum((square_grad, joint_grad, expand_grad, reduce_grad, vector_grad), "seq")


def micro_step(pixels, block_mask, targets, weights, count):
    square_w, joint_w, expand_w, reduce_w, vector_low = weights
    vector_w = vector_low.astype(jnp.float32)
    images, length, _ = pixels.shape
    features = square_w.shape[2]
    head_size = features // HEADS
    total_rows = images * length
    patches = GRID * GRID
    slot_index = lax.axis_index("seq") * length + jnp.arange(length)
    is_class = (slot_index == patches)[None, :, None]
    masked = block_mask.astype(jnp.float32)[:, :, None]
    take_mask = jnp.where(is_class, 0.0, masked)
    take_embed = jnp.where(is_class, 0.0, 1.0 - masked)
    flat_pixels = pixels.reshape(total_rows, -1)
    embedded = dense(flat_pixels, square_w[0]).reshape(images, length, features) + vector_w[2]
    stream_zero = jnp.where(is_class, vector_w[0], jnp.where(masked > 0.5, vector_w[1], embedded))
    stream_zero = (stream_zero + positions(slot_index.astype(jnp.float32), features)).reshape(
        total_rows, features
    )
    normed_one, unit_one, inverse_one = layer_norm(stream_zero, vector_w[3], vector_w[4])
    input_one = normed_one.astype(jnp.bfloat16)
    joint = dense(input_one, joint_w) + jnp.concatenate(
        [vector_w[5], jnp.zeros_like(vector_w[5]), vector_w[6]]
    )
    joint_low = joint.astype(jnp.bfloat16).reshape(images, length, 3 * features)
    query = joint_low[:, :, :features].reshape(images, length, HEADS, head_size)
    keys_local = joint_low[:, :, features : 2 * features]
    values_local = joint_low[:, :, 2 * features :]
    keys_all, values_all = (
        lax.all_gather(keys_local, "seq", axis=1, tiled=True),
        lax.all_gather(values_local, "seq", axis=1, tiled=True),
    )
    slots = keys_all.shape[1]
    keys_heads = keys_all.reshape(images, slots, HEADS, head_size)
    values_heads = values_all.reshape(images, slots, HEADS, head_size)
    key_valid = jnp.arange(slots) <= patches
    scale = head_size ** (-0.5)

    def scores_of():
        raw = (
            jnp.einsum("blhd,bkhd->bhlk", query, keys_heads, preferred_element_type=jnp.float32)
            * scale
        )
        return jnp.where(key_valid, raw, -1e30)

    scores = scores_of()
    top = jnp.max(scores, -1, keepdims=True)
    log_total = top + jnp.log(jnp.sum(jnp.exp(scores - top), -1, keepdims=True))
    probs_low = jnp.exp(scores - log_total).astype(jnp.bfloat16)
    attended = jnp.einsum(
        "bhlk,bkhd->blhd", probs_low, values_heads, preferred_element_type=jnp.float32
    )
    attended = attended.reshape(total_rows, features).astype(jnp.bfloat16)
    branch = dense(attended, square_w[1]) + vector_w[7]
    stream_one = stream_zero + vector_w[8] * branch
    normed_two, unit_two, inverse_two = layer_norm(stream_one, vector_w[9], vector_w[10])
    input_two = normed_two.astype(jnp.bfloat16)
    inner = dense(input_two, expand_w) + vector_w[16:].reshape(-1)
    activated, gelu_pull = jax.vjp(partial(jax.nn.gelu, approximate=False), inner)
    active_low = activated.astype(jnp.bfloat16)
    mlp_out = dense(active_low, reduce_w) + vector_w[11]
    stream_two = stream_one + vector_w[12] * mlp_out
    normed_three, unit_three, inverse_three = layer_norm(stream_two, vector_w[13], vector_w[14])
    input_three = normed_three.astype(jnp.bfloat16)
    predicted = dense(input_three, square_w[2]) + vector_w[15]
    residual = predicted - targets.reshape(total_rows, features).astype(jnp.float32)
    row_mask = masked.reshape(total_rows, 1)
    loss_part = jnp.sum(row_mask * smooth_terms(residual))
    grad_pred = row_mask * jnp.clip(0.5 * residual, -1.0, 1.0) / count
    pred_low = grad_pred.astype(jnp.bfloat16)
    head_grad = weight_grad(input_three, pred_low)
    grad_head_bias = jnp.sum(grad_pred, 0)
    grad_stream_two, grad_gain_three, grad_shift_three = norm_back(
        dense_back(pred_low, square_w[2]), unit_three, inverse_three, vector_w[13]
    )
    grad_scale_two = jnp.sum(grad_stream_two * mlp_out, 0)
    grad_mlp = grad_stream_two * vector_w[12]
    grad_mlp_bias = jnp.sum(grad_mlp, 0)
    mlp_low = grad_mlp.astype(jnp.bfloat16)
    reduce_grad = weight_grad(active_low, mlp_low)
    grad_inner = gelu_pull(dense_back(mlp_low, reduce_w))[0]
    grad_inner_bias = jnp.sum(grad_inner, 0)
    inner_low = grad_inner.astype(jnp.bfloat16)
    expand_grad = weight_grad(input_two, inner_low)
    grad_normed_two, grad_gain_two, grad_shift_two = norm_back(
        dense_back(inner_low, expand_w), unit_two, inverse_two, vector_w[9]
    )
    grad_stream_one = grad_stream_two + grad_normed_two
    grad_scale_one = jnp.sum(grad_stream_one * branch, 0)
    grad_branch = grad_stream_one * vector_w[8]
    grad_out_bias = jnp.sum(grad_branch, 0)
    branch_low = grad_branch.astype(jnp.bfloat16)
    out_grad = weight_grad(attended, branch_low)
    grad_attended = dense_back(branch_low, square_w[1]).astype(jnp.bfloat16)
    grad_attended = grad_attended.reshape(images, length, HEADS, head_size)
    probs = jnp.exp(scores_of() - log_total)
    probs_again = probs.astype(jnp.bfloat16)
    grad_probs = jnp.einsum(
        "blhd,bkhd->bhlk", grad_attended, values_heads, preferred_element_type=jnp.float32
    )
    grad_scores = (probs * (grad_probs - jnp.sum(probs * grad_probs, -1, keepdims=True))).astype(
        jnp.bfloat16
    )
    grad_query = (
        jnp.einsum("bhlk,bkhd->blhd", grad_scores, keys_heads, preferred_element_type=jnp.float32)
        * scale
    )
    grad_keys = (
        jnp.einsum("bhlk,blhd->bkhd", grad_scores, query, preferred_element_type=jnp.float32)
        * scale
    )
    grad_values = jnp.einsum(
        "bhlk,blhd->bkhd", probs_again, grad_attended, preferred_element_type=jnp.float32
    )
    grad_keys_own, grad_values_own = (
        lax.psum_scatter(
            grad_keys.reshape(images, slots, features).astype(jnp.bfloat16),
            "seq",
            scatter_dimension=1,
            tiled=True,
        ).astype(jnp.float32),
        lax.psum_scatter(
            grad_values.reshape(images, slots, features).astype(jnp.bfloat16),
            "seq",
            scatter_dimension=1,
            tiled=True,
        ).astype(jnp.float32),
    )
    grad_query = grad_query.reshape(total_rows, features)
    grad_values_own = grad_values_own.reshape(total_rows, features)
    grad_joint = jnp.concatenate(
        [grad_query, grad_keys_own.reshape(total_rows, features), grad_values_own], -1
    )
    joint_low_grad = grad_joint.astype(jnp.bfloat16)
    joint_grad = weight_grad(input_one, joint_low_grad)
    grad_normed_one, grad_gain_one, grad_shift_one = norm_back(
        dense_back(joint_low_grad, joint_w), unit_one, inverse_one, vector_w[3]
    )
    grad_stream_zero = grad_stream_one + grad_normed_one
    grad_zero = grad_stream_zero.reshape(images, length, features)
    grad_class = jnp.sum(jnp.where(is_class, grad_zero, 0.0), (0, 1))
    grad_token = jnp.sum(grad_zero * take_mask, (0, 1))
    grad_embed = grad_zero * take_embed
    grad_patch_bias = jnp.sum(grad_embed, (0, 1))
    patch_grad = weight_grad(
        flat_pixels, grad_embed.reshape(total_rows, features).astype(jnp.bfloat16)
    )
    vector_grad = jnp.concatenate(
        [
            jnp.stack(
                [
                    grad_class,
                    grad_token,
                    grad_patch_bias,
                    grad_gain_one,
                    grad_shift_one,
                    jnp.sum(grad_query, 0),
                    jnp.sum(grad_values_own, 0),
                    grad_out_bias,
                    grad_scale_one,
                    grad_gain_two,
                    grad_shift_two,
                    grad_mlp_bias,
                    grad_scale_two,
                    grad_gain_three,
                    grad_shift_three,
                    grad_head_bias,
                ]
            ),
            grad_inner_bias.reshape(-1, features),
        ],
        0,
    )
    square_grad = jnp.stack([patch_grad, out_grad, head_grad])
    return (loss_part, (square_grad, joint_grad, expand_grad, reduce_grad, vector_grad))


def local(
    pixels,
    block_mask,
    targets,
    square_weights,
    joint_weights,
    expand_weights,
    reduce_weights,
    vectors,
    square_moment,
    joint_moment,
    expand_moment,
    reduce_moment,
    vector_moment,
    square_variance,
    joint_variance,
    expand_variance,
    reduce_variance,
    vector_variance,
):
    masters = (square_weights, joint_weights, expand_weights, reduce_weights, vectors)
    count = lax.psum(jnp.sum(block_mask.astype(jnp.float32)), ("dp", "seq"))
    shards_low = tuple((master.astype(jnp.bfloat16) for master in masters))
    loss_part = jnp.zeros((), jnp.float32)
    summed = None
    for index in range(MICRO):
        gathered = fetch(shards_low)
        begin = index * IMG_MB
        part, grads = micro_step(
            pixels[begin : begin + IMG_MB],
            block_mask[begin : begin + IMG_MB],
            targets[begin : begin + IMG_MB],
            gathered,
            count,
        )
        loss_part = loss_part + part
        grads = reduce_grads(grads)
        summed = (
            grads if summed is None else tuple((left + right for left, right in zip(summed, grads)))
        )
    squares = sum((jnp.sum(grad * grad) for grad in summed))
    norm = jnp.sqrt(lax.psum(squares, "dp"))
    loss = lax.psum(loss_part, ("dp", "seq")) / count
    factor = clip_limit / jnp.maximum(norm, clip_limit)
    sq_m, sq_v, sq_w = adam(
        square_weights,
        square_moment,
        square_variance,
        summed[0] * factor,
        matrix_rate,
        weight_decay,
    )
    jt_m, jt_v, jt_w = adam(
        joint_weights, joint_moment, joint_variance, summed[1] * factor, matrix_rate, weight_decay
    )
    ex_m, ex_v, ex_w = adam(
        expand_weights,
        expand_moment,
        expand_variance,
        summed[2] * factor,
        matrix_rate,
        weight_decay,
    )
    rd_m, rd_v, rd_w = adam(
        reduce_weights,
        reduce_moment,
        reduce_variance,
        summed[3] * factor,
        matrix_rate,
        weight_decay,
    )
    vc_m, vc_v, vc_w = adam(
        vectors, vector_moment, vector_variance, summed[4] * factor, vector_rate, 0.0
    )
    return (
        loss,
        norm,
        sq_m,
        sq_v,
        sq_w,
        jt_m,
        jt_v,
        jt_w,
        ex_m,
        ex_v,
        ex_w,
        rd_m,
        rd_v,
        rd_w,
        vc_m,
        vc_v,
        vc_w,
    )


def solution(mesh):
    in_specs = (
        P("dp", "seq", None),
        P("dp", "seq"),
        P("dp", "seq", None),
        P(None, "dp", None),
        P("dp", None),
        P("dp", None),
        P("dp", None),
        P(None, "dp"),
        P(None, "dp", None),
        P("dp", None),
        P("dp", None),
        P("dp", None),
        P(None, "dp"),
        P(None, "dp", None),
        P("dp", None),
        P("dp", None),
        P("dp", None),
        P(None, "dp"),
    )
    out_specs = (
        P(),
        P(),
        P(None, "dp", None),
        P(None, "dp", None),
        P(None, "dp", None),
        P("dp", None),
        P("dp", None),
        P("dp", None),
        P("dp", None),
        P("dp", None),
        P("dp", None),
        P("dp", None),
        P("dp", None),
        P("dp", None),
        P(None, "dp"),
        P(None, "dp"),
        P(None, "dp"),
    )
    return jax.shard_map(local, mesh=mesh, in_specs=in_specs, out_specs=out_specs, check_vma=False)
```

profile of v0, /device:TPU:0, one launch (start us, length us, event | category | flops | bytes accessed | tf_op | source)
XLA Modules:
  0.0 1280.4 jit_solution(6879153318110326323)
XLA Ops:
  7.3 2.1 convert_element_type.207
  13.4 33.1 %all-gather = bf16[8,96,20]{1,2,0:T(8,128)(2,1)S(1)} all-gather(bf16[1,96,20]{1,2,0:T(8,128)(2,1)S(1)} %convert_bitcast_fusion), channel_id=1, replica_groups=mesh['dp'=8,'seq'=4] {'dp'}, dimensions={0}, use_global_device_ids=true | all-gather | bytes 34560 | tf_op jit(solution)/shard_map/all_gather | solution.py:88
  47.3 41.5 %psum.92 = f32[]{:T(128)} all-reduce(f32[]{:T(128)} %convert_reduce_fusion.2), channel_id=1, replica_groups=mesh['dp'=8,'seq'=4] {'dp','seq'}, use_global_device_ids=true, to_apply=%region_20.21 | all-reduce | flops 1 | bytes 8 | tf_op jit(solution)/shard_map/psum | solution.py:302
  97.4 48.5 %all-gather.8.cloned.1.call-done = bf16[768,2304]{1,0:T(8,128)(2,1)} async-done(((bf16[96,2304]{1,0:T(8,128)(2,1)}), bf16[768,2304]{1,0:T(8,128)(2,1)}) %all-gather.8.cloned.1.call-update) | async-done | bytes 3538960 | tf_op jit(solution)/shard_map/all_gather | solution.py:85
  146.0 2.9 fusion.1
  153.4 8.6 all_gather.36
  163.1 8.7 all_gather.40
  172.1 8.8 all_gather.35
  182.1 9.0 all_gather.39
  202.5 2.8 fusion.91
  207.4 19.4 %all-gather.10.cloned.1.call-done = bf16[768,3072]{1,0:T(8,128)(2,1)} async-done(((bf16[96,3072]{1,0:T(8,128)(2,1)}), bf16[768,3072]{1,0:T(8,128)(2,1)}) %all-gather.10.cloned.1.call-update) | async-done | bytes 4718608 | tf_op jit(solution)/shard_map/all_gather | solution.py:86
  226.8 4.5 convolution_add_fusion.5
  231.4 6.5 multiply_convert_fusion.5
  237.9 69.2 %all-gather.12.cloned.1.call-done = bf16[3072,768]{1,0:T(8,128)(2,1)} async-done(((bf16[384,768]{1,0:T(8,128)(2,1)}), bf16[3072,768]{1,0:T(8,128)(2,1)}) %all-gather.12.cloned.1.call-update) | async-done | bytes 4718608 | tf_op jit(solution)/shard_map/all_gather | solution.py:87
  307.1 3.5 convolution_add_fusion.14
  311.3 5.7 fusion.90
  325.7 5.5 fusion.105
  331.2 5.7 fusion.104
  338.7 2.4 multiply_reduce_fusion.8
  346.7 2.1 convolution_convert_fusion
  348.8 2.3 copy.158
  360.7 2.4 copy.147
  382.7 2.8 convolution_bitcast_fusion.3
  385.5 2.9 convolution_bitcast_fusion
  390.1 8.9 reduce-scatter.18.cloned.1.call-done
  400.7 24.6 %reduce-scatter.16.cloned.1.call-done = bf16[2,64,768]{2,1,0:T(8,128)(2,1)} async-done(((bf16[2,256,768]{2,1,0:T(8,128)(2,1)}), bf16[2,64,768]{2,1,0:T(8,128)(2,1)}) %reduce-scatter.16.cloned.1.call-update) | async-done | bytes 196624 | tf_op jit(solution)/shard_map/reduce_scatter | solution.py:225
  427.1 3.9 multiply_reduce_fusion.10
  432.1 19.6 %reduce-scatter.14.cloned.1.call-done = bf16[2,64,768]{2,1,0:T(8,128)(2,1)} async-done(((bf16[2,256,768]{2,1,0:T(8,128)(2,1)}), bf16[2,64,768]{2,1,0:T(8,128)(2,1)}) %reduce-scatter.14.cloned.1.call-update) | async-done | bytes 196624 | tf_op jit(solution)/shard_map/reduce_scatter | solution.py:219
  453.5 3.8 multiply_reduce_fusion.30
  460.8 3.3 maximum_add_fusion
  464.1 11.0 copy.168
  475.1 8.2 copy.179
  485.6 4.0 convolution_add_fusion
  492.8 5.1 convolution_add_fusion.2
  500.6 7.0 convolution_add_fusion.1
  510.4 102.2 %reduce-scatter.28.cloned.1.call-done = f32[96,2304]{1,0:T(8,128)} async-done(((f32[768,2304]{1,0:T(8,128)}), f32[96,2304]{1,0:T(8,128)}) %reduce-scatter.28.cloned.1.call-update) | async-done | bytes 884752
  615.3 129.2 %reduce-scatter.22.cloned.1.call-done = f32[96,2304]{1,0:T(8,128)} async-done(((f32[768,2304]{1,0:T(8,128)}), f32[96,2304]{1,0:T(8,128)}) %reduce-scatter.22.cloned.1.call-update) | async-done | bytes 884752 | tf_op jit(solution)/shard_map/reduce_scatter | solution.py:96
  744.4 164.9 %reduce-scatter.24.cloned.1.call-done = f32[96,3072]{1,0:T(8,128)} async-done(((f32[768,3072]{1,0:T(8,128)}), f32[96,3072]{1,0:T(8,128)}) %reduce-scatter.24.cloned.1.call-update) | async-done | bytes 1179664 | tf_op jit(solution)/shard_map/reduce_scatter | solution.py:97
  909.3 164.7 %reduce-scatter.26.cloned.1.call-done = f32[384,768]{1,0:T(8,128)} async-done(((f32[3072,768]{1,0:T(8,128)}), f32[384,768]{1,0:T(8,128)}) %reduce-scatter.26.cloned.1.call-update) | async-done | bytes 1179664 | tf_op jit(solution)/shard_map/reduce_scatter | solution.py:98
  1075.3 39.5 %psum.91 = f32[]{:T(128)} all-reduce(f32[]{:T(128)S(6)} %add.487), channel_id=1, replica_groups=mesh['dp'=8,'seq'=4] {'dp','seq'}, use_global_device_ids=true, to_apply=%region_18.19 | all-reduce | flops 1 | bytes 8 | tf_op jit(solution)/shard_map/psum | solution.py:323
  1114.8 24.4 %reduce-scatter.30.cloned.1.call-done = f32[96,20]{1,0:T(8,128)} async-done(((f32[768,20]{1,0:T(8,128)}), f32[96,20]{1,0:T(8,128)}) %reduce-scatter.30.cloned.1.call-update) | async-done | bytes 7696
  1140.0 10.7 psum.108
  1151.4 74.4 %all-reduce.3.cloned.1.call-done = (f32[3,96,768]{2,1,0:T(8,128)}, f32[96,2304]{1,0:T(8,128)}, f32[96,3072]{1,0:T(8,128)}, f32[384,768]{1,0:T(8,128)}) async-done(((f32[3,96,768]{2,1,0:T(8,128)}, f32[96,2304]{1,0:T(8,128)}, f32[96,3072]{1,0:T(8,128)}, f32[384,768]{1,0:T(8,128)}), (f32[3,96,768]{2,1,0:T(8,128)}, f32[96,2304]{1,0:T(8,128)}, f32[96,3072]{1,0:T(8,128)}, ...) | async-done | bytes 4128784 | tf_op jit(solution)/shard_map/psum | solution.py:101
  1225.8 2.3 multiply_reduce_fusion.2
  1235.3 22.0 %psum.103 = f32[]{:T(128)} all-reduce(f32[]{:T(128)S(6)} %add.500), channel_id=1, replica_groups=mesh['dp'=8,'seq'=4] {'dp'}, use_global_device_ids=true, to_apply=%region_98.99 | all-reduce | flops 1 | bytes 8 | tf_op jit(solution)/shard_map/psum | solution.py:322
  1258.7 3.8 multiply_subtract_fusion.3
  1265.5 2.4 multiply_subtract_fusion.1
  1269.1 2.4 multiply_subtract_fusion
  (585 shorter events, 112.1 us)
Async XLA Ops:
  7.2 85.1 %all-gather.6.cloned.1.call-start = ((), (), s32[]{:S(2)}) async-start(), calls=%async_computation.9 | async-start | bytes 3981312 | tf_op jit(solution)/shard_map/all_gather | solution.py:84
  9.4 136.5 %all-gather.8.cloned.1.call-start = ((), (), s32[]{:S(2)}) async-start(), calls=%async_computation.10 | async-start | bytes 3981312 | tf_op jit(solution)/shard_map/all_gather | solution.py:85
  10.3 216.5 %all-gather.10.cloned.1.call-start = ((), (), s32[]{:S(2)}) async-start(), calls=%async_computation.11 | async-start | bytes 5308416 | tf_op jit(solution)/shard_map/all_gather | solution.py:86
  11.3 79.4 %copy-start.87 = (bf16[4,64,768]{2,1,0:T(8,128)(2,1)S(1)}, bf16[4,64,768]{2,1,0:T(8,128)(2,1)}, u32[]{:S(2)}) copy-start(bf16[4,64,768]{2,1,0:T(8,128)(2,1)} %param.20) | copy-start | bytes 1179652
  11.3 81.0 %copy-start.88 = (bf16[4,64,768]{2,1,0:T(8,128)(2,1)S(1)}, bf16[4,64,768]{2,1,0:T(8,128)(2,1)}, u32[]{:S(2)}) copy-start(bf16[4,64,768]{2,1,0:T(8,128)(2,1)} %param.18) | copy-start | bytes 1179652
  11.3 295.8 %all-gather.12.cloned.1.call-start = ((), (), s32[]{:S(2)}) async-start(), calls=%async_computation.12 | async-start | bytes 5308416 | tf_op jit(solution)/shard_map/all_gather | solution.py:87
  12.6 375.7 %reduce-scatter.20.cloned.1.call-start = ((), (), s32[]{:S(2)}) async-start(), calls=%async_computation.16 | async-start | bytes 983040 | tf_op jit(solution)/shard_map/reduce_scatter | solution.py:225
  12.7 81.5 %copy-start.179 = (pred[64]{0:T(512)(128)(4,1)}, pred[64]{0:T(512)(128)(4,1)S(1)}, u32[]{:S(2)}) copy-start(pred[64]{0:T(512)(128)(4,1)S(1)} %fusion.78) | copy-start | bytes 196
  47.3 49.2 %copy-start.111 = (f32[768]{0:T(1024)}, f32[768]{0:T(1024)S(1)}, u32[]{:S(2)}) copy-start(f32[768]{0:T(1024)S(1)} %get-tuple-element.121) | copy-start | bytes 9220
  95.9 50.0 %copy-start.24 = (f32[2,64,768]{2,1,0:T(8,128)}, f32[2,64,768]{2,1,0:T(8,128)S(1)}, u32[]{:S(2)}) copy-start(f32[2,64,768]{2,1,0:T(8,128)S(1)} %get-tuple-element.208) | copy-start | bytes 1179652
  96.0 49.9 %copy-start.175 = (f32[128]{0:T(128)}, f32[128]{0:T(128)S(1)}, u32[]{:S(2)}) copy-start(f32[128]{0:T(128)S(1)} %div.184) | copy-start | bytes 1540
  96.1 49.8 %copy-start.177 = (f32[128]{0:T(128)}, f32[128]{0:T(128)S(1)}, u32[]{:S(2)}) copy-start(f32[128]{0:T(128)S(1)} %rsqrt.59) | copy-start | bytes 1540
  96.2 49.7 %copy-start.164 = (f32[128]{0:T(128)}, f32[128]{0:T(128)S(1)}, u32[]{:S(2)}) copy-start(f32[128]{0:T(128)S(1)} %div.177) | copy-start | bytes 1540
  96.5 49.5 %copy-start.166 = (f32[128]{0:T(128)}, f32[128]{0:T(128)S(1)}, u32[]{:S(2)}) copy-start(f32[128]{0:T(128)S(1)} %rsqrt.55) | copy-start | bytes 1540
  153.2 10.0 copy-start.81
  153.4 42.2 %copy-start.44 = (bf16[2,64,768]{1,2,0:T(8,128)(2,1)}, bf16[2,64,768]{1,2,0:T(8,128)(2,1)S(1)}, u32[]{:S(2)}) copy-start(bf16[2,64,768]{1,2,0:T(8,128)(2,1)S(1)} %copy.173) | copy-start | bytes 589828
  172.1 19.3 %copy-start.14 = (bf16[2,256,768]{1,2,0:T(8,128)(2,1)}, bf16[2,256,768]{1,2,0:T(8,128)(2,1)S(1)}, u32[]{:S(2)}) copy-start(bf16[2,256,768]{1,2,0:T(8,128)(2,1)S(1)} %copy.138) | copy-start | bytes 2359300
  172.1 10.0 copy-start.80
  205.3 135.7 %copy-start.3 = (f32[128,768]{1,0:T(8,128)}, f32[128,768]{1,0:T(8,128)S(1)}, u32[]{:S(2)}) copy-start(f32[128,768]{1,0:T(8,128)S(1)} %get-tuple-element.154) | copy-start | bytes 1179652
  311.3 6.2 copy-start.104
  311.3 6.2 copy-start.113
  317.0 7.2 copy-start.46
  317.0 7.3 copy-start.48
  317.0 7.2 copy-start.147
  317.0 7.2 copy-start.149
  317.2 7.0 copy-start.171
  317.4 6.8 copy-start.169
  325.3 15.8 %copy-start.34 = (f32[128,768]{1,0:T(8,128)}, f32[128,768]{1,0:T(8,128)S(1)}, u32[]{:S(2)}) copy-start(f32[128,768]{1,0:T(8,128)S(1)} %get-tuple-element.178) | copy-start | bytes 1179652
  325.3 15.8 %copy-start.61 = (f32[128,768]{1,0:T(8,128)}, f32[128,768]{1,0:T(8,128)S(1)}, u32[]{:S(2)}) copy-start(f32[128,768]{1,0:T(8,128)S(1)} %get-tuple-element.145) | copy-start | bytes 1179652
  325.7 11.2 slice-start
  331.2 7.4 copy-start.52
  351.1 47.9 %reduce-scatter.18.cloned.1.call-start = ((), (), s32[]{:S(2)}) async-start(), calls=%async_computation.15 | async-start | bytes 983040 | tf_op jit(solution)/shard_map/reduce_scatter | solution.py:219
  356.0 69.3 %reduce-scatter.16.cloned.1.call-start = ((), (), s32[]{:S(2)}) async-start(), calls=%async_computation.14 | async-start | bytes 983040 | tf_op jit(solution)/shard_map/reduce_scatter | solution.py:225
  360.7 9.1 copy-start.89
  360.7 9.9 copy-start.17
  363.1 88.6 %reduce-scatter.14.cloned.1.call-start = ((), (), s32[]{:S(2)}) async-start(), calls=%async_computation.13 | async-start | bytes 983040 | tf_op jit(solution)/shard_map/reduce_scatter | solution.py:219
  374.9 237.7 %reduce-scatter.28.cloned.1.call-start = ((), (), s32[]{:S(2)}) async-start(), calls=%async_computation.20 | async-start | bytes 7962624
  385.5 41.6 %copy-start.2 = (bf16[768,2304]{1,0:T(8,128)(2,1)S(1)}, bf16[768,2304]{1,0:T(8,128)(2,1)}, u32[]{:S(2)}) copy-start(bf16[768,2304]{1,0:T(8,128)(2,1)} %all-gather.8.cloned.1.call-done) | copy-start | bytes 10616836
  385.5 41.6 %copy-start.112 = (f32[768]{0:T(1024)S(1)}, f32[768]{0:T(1024)}, u32[]{:S(2)}) copy-start(f32[768]{0:T(1024)} %copy-done.111) | copy-start | bytes 9220
  385.5 41.6 %copy-start.176 = (f32[128]{0:T(128)S(1)}, f32[128]{0:T(128)}, u32[]{:S(2)}) copy-start(f32[128]{0:T(128)} %copy-done.175) | copy-start | bytes 1540
  483.4 261.1 %reduce-scatter.22.cloned.1.call-start = ((), (), s32[]{:S(2)}) async-start(), calls=%async_computation.17 | async-start | bytes 7962624 | tf_op jit(solution)/shard_map/reduce_scatter | solution.py:96
  489.7 419.6 %reduce-scatter.24.cloned.1.call-start = ((), (), s32[]{:S(2)}) async-start(), calls=%async_computation.18 | async-start | bytes 10616832 | tf_op jit(solution)/shard_map/reduce_scatter | solution.py:97
  497.9 576.0 %reduce-scatter.26.cloned.1.call-start = ((), (), s32[]{:S(2)}) async-start(), calls=%async_computation.19 | async-start | bytes 10616832 | tf_op jit(solution)/shard_map/reduce_scatter | solution.py:98
  507.9 631.3 %reduce-scatter.30.cloned.1.call-start = ((), (), s32[]{:S(2)}) async-start(), calls=%async_computation.21 | async-start | bytes 442368
  510.4 715.4 %all-reduce.3.cloned.1.call-start = ((), (), s32[]{:S(2)}) async-start(), calls=%async_computation.22 | async-start | bytes 8257536 | tf_op jit(solution)/shard_map/psum | solution.py:101
  1228.1 29.9 %copy-start.108 = (f32[20,96]{1,0:T(8,128)S(1)}, f32[20,96]{1,0:T(8,128)}, u32[]{:S(2)}) copy-start(f32[20,96]{1,0:T(8,128)} %param.25) | copy-start | bytes 23044
  1228.1 29.9 %copy-start.140 = (f32[20,96]{1,0:T(8,128)S(1)}, f32[20,96]{1,0:T(8,128)}, u32[]{:S(2)}) copy-start(f32[20,96]{1,0:T(8,128)} %param.35) | copy-start | bytes 23044
  1228.1 29.9 %copy-start.141 = (f32[20,96]{1,0:T(8,128)S(1)}, f32[20,96]{1,0:T(8,128)}, u32[]{:S(2)}) copy-start(f32[20,96]{1,0:T(8,128)} %param.30) | copy-start | bytes 23044
  (154 other events, 348.3 us)
Sparse Core Ops, SparseCore 0:
  10.8 69.2 all-gather.5
  82.8 63.0 all-gather.7
  148.7 78.0 all-gather.9
  229.4 77.6 all-gather.11
  351.2 21.5 reduce-scatter.19
  375.8 23.1 reduce-scatter.17
  402.1 23.1 reduce-scatter.15
  428.5 23.1 reduce-scatter.13
  483.4 129.1 reduce-scatter.27
  616.1 128.2 reduce-scatter.21
  748.0 161.2 reduce-scatter.23
  912.8 161.1 reduce-scatter.25
  1077.8 61.2 reduce-scatter.29
  1142.2 83.5 all-reduce.2
where the time goes:
time: 1290 us; the launch traced here: 1280 us
  waiting for transfers between devices  850 us (66%)
  blocking collectives  182 us (14%)
  matrix products  108 us (8%)
  local copies, waits for them, and re-layouts  76.5 us (6%)
  other arithmetic  36.7 us (3%)
  between operations  25.5 us (2%)
    reduce_scatter x1, waiting for transfers between devices, reduce_grads(): lax.psum_scatter(expand_grad, 'dp', scatter_dimension=0, tiled=True)  165 us
    reduce_scatter x1, waiting for transfers between devices, reduce_grads(): lax.psum_scatter(reduce_grad, 'dp', scatter_dimension=0, tiled=True)  165 us
    reduce_scatter x1, waiting for transfers between devices, reduce_grads(): lax.psum_scatter(joint_grad, 'dp', scatter_dimension=0, tiled=True)  129 us
    unnamed x16, waiting for transfers between devices  127 us
    psum x1, waiting for transfers between devices, reduce_grads(): lax.psum((square_grad, joint_grad, expand_grad, reduce_grad, vector_grad)...  74.4 us
    all_gather x1, waiting for transfers between devices, fetch(): lax.all_gather(reduce_low, 'dp', axis=0, tiled=True)  69.2 us
    all_gather x1, waiting for transfers between devices, fetch(): lax.all_gather(joint_low, 'dp', axis=0, tiled=True)  48.5 us
    psum x1, blocking collectives, local(): count = lax.psum(jnp.sum(block_mask.astype(jnp.float32)), ('dp', 'seq'))  41.5 us
  transfers between devices with their start and end apart: 14, of which 12 were waited for; matrix products, arithmetic and copies ran while one was open for 9% of the time, Pallas kernels for 0%

commit v1 on v0

v1 whole, which is shorter than its diff:
```python
from functools import partial
import math

import jax
import jax.numpy as jnp
from jax import lax
from jax.experimental import pallas as pl
from jax.experimental.pallas import tpu as pltpu
from jax.sharding import PartitionSpec as P

HEADS = 12
GRID = 14
LANES = 128
BLOCKS = 8
CUTS = 6

norm_eps = 1e-06
beta_one = 0.9
beta_two = 0.999
adam_eps = 1e-08
adam_step = 10.0
matrix_rate = 0.05
vector_rate = 0.3
weight_decay = 0.05
clip_limit = 0.1

f32 = jnp.float32
bf16 = jnp.bfloat16

ROW_P, ROW_QKV, ROW_O, ROW_ONE, ROW_TWO, ROW_H, ROWS = 0, 96, 384, 480, 864, 1248, 1344


def nn(left, right):
    return jnp.dot(left, right, preferred_element_type=f32)


def nt(left, right):
    return lax.dot_general(left, right, (((1,), (1,)), ((), ())), preferred_element_type=f32)


def tn(left, right):
    return lax.dot_general(left, right, (((0,), (0,)), ((), ())), preferred_element_type=f32)


def stats(stream):
    centred = stream - jnp.mean(stream, -1, keepdims=True)
    inverse = lax.rsqrt(jnp.mean(centred * centred, -1, keepdims=True) + norm_eps)
    return (centred * inverse, inverse)


def norm_back(upstream, normed, inverse, gain):
    scaled = upstream * gain
    return inverse * (
        scaled
        - jnp.mean(scaled, -1, keepdims=True)
        - normed * jnp.mean(scaled * normed, -1, keepdims=True)
    )


def column_sum(value):
    return jnp.sum(value, 0, keepdims=True)


def step_kernel(pieces, n_refs, *refs):
    info = refs[0]
    pix, target, mask, pos, vec, bias = refs[1:7]
    sources = refs[7 : 7 + n_refs]
    keep, send, vgrad, loss = refs[7 + n_refs : 11 + n_refs]
    (w, x0, x1, x2, branch, mlp, work, qkv, probs, attn, slope, act, hid, low, sem_in, sem_out) = refs[
        11 + n_refs :
    ]
    length, width = pix.shape
    pairs = width // 256
    first, second = (0, ROW_ONE), (ROW_ONE, ROWS)

    for group, (begin, end) in enumerate((first, second)):
        for source, lead, cut_slot, block_slot, row, rows in pieces:
            lo, hi = max(begin, row), min(end, row + rows)
            if lo >= hi:
                continue
            pltpu.make_async_copy(
                sources[source].at[lead, lo - row : hi - row],
                w.at[info[cut_slot], info[block_slot], lo:hi],
                sem_in.at[group],
            ).start()

    def arrived(group, begin, end):
        part = w.at[:, :, begin:end]
        pltpu.make_async_copy(part, part, sem_in.at[group]).wait()

    def block(cut, row, rows):
        return w[cut, :, row : row + rows, :].reshape(BLOCKS * rows, LANES)

    def pair(i, row, rows=96):
        return jnp.concatenate([block(2 * i, row, rows), block(2 * i + 1, row, rows)], 1)

    def cols(i, size=256):
        return pl.ds(pl.multiple_of(i * size, size), size)

    def all_cuts(row):
        return jnp.concatenate([block(cut, row, 96) for cut in range(CUTS)], 1)

    def put(cut, row, rows, value):
        w[cut, :, row : row + rows, :] = value.astype(bf16).reshape(BLOCKS, rows, LANES)

    def put_pair(i, row, value):
        put(2 * i, row, 96, value[:, :LANES])
        put(2 * i + 1, row, 96, value[:, LANES:])

    def leave(group, begin, end):
        core = info[0]
        for block_index in range(BLOCKS):
            place = info[8 + block_index]
            for number, (out, base) in enumerate(((keep, 3 * core), (send, 3 - 3 * core))):
                pltpu.make_async_copy(
                    w.at[pl.ds(base, 3), block_index, begin:end],
                    out.at[place, :, begin:end],
                    sem_out.at[number, group],
                ).start()

    row_index = lax.broadcasted_iota(jnp.int32, (length, 1), 0)
    is_class = row_index == GRID * GRID
    key_valid = lax.broadcasted_iota(jnp.int32, (1, length), 1) <= GRID * GRID
    lower_half = lax.broadcasted_iota(jnp.int32, (1, LANES), 1) < LANES // 2
    masked = mask[...] > 0.5

    arrived(0, *first)

    @pl.loop(0, pairs)
    def _(i):
        c = cols(i)
        embedded = nn(pix[...], pair(i, ROW_P)) + vec[2:3, c]
        value = jnp.where(is_class, vec[0:1, c], jnp.where(masked, vec[1:2, c], embedded))
        x0[:, c] = value + pos[:, c]

    normed, _ = stats(x0[...])
    low[...] = (normed * vec[3:4, :] + vec[4:5, :]).astype(bf16)

    @pl.loop(0, pairs)
    def _(i):
        parts = [
            w[2 * i + j // 3, :, ROW_QKV + 96 * (j % 3) : ROW_QKV + 96 * (j % 3) + 96, :].reshape(width, LANES)
            for j in range(6)
        ]
        shift = jnp.where(i == 0, vec[5:6, :], jnp.where(i == 1, 0.0, vec[6:7, :]))
        for j in range(3):
            value = nn(low[...], jnp.concatenate(parts[2 * j : 2 * j + 2], 1)) + shift[:, 256 * j : 256 * j + 256]
            qkv[i, :, 256 * j : 256 * j + 256] = value.astype(bf16)

    @pl.loop(0, HEADS // 2)
    def _(i):
        c = cols(i, LANES)
        query, key, value = qkv[0, :, c], qkv[1, :, c], qkv[2, :, c]
        outs = []
        for half in range(2):
            chosen = lower_half if half == 0 else jnp.logical_not(lower_half)
            scores = nt(jnp.where(chosen, query, jnp.zeros_like(query)), key) * 0.125
            scores = jnp.where(key_valid, scores, -1e30)
            shifted = jnp.exp(scores - jnp.max(scores, -1, keepdims=True))
            p = shifted * (1.0 / jnp.sum(shifted, -1, keepdims=True))
            probs[2 * i + half] = p
            outs.append(nn(p.astype(bf16), value))
        attn[:, c] = jnp.where(lower_half, outs[0], outs[1]).astype(bf16)

    @pl.loop(0, pairs)
    def _(i):
        c = cols(i)
        value = nn(attn[...], pair(i, ROW_O)) + vec[7:8, c]
        branch[:, c] = value
        x1[:, c] = x0[:, c] + vec[8:9, c] * value

    normed, _ = stats(x1[...])
    low[...] = (normed * vec[9:10, :] + vec[10:11, :]).astype(bf16)
    arrived(1, *second)

    @pl.loop(0, CUTS)
    def _(cut):
        for j in range(2):
            rhs = jnp.concatenate(
                [
                    w[cut, :, ROW_ONE + 96 * k : ROW_ONE + 96 * k + 96, :].reshape(width, LANES)
                    for k in (2 * j, 2 * j + 1)
                ],
                1,
            )
            c = cols(2 * cut + j)
            inner = nn(low[...], rhs) + bias[:, c]
            cdf = 0.5 + 0.5 * lax.erf(inner * math.sqrt(0.5))
            act[:, c] = (inner * cdf).astype(bf16)
            slope[:, c] = cdf + inner * (jnp.exp(-0.5 * inner * inner) * (1.0 / math.sqrt(2.0 * math.pi)))

    @pl.loop(0, pairs)
    def _(i):
        c = cols(i)
        value = nn(act[...], pair(i, ROW_TWO, 384)) + vec[11:12, c]
        mlp[:, c] = value
        x2[:, c] = x1[:, c] + vec[12:13, c] * value

    normed3, inverse3 = stats(x2[...])
    low[...] = (normed3 * vec[13:14, :] + vec[14:15, :]).astype(bf16)
    loss[...] = jnp.zeros_like(loss)

    @pl.loop(0, pairs)
    def _(i):
        c = cols(i)
        residual = nn(low[...], pair(i, ROW_H)) + vec[15:16, c] - target[:, c].astype(f32)
        size = jnp.abs(residual)
        terms = jnp.where(size < 2.0, 0.25 * residual * residual, size - 1.0)
        loss[0:1, 0:256] += column_sum(jnp.where(masked, terms, 0.0))
        grad = jnp.where(masked, jnp.clip(0.5 * residual, -1.0, 1.0), 0.0)
        vgrad[15:16, c] = column_sum(grad)
        hid[:, c] = grad.astype(bf16)

    upstream = nt(hid[...], all_cuts(ROW_H))
    vgrad[13:14, :] = column_sum(upstream * normed3)
    vgrad[14:15, :] = column_sum(upstream)
    grad2 = norm_back(upstream, normed3, inverse3, vec[13:14, :])
    x2[...] = grad2
    flipped = low[...].T

    @pl.loop(0, pairs)
    def _(i):
        put_pair(i, ROW_H, nn(flipped, hid[:, cols(i)]))

    vgrad[12:13, :] = column_sum(grad2 * mlp[...])
    grad_mlp = grad2 * vec[12:13, :]
    vgrad[11:12, :] = column_sum(grad_mlp)
    hid[...] = grad_mlp.astype(bf16)

    @pl.loop(0, BLOCKS)
    def _(q):
        c = cols(q, 384)
        rhs = jnp.concatenate([w[cut, q, ROW_TWO:ROW_H, :] for cut in range(CUTS)], 1)
        grad_inner = nt(hid[...], rhs) * slope[:, c]
        bias_grad = column_sum(grad_inner)
        slope[0:1, c] = bias_grad
        value = nn(act[:, c].T, hid[...]).astype(bf16)
        for cut in range(CUTS):
            w[cut, q, ROW_TWO:ROW_H, :] = value[:, LANES * cut : LANES * cut + LANES]
        act[:, c] = grad_inner.astype(bf16)

    for k in range(4):
        vgrad[16 + k : 17 + k, :] = slope[0:1, width * k : width * k + width]

    normed2, inverse2 = stats(x1[...])
    low[...] = (normed2 * vec[9:10, :] + vec[10:11, :]).astype(bf16)
    flipped = low[...].T
    work[...] = jnp.zeros_like(work)

    @pl.loop(0, CUTS)
    def _(cut):
        grad_inner = act[:, cols(cut, 512)]
        rhs = jnp.concatenate(
            [w[cut, :, ROW_ONE + 96 * k : ROW_ONE + 96 * k + 96, :].reshape(width, LANES) for k in range(4)], 1
        )
        work[...] += nt(grad_inner, rhs)
        for j in range(2):
            value = nn(flipped, grad_inner[:, 256 * j : 256 * j + 256])
            put(cut, ROW_ONE + 192 * j, 96, value[:, :LANES])
            put(cut, ROW_ONE + 192 * j + 96, 96, value[:, LANES:])

    leave(1, *second)

    upstream = work[...]
    vgrad[9:10, :] = column_sum(upstream * normed2)
    vgrad[10:11, :] = column_sum(upstream)
    grad1 = x2[...] + norm_back(upstream, normed2, inverse2, vec[9:10, :])
    x2[...] = grad1
    vgrad[8:9, :] = column_sum(grad1 * branch[...])
    grad_branch = grad1 * vec[8:9, :]
    vgrad[7:8, :] = column_sum(grad_branch)
    hid[...] = grad_branch.astype(bf16)
    low[...] = nt(hid[...], all_cuts(ROW_O)).astype(bf16)
    flipped = attn[...].T

    @pl.loop(0, pairs)
    def _(i):
        put_pair(i, ROW_O, nn(flipped, hid[:, cols(i)]))

    @pl.loop(0, HEADS // 2)
    def _(i):
        c = cols(i, LANES)
        query, key, value = qkv[0, :, c], qkv[1, :, c], qkv[2, :, c]
        out_grad = low[:, c]
        outs = []
        for half in range(2):
            chosen = lower_half if half == 0 else jnp.logical_not(lower_half)
            p = probs[2 * i + half]
            dp = nt(jnp.where(chosen, out_grad, jnp.zeros_like(out_grad)), value)
            ds = (p * (dp - jnp.sum(p * dp, -1, keepdims=True))).astype(bf16)
            outs.append((nn(ds, key), tn(ds, query), tn(p.astype(bf16), out_grad)))
        dq, dk, dv = (jnp.where(lower_half, one, two) for one, two in zip(*outs))
        dq, dk = (dq * 0.125, dk * 0.125)
        vgrad[5:6, c] = column_sum(dq)
        vgrad[6:7, c] = column_sum(dv)
        qkv[0, :, c], qkv[1, :, c], qkv[2, :, c] = (dq.astype(bf16), dk.astype(bf16), dv.astype(bf16))

    normed1, inverse1 = stats(x0[...])
    low[...] = (normed1 * vec[3:4, :] + vec[4:5, :]).astype(bf16)
    flipped = low[...].T
    work[...] = jnp.zeros_like(work)

    @pl.loop(0, pairs)
    def _(i):
        parts = [
            w[2 * i + j // 3, :, ROW_QKV + 96 * (j % 3) : ROW_QKV + 96 * (j % 3) + 96, :].reshape(width, LANES)
            for j in range(6)
        ]
        work[...] += nt(qkv[i], jnp.concatenate(parts, 1))
        for j in range(3):
            value = nn(flipped, qkv[i, :, 256 * j : 256 * j + 256]).astype(bf16)
            for half in range(2):
                k = 2 * j + half
                w[2 * i + k // 3, :, ROW_QKV + 96 * (k % 3) : ROW_QKV + 96 * (k % 3) + 96, :] = value[
                    :, LANES * half : LANES * half + LANES
                ].reshape(BLOCKS, 96, LANES)

    upstream = work[...]
    vgrad[3:4, :] = column_sum(upstream * normed1)
    vgrad[4:5, :] = column_sum(upstream)
    grad0 = x2[...] + norm_back(upstream, normed1, inverse1, vec[3:4, :])
    vgrad[0:1, :] = column_sum(jnp.where(is_class, grad0, 0.0))
    token = jnp.logical_and(masked, jnp.logical_not(is_class))
    vgrad[1:2, :] = column_sum(jnp.where(token, grad0, 0.0))
    grad_embed = jnp.where(jnp.logical_or(is_class, masked), 0.0, grad0)
    vgrad[2:3, :] = column_sum(grad_embed)
    hid[...] = grad_embed.astype(bf16)
    flipped = pix[...].T

    @pl.loop(0, pairs)
    def _(i):
        put_pair(i, ROW_P, nn(flipped, hid[:, cols(i)]))

    leave(0, *first)
    for number, out in enumerate((keep, send)):
        for group, (begin, end) in enumerate((first, second)):
            part = out.at[:, :, begin:end]
            pltpu.make_async_copy(part, part, sem_out.at[number, group]).wait()


def run_step(info, pix, target, mask, pos, vec, bias, pieces, sources):
    length, width = pix.shape
    hidden = bias.shape[1]
    vmem = pl.BlockSpec(memory_space=pltpu.VMEM)
    anywhere = pl.BlockSpec(memory_space=pl.ANY)
    half = jax.ShapeDtypeStruct((BLOCKS, 3, ROWS, LANES), bf16)
    big = pltpu.VMEM((length, width), f32)
    small = pltpu.VMEM((length, width), bf16)
    return pl.pallas_call(
        partial(step_kernel, pieces, len(sources)),
        out_shape=(
            half,
            half,
            jax.ShapeDtypeStruct((24, width), f32),
            jax.ShapeDtypeStruct((8, 256), f32),
        ),
        in_specs=[pl.BlockSpec(memory_space=pltpu.SMEM)] + [vmem] * 6 + [anywhere] * len(sources),
        out_specs=(anywhere, anywhere, vmem, vmem),
        scratch_shapes=[
            pltpu.VMEM((CUTS, BLOCKS, ROWS, LANES), bf16),
            big,
            big,
            big,
            big,
            big,
            big,
            pltpu.VMEM((3, length, width), bf16),
            pltpu.VMEM((HEADS, length, length), f32),
            small,
            pltpu.VMEM((length, hidden), f32),
            pltpu.VMEM((length, hidden), bf16),
            small,
            small,
            pltpu.SemaphoreType.DMA((2,)),
            pltpu.SemaphoreType.DMA((2, 2)),
        ],
        compiler_params=pltpu.CompilerParams(vmem_limit_bytes=60 * 1024 * 1024),
        name="step",
    )(info, pix, target, mask, pos, vec, bias, *sources)


def pack_kernel(square, joint, expand, reduce, out):
    for cut in range(CUTS):
        for row, n, rows, take in (
            (ROW_P, 1, 96, lambda c: square[0, :, c]),
            (ROW_QKV, 3, 96, lambda c: joint[:, c]),
            (ROW_O, 1, 96, lambda c: square[1, :, c]),
            (ROW_ONE, 4, 96, lambda c: expand[:, c]),
            (ROW_TWO, 1, 384, lambda c: reduce[:, c]),
            (ROW_H, 1, 96, lambda c: square[2, :, c]),
        ):
            for j in range(n):
                begin = LANES * (n * cut + j)
                out[cut, row + rows * j : row + rows * j + rows, :] = take(slice(begin, begin + LANES)).astype(bf16)


def pack(square, joint, expand, reduce):
    vmem = pl.BlockSpec(memory_space=pltpu.VMEM)
    return pl.pallas_call(
        pack_kernel,
        out_shape=jax.ShapeDtypeStruct((CUTS, ROWS, LANES), bf16),
        in_specs=[vmem] * 4,
        out_specs=vmem,
        name="pack",
    )(square, joint, expand, reduce)


def adam(weight, moment, variance, grad, rate, decay):
    moment_new = beta_one * moment + (1.0 - beta_one) * grad
    variance_new = beta_two * variance + (1.0 - beta_two) * grad * grad
    corrected = (
        moment_new
        / (1.0 - beta_one**adam_step)
        / (jnp.sqrt(variance_new / (1.0 - beta_two**adam_step)) + adam_eps)
    )
    return (moment_new, variance_new, weight - rate * (corrected + decay * weight))


def adam_kernel(core, factor, own, other, *refs):
    states, outs = refs[:12], refs[12:]
    cut = pl.program_id(0)
    mine = cut // 3 == core[0]
    scale = factor[0]

    def grad_of(row, rows):
        index = lax.rem(cut, 3)
        grad = jnp.where(mine, own[index, row : row + rows, :], other[index, row : row + rows, :])
        return grad.astype(f32) * scale

    def update(kind, where, row, rows):
        weight, moment, variance = (states[4 * k + kind][where] for k in range(3))
        results = adam(weight, moment, variance, grad_of(row, rows), matrix_rate, weight_decay)
        for k, result in enumerate(results):
            outs[4 * k + kind][where] = result

    for i, row in enumerate((ROW_P, ROW_O, ROW_H)):
        update(0, (i,), row, 96)
    for j in range(3):
        update(1, (slice(None), slice(LANES * j, LANES * j + LANES)), ROW_QKV + 96 * j, 96)
    for j in range(4):
        update(2, (slice(None), slice(LANES * j, LANES * j + LANES)), ROW_ONE + 96 * j, 96)
    update(3, (slice(None), slice(None)), ROW_TWO, 384)


def adam_all(core, factor, own, other, masters, moments, variances):
    smem = pl.BlockSpec(memory_space=pltpu.SMEM)
    whole = pl.BlockSpec(memory_space=pltpu.VMEM)
    blocks = [
        pl.BlockSpec((3, 96, LANES), lambda i: (0, 0, i)),
        pl.BlockSpec((96, 3 * LANES), lambda i: (0, i)),
        pl.BlockSpec((96, 4 * LANES), lambda i: (0, i)),
        pl.BlockSpec((384, LANES), lambda i: (0, i)),
    ]
    outs = [jax.ShapeDtypeStruct(master.shape, f32) for master in masters]
    results = pl.pallas_call(
        adam_kernel,
        grid=(CUTS,),
        out_shape=outs * 3,
        in_specs=[smem, smem, whole, whole] + blocks * 3,
        out_specs=blocks * 3,
        name="adam",
    )(core, factor, own, other, *masters, *moments, *variances)
    return (results[:4], results[4:8], results[8:])


def positions(slot_float, features):
    column = jnp.arange(features)
    frequency = jnp.exp((2 * (column // 2)).astype(f32) * (-math.log(10000.0) / features))
    angle = slot_float[:, None] * frequency[None, :]
    return jnp.where(column % 2 == 0, jnp.sin(angle), jnp.cos(angle))


def seq_flip(value, k, n_seq):
    return lax.ppermute(value, "seq", [(i, i ^ k) for i in range(n_seq)])


def dp_flip(value, k, n_dp):
    return lax.ppermute(value, "dp", [(i, i ^ k) for i in range(n_dp)])


def whole_image(pixels, block_mask, targets, n_seq):
    images, length, features = pixels.shape
    mask_rows = jnp.zeros((images, 16, features), bf16)
    mask_rows = lax.dynamic_update_slice(mask_rows, block_mask.astype(bf16)[:, None, :], (0, 0, 0))
    parcels = jnp.concatenate([pixels, targets, mask_rows], 1)
    me = lax.axis_index("seq")

    def parcel(k):
        return lax.dynamic_index_in_dim(parcels, me ^ k, 0, keepdims=False)

    got = jnp.stack([parcel(0)] + [seq_flip(parcel(k), k, n_seq) for k in range(1, n_seq)])
    got = jnp.take(got, me ^ jnp.arange(n_seq), axis=0)
    return (
        got[:, :length].reshape(n_seq * length, features),
        got[:, length : 2 * length].reshape(n_seq * length, features),
        got[:, 2 * length, :length].reshape(n_seq * length).astype(f32),
    )


def ring_of(n_dp):
    return list(range(0, n_dp, 2)) + list(range(n_dp - 1, 0, -2))


def tree_sum(values):
    while len(values) > 1:
        values = [left + right for left, right in zip(values[0::2], values[1::2])]
    return values[0]


def local(n_dp, n_seq, *args):
    pixels, block_mask, targets = args[:3]
    masters, moments, variances = args[3:8], args[8:13], args[13:18]
    features = pixels.shape[2]
    square, joint, expand, reduce, vectors = masters
    me, group = lax.axis_index("seq"), lax.axis_index("dp")
    ringed = n_dp == BLOCKS and n_seq == 4
    core = me % 2 if ringed else jnp.zeros((), jnp.int32)
    pix, target, mask = whole_image(pixels, block_mask, targets, n_seq)
    pos = positions(jnp.arange(pix.shape[0]).astype(f32), features)
    vectors_low = vectors.astype(bf16)
    if ringed:
        ring = ring_of(n_dp)
        forward = [(ring[i], ring[(i + 1) % n_dp]) for i in range(n_dp)]
        backward = [(b, a) for a, b in forward]
        place_of = jnp.argsort(jnp.array(ring)).astype(jnp.int32)
        ring_array = jnp.array(ring, jnp.int32)
        place = place_of[group]

        def ahead(value):
            return lax.ppermute(value, "dp", forward)

        def behind(value):
            return lax.ppermute(value, "dp", backward)

        def across(value):
            return seq_flip(value, 1, n_seq)

        stacked = jnp.stack([vectors_low] + [dp_flip(vectors_low, k, n_dp) for k in range(1, n_dp)])
        stacked = jnp.take(stacked, group ^ jnp.arange(n_dp), axis=0)
        vec = stacked.transpose(1, 0, 2).reshape(vectors.shape[0], features).astype(f32)

        slabs = pack(square, joint, expand, reduce)
        mine = lax.dynamic_slice_in_dim(slabs, 3 * core, 3, 0)
        sources, pieces = [slabs], [(0, cut, 24 + cut, 48, 0, ROWS) for cut in range(CUTS)]

        def add_piece(value, swapped, distance, row, rows):
            pieces.extend(
                (len(sources), i, 32 + 3 * swapped + i, 48 + distance, row, rows) for i in range(3)
            )
            sources.append(value)

        left, right = mine, mine
        for distance in range(1, 4):
            left, right = ahead(left), behind(right)
            for value, far in ((left, n_dp - distance), (right, distance)):
                add_piece(value, 0, far, 0, ROWS)
                add_piece(across(value), 1, far, 0, ROWS)
        half = ROWS // 2
        left, right = ahead(left[:, :half]), behind(right[:, half:])
        for value, row in ((left, 0), (right, half)):
            add_piece(value, 0, 4, row, half)
            add_piece(across(value), 1, 4, row, half)
        info = jnp.concatenate(
            [
                jnp.stack([core] + [core] * 7),
                (place_of - place) % n_dp,
                jnp.zeros(8, jnp.int32),
                jnp.arange(8, dtype=jnp.int32),
                jnp.stack([3 * core + i for i in range(3)] + [3 - 3 * core + i for i in range(3)] + [core] * 10),
                ring_array[(place + jnp.arange(8)) % n_dp],
                jnp.zeros(8, jnp.int32),
            ]
        ).astype(jnp.int32)
    else:
        gathered = [
            lax.all_gather(value.astype(bf16), "dp", axis=axis, tiled=True)
            for value, axis in zip(masters, (1, 0, 0, 0, 1))
        ]
        vec = gathered[4].astype(f32)

        def cut_up(matrix):
            rows, columns = matrix.shape
            blocks = columns // (CUTS * LANES)
            shaped = matrix.reshape(BLOCKS, rows // BLOCKS, CUTS, blocks, LANES)
            return shaped.transpose(2, 0, 3, 1, 4).reshape(CUTS, BLOCKS, -1, LANES)

        order = (gathered[0][0], gathered[1], gathered[0][1], gathered[2], gathered[3], gathered[0][2])
        slabs = jnp.concatenate([cut_up(matrix) for matrix in order], 2)
        sources = [slabs.reshape(CUTS * BLOCKS, ROWS, LANES)]
        pieces = [(0, BLOCKS * cut + q, 24 + cut, 48 + q, 0, ROWS) for cut in range(CUTS) for q in range(BLOCKS)]
        eight = jnp.arange(8, dtype=jnp.int32)
        info = jnp.concatenate([eight * 0, eight, eight * 0, eight, eight, eight, eight, eight])

    keep, send, vgrad, loss_rows = run_step(
        info, pix, target, mask[:, None], pos, vec, vec[16:].reshape(1, -1), tuple(pieces), tuple(sources)
    )
    rows = vectors.shape[0]
    loss_part, count_part = jnp.sum(loss_rows), jnp.sum(mask)

    if ringed:
        got = across(send)

        def partial_sum(r, part=slice(None)):
            return keep[r][:, part].astype(f32) + got[r][:, part].astype(f32)

        low_part, high_part = slice(0, half), slice(half, ROWS)
        left = ahead(partial_sum(4, low_part).astype(bf16))
        right = behind(partial_sum(4, high_part).astype(bf16))
        left = jnp.concatenate([partial_sum(3, low_part) + left.astype(f32), partial_sum(3, high_part)], 1)
        right = jnp.concatenate([partial_sum(5, low_part), partial_sum(5, high_part) + right.astype(f32)], 1)
        for r in (2, 1, 0):
            left, right = ahead(left.astype(bf16)).astype(f32), behind(right.astype(bf16)).astype(f32)
            if r:
                left, right = left + partial_sum(r), right + partial_sum(8 - r)
        own = (partial_sum(0) + left + right).astype(bf16)
        other_chip = seq_flip(own, 2, n_seq)
        own = (own.astype(f32) + other_chip.astype(f32)).astype(bf16)
        other = across(own)

        extra = jnp.stack([jnp.full((features,), loss_part), jnp.full((features,), count_part)])
        small = jnp.concatenate([vgrad[:rows], extra]).reshape(rows + 2, n_dp, -1).transpose(1, 0, 2)
        for k in (1, 2):
            small = small + seq_flip(small, k, n_seq)

        def row_of(k):
            return lax.dynamic_index_in_dim(small, group ^ k, 0, keepdims=False)

        small = tree_sum([row_of(0)] + [dp_flip(row_of(k), k, n_dp) for k in range(1, n_dp)])
        vector_grad, loss_sum, count = small[:rows], small[rows, 0], small[rows + 1, 0]
        squares = (
            jnp.sum(jnp.square(own.astype(f32))) + jnp.sum(jnp.square(other.astype(f32))) + jnp.sum(vector_grad**2)
        )
        squares = jnp.full((1, LANES), squares)
        squares = tree_sum([squares] + [dp_flip(squares, k, n_dp) for k in range(1, n_dp)])[0, 0]
    else:
        canonical = jnp.concatenate([keep, send], 1).transpose(1, 0, 2, 3)

        def join(row, end, blocks):
            part = canonical[:, :, row:end].astype(f32).reshape(CUTS, BLOCKS, blocks, -1, LANES)
            return part.transpose(1, 3, 0, 2, 4).reshape(-1, CUTS * blocks * LANES)

        whole = (
            jnp.stack([join(ROW_P, ROW_QKV, 1), join(ROW_O, ROW_ONE, 1), join(ROW_H, ROWS, 1)]),
            join(ROW_QKV, ROW_O, 3),
            join(ROW_ONE, ROW_TWO, 4),
            join(ROW_TWO, ROW_H, 1),
            vgrad[:rows],
        )
        grads = [
            lax.psum_scatter(grad, "dp", scatter_dimension=axis, tiled=True)
            for grad, axis in zip(whole, (1, 0, 0, 0, 1))
        ]
        grads = lax.psum(grads, "seq")
        vector_grad = grads[4]
        squares = lax.psum(sum(jnp.sum(grad * grad) for grad in grads), "dp")
        loss_sum, count = lax.psum((loss_part, count_part), ("dp", "seq"))

    norm = jnp.sqrt(squares) / count
    factor = clip_limit / jnp.maximum(norm, clip_limit) / count
    if ringed:
        new = adam_all(
            core.reshape(1), factor.reshape(1), own, other, masters[:4], moments[:4], variances[:4]
        )
    else:
        updated = [
            adam(master, moment, variance, grad * factor, matrix_rate, weight_decay)
            for master, moment, variance, grad in zip(masters[:4], moments, variances, grads)
        ]
        new = tuple(zip(*updated))
    last = adam(vectors, moments[4], variances[4], vector_grad * factor, vector_rate, 0.0)
    outs = []
    for kind in range(4):
        outs.extend((new[0][kind], new[1][kind], new[2][kind]))
    return (loss_sum / count, norm, *outs, *last)


def solution(mesh):
    matrix = P("dp", None)
    state = (P(None, "dp", None), matrix, matrix, matrix, P(None, "dp"))
    in_specs = (P("dp", "seq", None), P("dp", "seq"), P("dp", "seq", None)) + state * 3
    out_specs = (P(), P()) + tuple(spec for spec in state for _ in range(3))
    return jax.shard_map(
        partial(local, mesh.shape["dp"], mesh.shape["seq"]),
        mesh=mesh,
        in_specs=in_specs,
        out_specs=out_specs,
        check_vma=False,
    )
```

time: 1290 us -> 344 us (0.27)
  waiting for transfers between devices: 850 us -> 176 us
  blocking collectives: 182 us -> 0 us
  matrix products: 108 us -> 0 us
  Pallas kernels: 0 us -> 61.3 us
  starting transfers between devices: 1.2 us -> 61.3 us
  local copies, waits for them, and re-layouts: 76.5 us -> 20.8 us
  other arithmetic: 36.7 us -> 16.3 us
  between operations: 25.5 us -> 8.13 us
    reduce_scatter x7 -> x0, waiting for transfers between devices: 512 us -> none  [the longest x1 165 us: reduce_grads(): lax.psum_scatter(expand_grad, 'dp', scatter_dimension=0, tiled=True)]
    ppermute x0 -> x53, waiting for transfers between devices: none -> 176 us  [the longest x8 84.3 us: ahead(): return lax.ppermute(value, 'dp', forward)]
    all_gather x4 -> x0, waiting for transfers between devices: 137 us -> none  [the longest x1 69.2 us: fetch(): lax.all_gather(reduce_low, 'dp', axis=0, tiled=True)]
    unnamed x16 -> x0, waiting for transfers between devices: 127 us -> none
    psum x4 -> x0, blocking collectives: 114 us -> none  [the longest x1 41.5 us: local(): count = lax.psum(jnp.sum(block_mask.astype(jnp.float32)), ('dp', 'seq'))]
    dot_general x46 -> x0, matrix products: 108 us -> none  [the longest x12 36 us: dense(): return jnp.dot(left, right, preferred_element_type=jnp.float32)]
    psum x1 -> x0, waiting for transfers between devices: 74.4 us -> none  [reduce_grads(): lax.psum((square_grad, joint_grad, expand_grad, reduce_grad, vector_grad)...]
    all_gather x5 -> x0, blocking collectives: 68.2 us -> none  [the longest x1 33.1 us: fetch(): lax.all_gather(vector_low, 'dp', axis=1, tiled=True)]
  transfers between devices with their start and end apart: 14 -> 53, of which waited for: 12 -> 22; matrix products, arithmetic and copies ran while one was open for 9% -> 8% of each run, Pallas kernels for 0% -> 0%
where the time goes in v1:
time: 344 us
  waiting for transfers between devices  176 us (51%)
  Pallas kernels  61.3 us (18%)
  starting transfers between devices  61.3 us (18%)
  local copies, waits for them, and re-layouts  20.8 us (6%)
  other arithmetic  16.3 us (5%)
  between operations  8.13 us (2%)
    ppermute x8, waiting for transfers between devices, ahead(): return lax.ppermute(value, 'dp', forward)  84.3 us
    pallas_call x1, Pallas kernels, run_step(): pl.pallas_call(partial(step_kernel, pieces, len(sources)), out_shape=(hal...  44.8 us
    ppermute x16, waiting for transfers between devices, seq_flip(): return lax.ppermute(value, 'seq', [(i, i ^ k) for i in range(n_seq)])  39.4 us
    ppermute x21, starting transfers between devices, dp_flip(): return lax.ppermute(value, 'dp', [(i, i ^ k) for i in range(n_dp)])  36.3 us
    ppermute x8, waiting for transfers between devices, behind(): return lax.ppermute(value, 'dp', backward)  34.1 us
    ppermute x21, waiting for transfers between devices, dp_flip(): return lax.ppermute(value, 'dp', [(i, i ^ k) for i in range(n_dp)])  17.9 us
    pallas_call x1, Pallas kernels, adam_all(): pl.pallas_call(adam_kernel, grid=(CUTS,), out_shape=outs * 3, in_specs=[s...  12.8 us
    ppermute x8, starting transfers between devices, behind(): return lax.ppermute(value, 'dp', backward)  10.3 us
  transfers between devices with their start and end apart: 53, of which 22 were waited for; matrix products, arithmetic and copies ran while one was open for 8% of the time, Pallas kernels for 0%

profile of v1, /device:TPU:0, one launch (start us, length us, event | category | flops | bytes accessed | tf_op | source)
XLA Modules:
  0.0 343.7 jit_solution(4417751390158739912)
XLA Ops:
  0.7 3.7 %pack.1.refs_7_ = bf16[6,1344,128]{2,1,0:T(8,128)(2,1)} custom-call(f32[3,96,768]{2,1,0:T(8,128)} %refs_0_.1, f32[96,2304]{1,0:T(8,128)} %refs_1_.1, f32[96,3072]{1,0:T(8,128)} %refs_2_.1, f32[384,768]{1,0:T(8,128)} %refs_3_.1), custom_call_target="tpu_custom_call" | custom-call | tf_op jit(solution)/shard_map/pack/pallas_call | solution.py:399
  5.8 3.1 collective-permute-start.10
  9.5 2.0 collective-permute-start.3
  11.5 1.6 collective-permute-start.4
  15.0 16.7 %collective-permute-done.10.refs_8_ = bf16[3,1344,128]{2,1,0:T(8,128)(2,1)S(1)} collective-permute-done((bf16[3,1344,128]{2,1,0:T(8,128)(2,1)S(1)}, bf16[3,1344,128]{2,1,0:T(8,128)(2,1)S(1)}, u32[]{:S(2)}, u32[]{:S(2)}) %collective-permute-start.10) | collective-permute-done | bytes 1032224 | tf_op jit(solution)/shard_map/ppermute | solution.py:530
  31.7 1.9 collective-permute-start.14
  34.6 3.8 %fusion.8.refs_4_ = f32[256,768]{1,0:T(8,128)} fusion(f32[768]{0:T(1024)S(1)} %fusion.17, f32[256]{0:T(256)S(1)} %iota_convert_fusion, pred[768]{0:T(1024)(128)(4,1)S(1)} %fusion.12), kind=kLoop, calls=%fused_computation.38 | loop fusion | flops 393216 | bytes 791296 | tf_op jit(solution)/shard_map/jit(_where)/select_n | solution.py:470
  38.9 2.7 collective-permute-start.6
  44.4 3.6 %collective-permute-start.8 = (bf16[20,96]{1,0:T(8,128)(2,1)S(1)}, bf16[20,96]{1,0:T(8,128)(2,1)S(1)}, u32[]{:S(2)}, u32[]{:S(2)}) collective-permute-start(bf16[20,96]{1,0:T(8,128)(2,1)S(1)} %get-tuple-element.59), channel_id=1, source_target_pairs={{0,24},{4,28},{8,16},{12,20},{16,8},{20,12},{24,0},{28,4},{1,25},{... | collective-permute-start | bytes 11528 | tf_op jit(solution)/shard_map/ppermute | solution.py:478
  48.0 10.7 %collective-permute-done.6 = bf16[20,96]{1,0:T(8,128)(2,1)S(1)} collective-permute-done((bf16[20,96]{1,0:T(8,128)(2,1)S(1)}, bf16[20,96]{1,0:T(8,128)(2,1)S(1)}, u32[]{:S(2)}, u32[]{:S(2)}) %collective-permute-start.6) | collective-permute-done | bytes 3872 | tf_op jit(solution)/shard_map/ppermute | solution.py:478
  58.7 2.6 collective-permute-start.9
  61.3 2.0 collective-permute-start.20
  68.0 18.8 %collective-permute-done.18.refs_16_ = bf16[3,1344,128]{2,1,0:T(8,128)(2,1)S(1)} collective-permute-done((bf16[3,1344,128]{2,1,0:T(8,128)(2,1)}, bf16[3,1344,128]{2,1,0:T(8,128)(2,1)S(1)}, u32[]{:S(2)}, u32[]{:S(2)}) %collective-permute-start.18) | collective-permute-done | bytes 1032224 | tf_op jit(solution)/shard_map/ppermute | solution.py:530
  86.7 1.5 collective-permute-start.1
  89.6 1.9 slice.174
  91.5 3.5 %collective-permute-done.1 = bf16[144,768]{1,0:T(8,128)(2,1)S(1)} collective-permute-done((bf16[144,768]{1,0:T(8,128)(2,1)S(1)}, bf16[144,768]{1,0:T(8,128)(2,1)S(1)}, u32[]{:S(2)}, u32[]{:S(2)}) %collective-permute-start.1) | collective-permute-done | bytes 221216 | tf_op jit(solution)/shard_map/ppermute | solution.py:474
  95.0 2.5 collective-permute-done.2
  98.0 1.6 collective-permute-start.24
  106.4 6.0 %collective-permute-done.22.refs_20_ = bf16[3,672,128]{2,1,0:T(8,128)(2,1)S(1)} collective-permute-done((bf16[3,672,128]{2,1,0:T(8,128)(2,1)}, bf16[3,672,128]{2,1,0:T(8,128)(2,1)S(1)}, u32[]{:S(2)}, u32[]{:S(2)}) %collective-permute-start.22) | collective-permute-done | bytes 516128 | tf_op jit(solution)/shard_map/ppermute | solution.py:530
  115.4 44.8 %step.1 = (bf16[8,3,1344,128]{3,2,1,0:T(8,128)(2,1)}, bf16[8,3,1344,128]{3,2,1,0:T(8,128)(2,1)}, f32[24,768]{1,0:T(8,128)}, f32[8,256]{1,0:T(8,128)}) custom-call(s32[64]{0:T(128)} %concatenate.17.refs_0_, bf16[256,768]{1,0:T(8,128)(2,1)} %bitcast.119, bf16[256,768]{1,0:T(8,128)(2,1)} %bitcast.118, f32[256,1]{1,0:T(8,128)} %reshape.224.refs_3_, ...), custom_call_target="tpu_custom_call" | custom-call | tf_op jit(solution)/shard_map/step/pallas_call | solution.py:349
  160.6 2.0 slice_bitcast_fusion.5
  162.7 10.8 %collective-permute-done.35 = bf16[8,3,1344,128]{3,2,1,0:T(8,128)(2,1)S(1)} collective-permute-done((bf16[8,3,1344,128]{3,2,1,0:T(8,128)(2,1)}, bf16[8,3,1344,128]{3,2,1,0:T(8,128)(2,1)S(1)}, u32[]{:S(2)}, u32[]{:S(2)}) %collective-permute-start.35) | collective-permute-done | bytes 8257568 | tf_op jit(solution)/shard_map/ppermute | solution.py:474
  173.9 1.6 collective-permute-start.40
  176.0 12.0 %collective-permute-done.40 = bf16[3,672,128]{2,1,0:T(8,128)(2,1)S(1)} collective-permute-done((bf16[3,672,128]{2,1,0:T(8,128)(2,1)S(1)}, bf16[3,672,128]{2,1,0:T(8,128)(2,1)S(1)}, u32[]{:S(2)}, u32[]{:S(2)}) %collective-permute-start.40) | collective-permute-done | bytes 516128 | tf_op jit(solution)/shard_map/ppermute | solution.py:533
  188.4 1.8 collective-permute-start.41
  191.2 21.7 %collective-permute-done.41 = bf16[3,1344,128]{2,1,0:T(8,128)(2,1)S(1)} collective-permute-done((bf16[3,1344,128]{2,1,0:T(8,128)(2,1)S(1)}, bf16[3,1344,128]{2,1,0:T(8,128)(2,1)S(1)}, u32[]{:S(2)}, u32[]{:S(2)}) %collective-permute-start.41) | collective-permute-done | bytes 1032224 | tf_op jit(solution)/shard_map/ppermute | solution.py:533
  212.9 1.8 collective-permute-done.37
  216.0 1.6 collective-permute-start.42
  217.6 21.1 %collective-permute-done.38 = bf16[3,1344,128]{2,1,0:T(8,128)(2,1)S(1)} collective-permute-done((bf16[3,1344,128]{2,1,0:T(8,128)(2,1)S(1)}, bf16[3,1344,128]{2,1,0:T(8,128)(2,1)S(1)}, u32[]{:S(2)}, u32[]{:S(2)}) %collective-permute-start.38) | collective-permute-done | bytes 1032224 | tf_op jit(solution)/shard_map/ppermute | solution.py:530
  240.1 1.6 collective-permute-start.43
  241.7 20.1 %collective-permute-done.39 = bf16[3,1344,128]{2,1,0:T(8,128)(2,1)S(1)} collective-permute-done((bf16[3,1344,128]{2,1,0:T(8,128)(2,1)S(1)}, bf16[3,1344,128]{2,1,0:T(8,128)(2,1)S(1)}, u32[]{:S(2)}, u32[]{:S(2)}) %collective-permute-start.39) | collective-permute-done | bytes 1032224 | tf_op jit(solution)/shard_map/ppermute | solution.py:530
  262.4 1.7 collective-permute-start.44
  266.2 17.4 %collective-permute-done.44 = bf16[3,1344,128]{2,1,0:T(8,128)(2,1)S(1)} collective-permute-done((bf16[3,1344,128]{2,1,0:T(8,128)(2,1)S(1)}, bf16[3,1344,128]{2,1,0:T(8,128)(2,1)S(1)}, u32[]{:S(2)}, u32[]{:S(2)}) %collective-permute-start.44) | collective-permute-done | bytes 1032224 | tf_op jit(solution)/shard_map/ppermute | solution.py:474
  285.5 2.0 collective-permute-done.26
  287.5 1.6 collective-permute-start.27
  289.2 3.1 collective-permute-done.27
  292.4 1.5 collective-permute-start.28
  295.9 2.0 collective-permute-start.31
  297.9 1.9 collective-permute-start.32
  301.1 2.6 collective-permute-start.34
  303.7 1.7 collective-permute-done.33
  305.3 2.2 collective-permute-done.34
  312.6 2.1 collective-permute-start.48
  315.9 2.6 collective-permute-start.50
  318.5 1.7 collective-permute-start.51
  320.2 2.2 collective-permute-start.52
  324.3 2.2 collective-permute-done.52
  328.6 12.8 %adam.1 = (f32[3,96,768]{2,1,0:T(8,128)}, f32[96,2304]{1,0:T(8,128)}, f32[96,3072]{1,0:T(8,128)}, f32[384,768]{1,0:T(8,128)}, f32[3,96,768]{2,1,0:T(8,128)}, /*i...) custom-call(s32[1]{0:T(128)} %bitcast.core, ...), custom_call_target="tpu_custom_call" | custom-call | tf_op jit(solution)/shard_map/adam/pallas_call | solution.py:455
  (181 shorter events, 43.5 us)
Async XLA Ops:
  5.8 25.9 %collective-permute-start.10 = (bf16[3,1344,128]{2,1,0:T(8,128)(2,1)S(1)}, bf16[3,1344,128]{2,1,0:T(8,128)(2,1)S(1)}, u32[]{:S(2)}, u32[]{:S(2)}) collective-permute-start(bf16[3,1344,128]{2,1,0:T(8,128)(2,1)S(1)} %constant_dynamic-slice_fusion.8), channel_id=1, source_target_pairs={{0,8},{8,16},{16,24},{24,28},{28,20},{20,12},{12,4},{4,0},{1,9},{9... | collective-permute-start | bytes 3096584 | tf_op jit(solution)/shard_map/ppermute | solution.py:530
  8.9 24.7 %collective-permute-start.12 = (bf16[3,1344,128]{2,1,0:T(8,128)(2,1)S(1)}, bf16[3,1344,128]{2,1,0:T(8,128)(2,1)}, u32[]{:S(2)}, u32[]{:S(2)}) collective-permute-start(bf16[3,1344,128]{2,1,0:T(8,128)(2,1)S(1)} %constant_dynamic-slice_fusion.8), channel_id=1, source_target_pairs={{8,0},{16,8},{24,16},{28,24},{20,28},{12,20},{4,12},{0,4},{9,1},{1... | collective-permute-start | bytes 3096584 | tf_op jit(solution)/shard_map/ppermute | solution.py:533
  9.5 29.4 %collective-permute-start.3 = (bf16[20,96]{1,0:T(8,128)(2,1)S(1)}, bf16[20,96]{1,0:T(8,128)(2,1)S(1)}, u32[]{:S(2)}, u32[]{:S(2)}) collective-permute-start(bf16[20,96]{1,0:T(8,128)(2,1)S(1)} %get-tuple-element.59), channel_id=1, source_target_pairs={{0,4},{4,0},{8,12},{12,8},{16,20},{20,16},{24,28},{28,24},{1,5},{5... | collective-permute-start | bytes 11528 | tf_op jit(solution)/shard_map/ppermute | solution.py:478
  11.5 30.2 %collective-permute-start.4 = (bf16[20,96]{1,0:T(8,128)(2,1)S(1)}, bf16[20,96]{1,0:T(8,128)(2,1)S(1)}, u32[]{:S(2)}, u32[]{:S(2)}) collective-permute-start(bf16[20,96]{1,0:T(8,128)(2,1)S(1)} %get-tuple-element.59), channel_id=1, source_target_pairs={{0,8},{4,12},{8,0},{12,4},{16,24},{20,28},{24,16},{28,20},{1,9},{5... | collective-permute-start | bytes 11528 | tf_op jit(solution)/shard_map/ppermute | solution.py:478
  13.0 31.3 %collective-permute-start.5 = (bf16[20,96]{1,0:T(8,128)(2,1)S(1)}, bf16[20,96]{1,0:T(8,128)(2,1)S(1)}, u32[]{:S(2)}, u32[]{:S(2)}) collective-permute-start(bf16[20,96]{1,0:T(8,128)(2,1)S(1)} %get-tuple-element.59), channel_id=1, source_target_pairs={{0,12},{4,8},{8,4},{12,0},{16,28},{20,24},{24,20},{28,16},{1,13},{... | collective-permute-start | bytes 11528 | tf_op jit(solution)/shard_map/ppermute | solution.py:478
  31.7 29.5 %collective-permute-start.14 = (bf16[3,1344,128]{2,1,0:T(8,128)(2,1)S(1)}, bf16[3,1344,128]{2,1,0:T(8,128)(2,1)}, u32[]{:S(2)}, u32[]{:S(2)}) collective-permute-start(bf16[3,1344,128]{2,1,0:T(8,128)(2,1)S(1)} %collective-permute-done.10.refs_8_), channel_id=1, source_target_pairs={{0,8},{8,16},{16,24},{24,28},{28,20},{20,12},{12,4},{4,0},{1,9},{9... | collective-permute-start | bytes 3096584 | tf_op jit(solution)/shard_map/ppermute | solution.py:530
  33.6 27.7 %collective-permute-start.16 = (bf16[3,1344,128]{2,1,0:T(8,128)(2,1)}, bf16[3,1344,128]{2,1,0:T(8,128)(2,1)}, u32[]{:S(2)}, u32[]{:S(2)}) collective-permute-start(bf16[3,1344,128]{2,1,0:T(8,128)(2,1)} %collective-permute-done.12.refs_10_), channel_id=1, source_target_pairs={{8,0},{16,8},{24,16},{28,24},{20,28},{12,20},{4,12},{0,4},{9,1},{1... | collective-permute-start | bytes 3096584 | tf_op jit(solution)/shard_map/ppermute | solution.py:533
  38.9 19.8 %collective-permute-start.6 = (bf16[20,96]{1,0:T(8,128)(2,1)S(1)}, bf16[20,96]{1,0:T(8,128)(2,1)S(1)}, u32[]{:S(2)}, u32[]{:S(2)}) collective-permute-start(bf16[20,96]{1,0:T(8,128)(2,1)S(1)} %get-tuple-element.59), channel_id=1, source_target_pairs={{0,16},{4,20},{8,24},{12,28},{16,0},{20,4},{24,8},{28,12},{1,17},{... | collective-permute-start | bytes 11528 | tf_op jit(solution)/shard_map/ppermute | solution.py:478
  41.6 19.6 %collective-permute-start.7 = (bf16[20,96]{1,0:T(8,128)(2,1)S(1)}, bf16[20,96]{1,0:T(8,128)(2,1)S(1)}, u32[]{:S(2)}, u32[]{:S(2)}) collective-permute-start(bf16[20,96]{1,0:T(8,128)(2,1)S(1)} %get-tuple-element.59), channel_id=1, source_target_pairs={{0,20},{4,16},{8,28},{12,24},{16,4},{20,0},{24,12},{28,8},{1,21},{... | collective-permute-start | bytes 11528 | tf_op jit(solution)/shard_map/ppermute | solution.py:478
  44.4 19.5 %collective-permute-start.8 = (bf16[20,96]{1,0:T(8,128)(2,1)S(1)}, bf16[20,96]{1,0:T(8,128)(2,1)S(1)}, u32[]{:S(2)}, u32[]{:S(2)}) collective-permute-start(bf16[20,96]{1,0:T(8,128)(2,1)S(1)} %get-tuple-element.59), channel_id=1, source_target_pairs={{0,24},{4,28},{8,16},{12,20},{16,8},{20,12},{24,0},{28,4},{1,25},{... | collective-permute-start | bytes 11528 | tf_op jit(solution)/shard_map/ppermute | solution.py:478
  58.7 6.4 %collective-permute-start.9 = (bf16[20,96]{1,0:T(8,128)(2,1)S(1)}, bf16[20,96]{1,0:T(8,128)(2,1)S(1)}, u32[]{:S(2)}, u32[]{:S(2)}) collective-permute-start(bf16[20,96]{1,0:T(8,128)(2,1)S(1)} %get-tuple-element.59), channel_id=1, source_target_pairs={{0,28},{4,24},{8,20},{12,16},{16,12},{20,8},{24,4},{28,0},{1,29},{... | collective-permute-start | bytes 11528 | tf_op jit(solution)/shard_map/ppermute | solution.py:478
  61.2 25.5 %collective-permute-start.18 = (bf16[3,1344,128]{2,1,0:T(8,128)(2,1)}, bf16[3,1344,128]{2,1,0:T(8,128)(2,1)S(1)}, u32[]{:S(2)}, u32[]{:S(2)}) collective-permute-start(bf16[3,1344,128]{2,1,0:T(8,128)(2,1)} %collective-permute-done.14.refs_12_), channel_id=1, source_target_pairs={{0,8},{8,16},{16,24},{24,28},{28,20},{20,12},{12,4},{4,0},{1,9},{9... | collective-permute-start | bytes 3096584 | tf_op jit(solution)/shard_map/ppermute | solution.py:530
  61.3 26.9 %collective-permute-start.20 = (bf16[3,1344,128]{2,1,0:T(8,128)(2,1)}, bf16[3,1344,128]{2,1,0:T(8,128)(2,1)}, u32[]{:S(2)}, u32[]{:S(2)}) collective-permute-start(bf16[3,1344,128]{2,1,0:T(8,128)(2,1)} %collective-permute-done.16.refs_14_), channel_id=1, source_target_pairs={{8,0},{16,8},{24,16},{28,24},{20,28},{12,20},{4,12},{0,4},{9,1},{1... | collective-permute-start | bytes 3096584 | tf_op jit(solution)/shard_map/ppermute | solution.py:533
  63.9 34.1 %collective-permute-start.11 = (bf16[3,1344,128]{2,1,0:T(8,128)(2,1)S(1)}, bf16[3,1344,128]{2,1,0:T(8,128)(2,1)S(1)}, u32[]{:S(2)}, u32[]{:S(2)}) collective-permute-start(bf16[3,1344,128]{2,1,0:T(8,128)(2,1)S(1)} %collective-permute-done.10.refs_8_), channel_id=1, source_target_pairs={{0,1},{1,0},{2,3},{3,2},{4,5},{5,4},{6,7},{7,6},{8,9},{9,8},{10,11... | collective-permute-start | bytes 3096584 | tf_op jit(solution)/shard_map/ppermute | solution.py:474
  65.1 34.5 %collective-permute-start.13 = (bf16[3,1344,128]{2,1,0:T(8,128)(2,1)}, bf16[3,1344,128]{2,1,0:T(8,128)(2,1)S(1)}, u32[]{:S(2)}, u32[]{:S(2)}) collective-permute-start(bf16[3,1344,128]{2,1,0:T(8,128)(2,1)} %collective-permute-done.12.refs_10_), channel_id=1, source_target_pairs={{0,1},{1,0},{2,3},{3,2},{4,5},{5,4},{6,7},{7,6},{8,9},{9,8},{10,11... | collective-permute-start | bytes 3096584 | tf_op jit(solution)/shard_map/ppermute | solution.py:474
  65.1 35.8 %collective-permute-start.15 = (bf16[3,1344,128]{2,1,0:T(8,128)(2,1)}, bf16[3,1344,128]{2,1,0:T(8,128)(2,1)}, u32[]{:S(2)}, u32[]{:S(2)}) collective-permute-start(bf16[3,1344,128]{2,1,0:T(8,128)(2,1)} %collective-permute-done.14.refs_12_), channel_id=1, source_target_pairs={{0,1},{1,0},{2,3},{3,2},{4,5},{5,4},{6,7},{7,6},{8,9},{9,8},{10,11... | collective-permute-start | bytes 3096584 | tf_op jit(solution)/shard_map/ppermute | solution.py:474
  86.7 8.3 %collective-permute-start.1 = (bf16[144,768]{1,0:T(8,128)(2,1)S(1)}, bf16[144,768]{1,0:T(8,128)(2,1)S(1)}, u32[]{:S(2)}, u32[]{:S(2)}) collective-permute-start(bf16[144,768]{1,0:T(8,128)(2,1)S(1)} %get-tuple-element.80), channel_id=1, source_target_pairs={{0,2},{1,3},{2,0},{3,1},{4,6},{5,7},{6,4},{7,5},{8,10},{9,11},{10,... | collective-permute-start | bytes 663560 | tf_op jit(solution)/shard_map/ppermute | solution.py:474
  88.2 9.3 %collective-permute-start.2 = (bf16[144,768]{1,0:T(8,128)(2,1)S(1)}, bf16[144,768]{1,0:T(8,128)(2,1)}, u32[]{:S(2)}, u32[]{:S(2)}) collective-permute-start(bf16[144,768]{1,0:T(8,128)(2,1)S(1)} %get-tuple-element.79), channel_id=1, source_target_pairs={{0,3},{1,2},{2,1},{3,0},{4,7},{5,6},{6,5},{7,4},{8,11},{9,10},{10,... | collective-permute-start | bytes 663560 | tf_op jit(solution)/shard_map/ppermute | solution.py:474
  95.0 20.3 %collective-permute-start.17 = (bf16[3,1344,128]{2,1,0:T(8,128)(2,1)}, bf16[3,1344,128]{2,1,0:T(8,128)(2,1)}, u32[]{:S(2)}, u32[]{:S(2)}) collective-permute-start(bf16[3,1344,128]{2,1,0:T(8,128)(2,1)} %collective-permute-done.16.refs_14_), channel_id=1, source_target_pairs={{0,1},{1,0},{2,3},{3,2},{4,5},{5,4},{6,7},{7,6},{8,9},{9,8},{10,11... | collective-permute-start | bytes 3096584 | tf_op jit(solution)/shard_map/ppermute | solution.py:474
  97.6 14.8 %collective-permute-start.22 = (bf16[3,672,128]{2,1,0:T(8,128)(2,1)}, bf16[3,672,128]{2,1,0:T(8,128)(2,1)S(1)}, u32[]{:S(2)}, u32[]{:S(2)}) collective-permute-start(bf16[3,672,128]{2,1,0:T(8,128)(2,1)} %slice.173), channel_id=1, source_target_pairs={{0,8},{8,16},{16,24},{24,28},{28,20},{20,12},{12,4},{4,0},{1,9},{9... | collective-permute-start | bytes 1548296 | tf_op jit(solution)/shard_map/ppermute | solution.py:530
  98.0 14.7 %collective-permute-start.24 = (bf16[3,672,128]{2,1,0:T(8,128)(2,1)}, bf16[3,672,128]{2,1,0:T(8,128)(2,1)}, u32[]{:S(2)}, u32[]{:S(2)}) collective-permute-start(bf16[3,672,128]{2,1,0:T(8,128)(2,1)} %slice.174), channel_id=1, source_target_pairs={{8,0},{16,8},{24,16},{28,24},{20,28},{12,20},{4,12},{0,4},{9,1},{1... | collective-permute-start | bytes 1548296 | tf_op jit(solution)/shard_map/ppermute | solution.py:533
  100.6 14.8 %collective-permute-start.19 = (bf16[3,1344,128]{2,1,0:T(8,128)(2,1)S(1)}, bf16[3,1344,128]{2,1,0:T(8,128)(2,1)}, u32[]{:S(2)}, u32[]{:S(2)}) collective-permute-start(bf16[3,1344,128]{2,1,0:T(8,128)(2,1)S(1)} %collective-permute-done.18.refs_16_), channel_id=1, source_target_pairs={{0,1},{1,0},{2,3},{3,2},{4,5},{5,4},{6,7},{7,6},{8,9},{9,8},{10,11... | collective-permute-start | bytes 3096584 | tf_op jit(solution)/shard_map/ppermute | solution.py:474
  100.9 14.4 %collective-permute-start.21 = (bf16[3,1344,128]{2,1,0:T(8,128)(2,1)}, bf16[3,1344,128]{2,1,0:T(8,128)(2,1)}, u32[]{:S(2)}, u32[]{:S(2)}) collective-permute-start(bf16[3,1344,128]{2,1,0:T(8,128)(2,1)} %collective-permute-done.20.refs_18_), channel_id=1, source_target_pairs={{0,1},{1,0},{2,3},{3,2},{4,5},{5,4},{6,7},{7,6},{8,9},{9,8},{10,11... | collective-permute-start | bytes 3096584 | tf_op jit(solution)/shard_map/ppermute | solution.py:474
  160.2 13.2 %collective-permute-start.35 = (bf16[8,3,1344,128]{3,2,1,0:T(8,128)(2,1)}, bf16[8,3,1344,128]{3,2,1,0:T(8,128)(2,1)S(1)}, u32[]{:S(2)}, u32[]{:S(2)}) collective-permute-start(bf16[8,3,1344,128]{3,2,1,0:T(8,128)(2,1)} %get-tuple-element.38), channel_id=1, source_target_pairs={{0,1},{1,0},{2,3},{3,2},{4,5},{5,4},{6,7},{7,6},{8,9},{9,8},{10,11... | collective-permute-start | bytes 24772616 | tf_op jit(solution)/shard_map/ppermute | solution.py:474
  173.9 14.1 %collective-permute-start.40 = (bf16[3,672,128]{2,1,0:T(8,128)(2,1)S(1)}, bf16[3,672,128]{2,1,0:T(8,128)(2,1)S(1)}, u32[]{:S(2)}, u32[]{:S(2)}) collective-permute-start(bf16[3,672,128]{2,1,0:T(8,128)(2,1)S(1)} %get-tuple-element.73), channel_id=1, source_target_pairs={{8,0},{16,8},{24,16},{28,24},{20,28},{12,20},{4,12},{0,4},{9,1},{1... | collective-permute-start | bytes 1548296 | tf_op jit(solution)/shard_map/ppermute | solution.py:533
  175.5 14.7 %collective-permute-start.36 = (bf16[3,672,128]{2,1,0:T(8,128)(2,1)S(1)}, bf16[3,672,128]{2,1,0:T(8,128)(2,1)S(1)}, u32[]{:S(2)}, u32[]{:S(2)}) collective-permute-start(bf16[3,672,128]{2,1,0:T(8,128)(2,1)S(1)} %get-tuple-element.72), channel_id=1, source_target_pairs={{0,8},{8,16},{16,24},{24,28},{28,20},{20,12},{12,4},{4,0},{1,9},{9... | collective-permute-start | bytes 1548296 | tf_op jit(solution)/shard_map/ppermute | solution.py:530
  188.4 24.5 %collective-permute-start.41 = (bf16[3,1344,128]{2,1,0:T(8,128)(2,1)S(1)}, bf16[3,1344,128]{2,1,0:T(8,128)(2,1)S(1)}, u32[]{:S(2)}, u32[]{:S(2)}) collective-permute-start(bf16[3,1344,128]{2,1,0:T(8,128)(2,1)S(1)} %pad_maximum_fusion.1), channel_id=1, source_target_pairs={{8,0},{16,8},{24,16},{28,24},{20,28},{12,20},{4,12},{0,4},{9,1},{1... | collective-permute-start | bytes 3096584 | tf_op jit(solution)/shard_map/ppermute | solution.py:533
  190.7 24.0 %collective-permute-start.37 = (bf16[3,1344,128]{2,1,0:T(8,128)(2,1)S(1)}, bf16[3,1344,128]{2,1,0:T(8,128)(2,1)S(1)}, u32[]{:S(2)}, u32[]{:S(2)}) collective-permute-start(bf16[3,1344,128]{2,1,0:T(8,128)(2,1)S(1)} %pad_maximum_fusion), channel_id=1, source_target_pairs={{0,8},{8,16},{16,24},{24,28},{28,20},{20,12},{12,4},{4,0},{1,9},{9... | collective-permute-start | bytes 3096584 | tf_op jit(solution)/shard_map/ppermute | solution.py:530
  215.5 23.1 %collective-permute-start.38 = (bf16[3,1344,128]{2,1,0:T(8,128)(2,1)S(1)}, bf16[3,1344,128]{2,1,0:T(8,128)(2,1)S(1)}, u32[]{:S(2)}, u32[]{:S(2)}) collective-permute-start(bf16[3,1344,128]{2,1,0:T(8,128)(2,1)S(1)} %get-tuple-element.62), channel_id=1, source_target_pairs={{0,8},{8,16},{16,24},{24,28},{28,20},{20,12},{12,4},{4,0},{1,9},{9... | collective-permute-start | bytes 3096584 | tf_op jit(solution)/shard_map/ppermute | solution.py:530
  216.0 22.8 %collective-permute-start.42 = (bf16[3,1344,128]{2,1,0:T(8,128)(2,1)S(1)}, bf16[3,1344,128]{2,1,0:T(8,128)(2,1)S(1)}, u32[]{:S(2)}, u32[]{:S(2)}) collective-permute-start(bf16[3,1344,128]{2,1,0:T(8,128)(2,1)S(1)} %get-tuple-element.63), channel_id=1, source_target_pairs={{8,0},{16,8},{24,16},{28,24},{20,28},{12,20},{4,12},{0,4},{9,1},{1... | collective-permute-start | bytes 3096584 | tf_op jit(solution)/shard_map/ppermute | solution.py:533
  239.6 22.1 %collective-permute-start.39 = (bf16[3,1344,128]{2,1,0:T(8,128)(2,1)S(1)}, bf16[3,1344,128]{2,1,0:T(8,128)(2,1)S(1)}, u32[]{:S(2)}, u32[]{:S(2)}) collective-permute-start(bf16[3,1344,128]{2,1,0:T(8,128)(2,1)S(1)} %get-tuple-element.60), channel_id=1, source_target_pairs={{0,8},{8,16},{16,24},{24,28},{28,20},{20,12},{12,4},{4,0},{1,9},{9... | collective-permute-start | bytes 3096584 | tf_op jit(solution)/shard_map/ppermute | solution.py:530
  240.1 21.8 %collective-permute-start.43 = (bf16[3,1344,128]{2,1,0:T(8,128)(2,1)S(1)}, bf16[3,1344,128]{2,1,0:T(8,128)(2,1)S(1)}, u32[]{:S(2)}, u32[]{:S(2)}) collective-permute-start(bf16[3,1344,128]{2,1,0:T(8,128)(2,1)S(1)} %get-tuple-element.61), channel_id=1, source_target_pairs={{8,0},{16,8},{24,16},{28,24},{20,28},{12,20},{4,12},{0,4},{9,1},{1... | collective-permute-start | bytes 3096584 | tf_op jit(solution)/shard_map/ppermute | solution.py:533
  262.4 21.2 %collective-permute-start.44 = (bf16[3,1344,128]{2,1,0:T(8,128)(2,1)S(1)}, bf16[3,1344,128]{2,1,0:T(8,128)(2,1)S(1)}, u32[]{:S(2)}, u32[]{:S(2)}) collective-permute-start(bf16[3,1344,128]{2,1,0:T(8,128)(2,1)S(1)} %fusion.5), channel_id=1, source_target_pairs={{0,2},{1,3},{2,0},{3,1},{4,6},{5,7},{6,4},{7,5},{8,10},{9,11},{10,... | collective-permute-start | bytes 3096584 | tf_op jit(solution)/shard_map/ppermute | solution.py:474
  284.7 23.4 %collective-permute-start.45 = (bf16[3,1344,128]{2,1,0:T(8,128)(2,1)S(1)}, bf16[3,1344,128]{2,1,0:T(8,128)(2,1)S(1)}, u32[]{:S(2)}, u32[]{:S(2)}) collective-permute-start(bf16[3,1344,128]{2,1,0:T(8,128)(2,1)S(1)} %get-tuple-element.57.own), channel_id=1, source_target_pairs={{0,1},{1,0},{2,3},{3,2},{4,5},{5,4},{6,7},{7,6},{8,9},{9,8},{10,11... | collective-permute-start | bytes 3096584 | tf_op jit(solution)/shard_map/ppermute | solution.py:474
  292.4 5.5 %collective-permute-start.28 = (f32[22,96]{1,0:T(8,128)S(1)}, f32[22,96]{1,0:T(8,128)S(1)}, u32[]{:S(2)}, u32[]{:S(2)}) collective-permute-start(f32[22,96]{1,0:T(8,128)S(1)} %bitcast.130), channel_id=1, source_target_pairs={{0,4},{4,0},{8,12},{12,8},{16,20},{20,16},{24,28},{28,24},{1,5},{5... | collective-permute-start | bytes 25352 | tf_op jit(solution)/shard_map/ppermute | solution.py:478
  293.9 5.9 %collective-permute-start.29 = (f32[22,96]{1,0:T(8,128)S(1)}, f32[22,96]{1,0:T(8,128)S(1)}, u32[]{:S(2)}, u32[]{:S(2)}) collective-permute-start(f32[22,96]{1,0:T(8,128)S(1)} %bitcast.129), channel_id=1, source_target_pairs={{0,8},{4,12},{8,0},{12,4},{16,24},{20,28},{24,16},{28,20},{1,9},{5... | collective-permute-start | bytes 25352 | tf_op jit(solution)/shard_map/ppermute | solution.py:478
  295.2 5.9 %collective-permute-start.30 = (f32[22,96]{1,0:T(8,128)S(1)}, f32[22,96]{1,0:T(8,128)S(1)}, u32[]{:S(2)}, u32[]{:S(2)}) collective-permute-start(f32[22,96]{1,0:T(8,128)S(1)} %bitcast.127), channel_id=1, source_target_pairs={{0,12},{4,8},{8,4},{12,0},{16,28},{20,24},{24,20},{28,16},{1,13},{... | collective-permute-start | bytes 25352 | tf_op jit(solution)/shard_map/ppermute | solution.py:478
  295.9 7.7 %collective-permute-start.31 = (f32[22,96]{1,0:T(8,128)S(1)}, f32[22,96]{1,0:T(8,128)S(1)}, u32[]{:S(2)}, u32[]{:S(2)}) collective-permute-start(f32[22,96]{1,0:T(8,128)S(1)} %bitcast.125), channel_id=1, source_target_pairs={{0,16},{4,20},{8,24},{12,28},{16,0},{20,4},{24,8},{28,12},{1,17},{... | collective-permute-start | bytes 25352 | tf_op jit(solution)/shard_map/ppermute | solution.py:478
  297.9 5.8 %collective-permute-start.32 = (f32[22,96]{1,0:T(8,128)S(1)}, f32[22,96]{1,0:T(8,128)S(1)}, u32[]{:S(2)}, u32[]{:S(2)}) collective-permute-start(f32[22,96]{1,0:T(8,128)S(1)} %bitcast.128), channel_id=1, source_target_pairs={{0,20},{4,16},{8,28},{12,24},{16,4},{20,0},{24,12},{28,8},{1,21},{... | collective-permute-start | bytes 25352 | tf_op jit(solution)/shard_map/ppermute | solution.py:478
  299.8 5.5 %collective-permute-start.33 = (f32[22,96]{1,0:T(8,128)S(1)}, f32[22,96]{1,0:T(8,128)S(1)}, u32[]{:S(2)}, u32[]{:S(2)}) collective-permute-start(f32[22,96]{1,0:T(8,128)S(1)} %bitcast.126), channel_id=1, source_target_pairs={{0,24},{4,28},{8,16},{12,20},{16,8},{20,12},{24,0},{28,4},{1,25},{... | collective-permute-start | bytes 25352 | tf_op jit(solution)/shard_map/ppermute | solution.py:478
  301.1 6.4 %collective-permute-start.34 = (f32[22,96]{1,0:T(8,128)S(1)}, f32[22,96]{1,0:T(8,128)S(1)}, u32[]{:S(2)}, u32[]{:S(2)}) collective-permute-start(f32[22,96]{1,0:T(8,128)S(1)} %bitcast.124), channel_id=1, source_target_pairs={{0,28},{4,24},{8,20},{12,16},{16,12},{20,8},{24,4},{28,0},{1,29},{... | collective-permute-start | bytes 25352 | tf_op jit(solution)/shard_map/ppermute | solution.py:478
  311.2 7.3 %collective-permute-start.46 = (f32[1,128]{1,0:T(1,128)S(1)}, f32[1,128]{1,0:T(1,128)S(1)}, u32[]{:S(2)}, u32[]{:S(2)}) collective-permute-start(f32[1,128]{1,0:T(1,128)S(1)} %broadcast_in_dim.41), channel_id=1, source_target_pairs={{0,4},{4,0},{8,12},{12,8},{16,20},{20,16},{24,28},{28,24},{1,5},{5... | collective-permute-start | bytes 1544 | tf_op jit(solution)/shard_map/ppermute | solution.py:478
  312.6 7.6 %collective-permute-start.47 = (f32[1,128]{1,0:T(1,128)S(1)}, f32[1,128]{1,0:T(1,128)S(1)}, u32[]{:S(2)}, u32[]{:S(2)}) collective-permute-start(f32[1,128]{1,0:T(1,128)S(1)} %broadcast_in_dim.41), channel_id=1, source_target_pairs={{0,8},{4,12},{8,0},{12,4},{16,24},{20,28},{24,16},{28,20},{1,9},{5... | collective-permute-start | bytes 1544 | tf_op jit(solution)/shard_map/ppermute | solution.py:478
  312.6 11.6 %collective-permute-start.48 = (f32[1,128]{1,0:T(1,128)S(1)}, f32[1,128]{1,0:T(1,128)S(1)}, u32[]{:S(2)}, u32[]{:S(2)}) collective-permute-start(f32[1,128]{1,0:T(1,128)S(1)} %broadcast_in_dim.41), channel_id=1, source_target_pairs={{0,12},{4,8},{8,4},{12,0},{16,28},{20,24},{24,20},{28,16},{1,13},{... | collective-permute-start | bytes 1544 | tf_op jit(solution)/shard_map/ppermute | solution.py:478
  314.7 9.5 %collective-permute-start.49 = (f32[1,128]{1,0:T(1,128)S(1)}, f32[1,128]{1,0:T(1,128)S(1)}, u32[]{:S(2)}, u32[]{:S(2)}) collective-permute-start(f32[1,128]{1,0:T(1,128)S(1)} %broadcast_in_dim.41), channel_id=1, source_target_pairs={{0,16},{4,20},{8,24},{12,28},{16,0},{20,4},{24,8},{28,12},{1,17},{... | collective-permute-start | bytes 1544 | tf_op jit(solution)/shard_map/ppermute | solution.py:478
  315.9 8.4 %collective-permute-start.50 = (f32[1,128]{1,0:T(1,128)S(1)}, f32[1,128]{1,0:T(1,128)S(1)}, u32[]{:S(2)}, u32[]{:S(2)}) collective-permute-start(f32[1,128]{1,0:T(1,128)S(1)} %broadcast_in_dim.41), channel_id=1, source_target_pairs={{0,20},{4,16},{8,28},{12,24},{16,4},{20,0},{24,12},{28,8},{1,21},{... | collective-permute-start | bytes 1544 | tf_op jit(solution)/shard_map/ppermute | solution.py:478
  318.5 5.8 %collective-permute-start.51 = (f32[1,128]{1,0:T(1,128)S(1)}, f32[1,128]{1,0:T(1,128)S(1)}, u32[]{:S(2)}, u32[]{:S(2)}) collective-permute-start(f32[1,128]{1,0:T(1,128)S(1)} %broadcast_in_dim.41), channel_id=1, source_target_pairs={{0,24},{4,28},{8,16},{12,20},{16,8},{20,12},{24,0},{28,4},{1,25},{... | collective-permute-start | bytes 1544 | tf_op jit(solution)/shard_map/ppermute | solution.py:478
  320.2 6.3 %collective-permute-start.52 = (f32[1,128]{1,0:T(1,128)S(1)}, f32[1,128]{1,0:T(1,128)S(1)}, u32[]{:S(2)}, u32[]{:S(2)}) collective-permute-start(f32[1,128]{1,0:T(1,128)S(1)} %broadcast_in_dim.41), channel_id=1, source_target_pairs={{0,28},{4,24},{8,20},{12,16},{16,12},{20,8},{24,4},{28,0},{1,29},{... | collective-permute-start | bytes 1544 | tf_op jit(solution)/shard_map/ppermute | solution.py:478
  (25 other events, 476.3 us)

commit v2 on v1

--- a/solution.py
+++ b/solution.py
@@ -28,6 +28,11 @@
 bf16 = jnp.bfloat16
 
 ROW_P, ROW_QKV, ROW_O, ROW_ONE, ROW_TWO, ROW_H, ROWS = 0, 96, 384, 480, 864, 1248, 1344
+VEC_ROWS = 32
+PLACES = ((4,), (3, 5), (2, 6, 1, 7, 0))
+SPLIT_PLACES = ((4, 3, 5), (2, 6, 1, 7, 0))
+OUTS = 2 * len(PLACES) + 2 * len(SPLIT_PLACES)
+PART, CUT, BLOCK = 8, 24, 48
 
 
 def nn(left, right):
@@ -61,28 +66,50 @@
     return jnp.sum(value, 0, keepdims=True)
 
 
-def step_kernel(pieces, n_refs, *refs):
-    info = refs[0]
-    pix, target, mask, pos, vec, bias = refs[1:7]
-    sources = refs[7 : 7 + n_refs]
-    keep, send, vgrad, loss = refs[7 + n_refs : 11 + n_refs]
-    (w, x0, x1, x2, branch, mlp, work, qkv, probs, attn, slope, act, hid, low, sem_in, sem_out) = refs[
-        11 + n_refs :
-    ]
+def step_kernel(pieces, vec_pieces, n_refs, *refs):
+    info, pos = refs[:2]
+    n_parts = n_refs[0]
+    parcels, sources = refs[2 : 2 + n_parts], refs[2 + n_parts : 2 + sum(n_refs)]
+    *outs, vgrad = refs[2 + sum(n_refs) : 3 + sum(n_refs) + OUTS]
+    w, vec_blocks, vec, pix, target, mask_rows, mask, bias, *refs = refs[3 + sum(n_refs) + OUTS :]
+    (x0, x1, x2, branch, mlp, work, qkv, probs, attn, slope, act, hid, low, sem_in, sem_part, sem_out) = refs
     length, width = pix.shape
+    part = length // n_parts
     pairs = width // 256
     first, second = (0, ROW_ONE), (ROW_ONE, ROWS)
 
+    for k in range(n_parts):
+        slot = info[PART + k]
+        here = pl.ds(pl.multiple_of(slot * part, part), part)
+        pltpu.make_async_copy(parcels[k].at[:part], pix.at[here], sem_part.at[0]).start()
+        pltpu.make_async_copy(parcels[k].at[part : 2 * part], target.at[here], sem_part.at[1]).start()
+        pltpu.make_async_copy(parcels[k].at[2 * part :, :LANES], mask_rows.at[slot], sem_part.at[2]).start()
+
+    for source, lead, row, block_slot in vec_pieces:
+        pltpu.make_async_copy(
+            sources[source].at[lead, row : row + VEC_ROWS], vec_blocks.at[info[block_slot]], sem_part.at[3]
+        ).start()
+
     for group, (begin, end) in enumerate((first, second)):
-        for source, lead, cut_slot, block_slot, row, rows in pieces:
-            lo, hi = max(begin, row), min(end, row + rows)
-            if lo >= hi:
-                continue
+        for source, lead, cut_slot, block_slot in pieces:
             pltpu.make_async_copy(
-                sources[source].at[lead, lo - row : hi - row],
-                w.at[info[cut_slot], info[block_slot], lo:hi],
+                sources[source].at[lead, begin:end],
+                w.at[info[cut_slot], info[block_slot], begin:end],
                 sem_in.at[group],
             ).start()
+
+    for number, whole in enumerate((pix, target, mask_rows, vec_blocks)):
+        pltpu.make_async_copy(whole, whole, sem_part.at[number]).wait()
+    diagonal = lax.broadcasted_iota(jnp.int32, (part, LANES), 0) == lax.broadcasted_iota(
+        jnp.int32, (part, LANES), 1
+    )
+    for k in range(n_parts):
+        row = mask_rows[k].astype(f32)[:1]
+        mask[part * k : part * k + part, :] = jnp.sum(jnp.where(diagonal, row, 0.0), 1, keepdims=True)
+    for q in range(BLOCKS):
+        vec[:, 96 * q : 96 * q + 96] = vec_blocks[q].astype(f32)[:, :96]
+    for k in range(4):
+        bias[:, width * k : width * k + width] = vec[16 + k : 17 + k, :]
 
     def arrived(group, begin, end):
         part = w.at[:, :, begin:end]
@@ -107,16 +134,30 @@
         put(2 * i, row, 96, value[:, :LANES])
         put(2 * i + 1, row, 96, value[:, LANES:])
 
+    def out_rows(number, begin, end):
+        return (begin, end) if number < 2 * len(PLACES) else (begin // 2, end // 2)
+
     def leave(group, begin, end):
-        core = info[0]
-        for block_index in range(BLOCKS):
-            place = info[8 + block_index]
-            for number, (out, base) in enumerate(((keep, 3 * core), (send, 3 - 3 * core))):
-                pltpu.make_async_copy(
-                    w.at[pl.ds(base, 3), block_index, begin:end],
-                    out.at[place, :, begin:end],
-                    sem_out.at[number, group],
-                ).start()
+        core, side = info[0], info[1]
+        half = (end - begin) // 2
+        for number, out in enumerate(outs):
+            split, away = number >= 2 * len(PLACES), number % 2
+            first_cut = 3 * (core ^ away)
+            lo, hi = out_rows(number, begin, end)
+            for i, place in enumerate((PLACES + SPLIT_PLACES)[number // 2]):
+                block_index = info[BLOCK + place]
+                if not split:
+                    pltpu.make_async_copy(
+                        w.at[pl.ds(first_cut, 2), block_index, begin:end],
+                        out.at[i, :, lo:hi],
+                        sem_out.at[number, group],
+                    ).start()
+                    continue
+                for part in range(2):
+                    rows = pl.ds(pl.multiple_of(begin + half * (side ^ part), 16), half)
+                    pltpu.make_async_copy(
+                        w.at[first_cut + 2, block_index, rows], out.at[i, part, lo:hi], sem_out.at[number, group]
+                    ).start()
 
     row_index = lax.broadcasted_iota(jnp.int32, (length, 1), 0)
     is_class = row_index == GRID * GRID
@@ -198,7 +239,8 @@
 
     normed3, inverse3 = stats(x2[...])
     low[...] = (normed3 * vec[13:14, :] + vec[14:15, :]).astype(bf16)
-    loss[...] = jnp.zeros_like(loss)
+    loss = work
+    loss[0:1, 0:256] = jnp.zeros((1, 256), f32)
 
     @pl.loop(0, pairs)
     def _(i):
@@ -211,6 +253,9 @@
         vgrad[15:16, c] = column_sum(grad)
         hid[:, c] = grad.astype(bf16)
 
+    vgrad[20:21, :] = jnp.broadcast_to(jnp.sum(loss[0:1, 0:256], 1, keepdims=True), (1, width))
+    vgrad[21:22, :] = jnp.broadcast_to(jnp.sum(mask[...], 0, keepdims=True), (1, width))
+    vgrad[22:24, :] = jnp.zeros((2, width), f32)
     upstream = nt(hid[...], all_cuts(ROW_H))
     vgrad[13:14, :] = column_sum(upstream * normed3)
     vgrad[14:15, :] = column_sum(upstream)
@@ -332,32 +377,42 @@
         put_pair(i, ROW_P, nn(flipped, hid[:, cols(i)]))
 
     leave(0, *first)
-    for number, out in enumerate((keep, send)):
+    for number, out in enumerate(outs):
         for group, (begin, end) in enumerate((first, second)):
-            part = out.at[:, :, begin:end]
-            pltpu.make_async_copy(part, part, sem_out.at[number, group]).wait()
-
-
-def run_step(info, pix, target, mask, pos, vec, bias, pieces, sources):
-    length, width = pix.shape
-    hidden = bias.shape[1]
+            lo, hi = out_rows(number, begin, end)
+            rows = out.at[:, :, lo:hi]
+            pltpu.make_async_copy(rows, rows, sem_out.at[number, group]).wait()
+
+
+def run_step(info, pos, parcels, pieces, vec_pieces, sources):
+    length, width = pos.shape
+    hidden = 4 * width
     vmem = pl.BlockSpec(memory_space=pltpu.VMEM)
     anywhere = pl.BlockSpec(memory_space=pl.ANY)
-    half = jax.ShapeDtypeStruct((BLOCKS, 3, ROWS, LANES), bf16)
     big = pltpu.VMEM((length, width), f32)
     small = pltpu.VMEM((length, width), bf16)
-    return pl.pallas_call(
-        partial(step_kernel, pieces, len(sources)),
+    *outs, vgrad = pl.pallas_call(
+        partial(step_kernel, pieces, vec_pieces, (len(parcels), len(sources))),
         out_shape=(
-            half,
-            half,
+            *(jax.ShapeDtypeStruct((len(places), 2, ROWS, LANES), bf16) for places in PLACES for _ in range(2)),
+            *(
+                jax.ShapeDtypeStruct((len(places), 2, ROWS // 2, LANES), bf16)
+                for places in SPLIT_PLACES
+                for _ in range(2)
+            ),
             jax.ShapeDtypeStruct((24, width), f32),
-            jax.ShapeDtypeStruct((8, 256), f32),
         ),
-        in_specs=[pl.BlockSpec(memory_space=pltpu.SMEM)] + [vmem] * 6 + [anywhere] * len(sources),
-        out_specs=(anywhere, anywhere, vmem, vmem),
+        in_specs=[pl.BlockSpec(memory_space=pltpu.SMEM)] + [vmem] + [anywhere] * (len(parcels) + len(sources)),
+        out_specs=(*[anywhere] * OUTS, vmem),
         scratch_shapes=[
             pltpu.VMEM((CUTS, BLOCKS, ROWS, LANES), bf16),
+            pltpu.VMEM((BLOCKS, VEC_ROWS, LANES), bf16),
+            pltpu.VMEM((VEC_ROWS, width), f32),
+            small,
+            small,
+            pltpu.VMEM((len(parcels), 16, LANES), bf16),
+            pltpu.VMEM((length, 1), f32),
+            pltpu.VMEM((1, hidden), f32),
             big,
             big,
             big,
@@ -372,14 +427,16 @@
             small,
             small,
             pltpu.SemaphoreType.DMA((2,)),
-            pltpu.SemaphoreType.DMA((2, 2)),
+            pltpu.SemaphoreType.DMA((4,)),
+            pltpu.SemaphoreType.DMA((OUTS, 2)),
         ],
         compiler_params=pltpu.CompilerParams(vmem_limit_bytes=60 * 1024 * 1024),
         name="step",
-    )(info, pix, target, mask, pos, vec, bias, *sources)
-
-
-def pack_kernel(square, joint, expand, reduce, out):
+    )(info, pos, *parcels, *sources)
+    return outs, vgrad
+
+
+def pack_kernel(chosen, square, joint, expand, reduce, vectors, out, *streams):
     for cut in range(CUTS):
         for row, n, rows, take in (
             (ROW_P, 1, 96, lambda c: square[0, :, c]),
@@ -392,17 +449,49 @@
             for j in range(n):
                 begin = LANES * (n * cut + j)
                 out[cut, row + rows * j : row + rows * j + rows, :] = take(slice(begin, begin + LANES)).astype(bf16)
-
-
-def pack(square, joint, expand, reduce):
+    for number, stream in enumerate(streams):
+        for i in range(2):
+            stream[i, :ROWS] = out[chosen[2 * number + i]]
+            stream[i, ROWS:] = jnp.zeros((VEC_ROWS, LANES), bf16)
+            stream[i, ROWS:, : vectors.shape[1]] = jnp.concatenate(
+                [vectors[...], jnp.zeros((VEC_ROWS - vectors.shape[0], vectors.shape[1]), f32)]
+            ).astype(bf16)
+
+
+def pack(chosen, *shards):
     vmem = pl.BlockSpec(memory_space=pltpu.VMEM)
     return pl.pallas_call(
         pack_kernel,
-        out_shape=jax.ShapeDtypeStruct((CUTS, ROWS, LANES), bf16),
-        in_specs=[vmem] * 4,
-        out_specs=vmem,
+        out_shape=[jax.ShapeDtypeStruct((CUTS, ROWS, LANES), bf16)]
+        + [jax.ShapeDtypeStruct((2, ROWS + VEC_ROWS, LANES), bf16)] * 2,
+        in_specs=[pl.BlockSpec(memory_space=pltpu.SMEM)] + [vmem] * 5,
+        out_specs=[vmem] * 3,
         name="pack",
-    )(square, joint, expand, reduce)
+    )(chosen, *shards)
+
+
+def parcel_kernel(slots, pixels, block_mask, targets, *outs):
+    length = pixels.shape[1]
+    top = lax.broadcasted_iota(jnp.int32, (16, length), 0) == 0
+    for k, out in enumerate(outs):
+        slot = slots[k]
+        out[:length, :] = pixels[slot]
+        out[length : 2 * length, :] = targets[slot]
+        out[2 * length :, :] = jnp.zeros((16, out.shape[1]), bf16)
+        row = block_mask[pl.ds(slot, 1), :].astype(f32)
+        out[2 * length :, :length] = jnp.where(top, row, 0.0).astype(bf16)
+
+
+def make_parcels(slots, pixels, block_mask, targets):
+    images, length, features = pixels.shape
+    vmem = pl.BlockSpec(memory_space=pltpu.VMEM)
+    return pl.pallas_call(
+        parcel_kernel,
+        out_shape=[jax.ShapeDtypeStruct((2 * length + 16, features), bf16)] * images,
+        in_specs=[pl.BlockSpec(memory_space=pltpu.SMEM)] + [vmem] * 3,
+        out_specs=[vmem] * images,
+        name="parcels",
+    )(slots, pixels, block_mask, targets)
 
 
 def adam(weight, moment, variance, grad, rate, decay):
@@ -410,57 +499,94 @@
     variance_new = beta_two * variance + (1.0 - beta_two) * grad * grad
     corrected = (
         moment_new
-        / (1.0 - beta_one**adam_step)
-        / (jnp.sqrt(variance_new / (1.0 - beta_two**adam_step)) + adam_eps)
+        * (1.0 / (1.0 - beta_one**adam_step))
+        / (jnp.sqrt(variance_new * (1.0 / (1.0 - beta_two**adam_step))) + adam_eps)
     )
     return (moment_new, variance_new, weight - rate * (corrected + decay * weight))
 
 
-def adam_kernel(core, factor, own, other, *refs):
-    states, outs = refs[:12], refs[12:]
-    cut = pl.program_id(0)
-    mine = cut // 3 == core[0]
-    scale = factor[0]
-
-    def grad_of(row, rows):
-        index = lax.rem(cut, 3)
-        grad = jnp.where(mine, own[index, row : row + rows, :], other[index, row : row + rows, :])
-        return grad.astype(f32) * scale
-
-    def update(kind, where, row, rows):
-        weight, moment, variance = (states[4 * k + kind][where] for k in range(3))
-        results = adam(weight, moment, variance, grad_of(row, rows), matrix_rate, weight_decay)
-        for k, result in enumerate(results):
-            outs[4 * k + kind][where] = result
-
-    for i, row in enumerate((ROW_P, ROW_O, ROW_H)):
-        update(0, (i,), row, 96)
-    for j in range(3):
-        update(1, (slice(None), slice(LANES * j, LANES * j + LANES)), ROW_QKV + 96 * j, 96)
-    for j in range(4):
-        update(2, (slice(None), slice(LANES * j, LANES * j + LANES)), ROW_ONE + 96 * j, 96)
-    update(3, (slice(None), slice(None)), ROW_TWO, 384)
-
-
-def adam_all(core, factor, own, other, masters, moments, variances):
+def adam_kernel(core, squares, table, own, split_own, other, split_other, *refs):
+    masters, moments, variances = refs[:5], refs[5:10], refs[10:15]
+    loss_out, norm_out, *outs = refs[15:32]
+    buffers, sem_in, sem_out = refs[32:44], *refs[44:]
+    order = (3, 2, 1, 0)
+    for kind in order:
+        for k, state in enumerate((masters, moments, variances)):
+            pltpu.make_async_copy(state[kind], buffers[4 * k + kind], sem_in.at[4 * k + kind]).start()
+    rows = masters[4].shape[0]
+    count = table[rows + 1 : rows + 2, 0:1]
+    norm = jnp.sqrt(squares[0:1, 0:1]) / count
+    scale = clip_limit / jnp.maximum(norm, clip_limit) / count
+    loss_out[0, 0] = (table[rows : rows + 1, 0:1] / count)[0, 0]
+    norm_out[0, 0] = norm[0, 0]
+
+    def grad_of(cut, row, rows):
+        mine = cut // 3 == core[0]
+        index, part = jnp.minimum(lax.rem(cut, 3), 1), slice(row, row + rows)
+        grad = jnp.where(mine, own[index, part, :], other[index, part, :])
+        split = jnp.where(mine, split_own[part, :], split_other[part, :])
+        return jnp.where(lax.rem(cut, 3) == 2, split, grad).astype(f32) * scale
+
+    def update(kind, where, cut, row, rows):
+        states = (buffers[4 * k + kind][where] for k in range(3))
+        values = adam(*states, grad_of(cut, row, rows), matrix_rate, weight_decay)
+        for k, value in zip((1, 2, 0), values):
+            buffers[4 * k + kind][where] = value
+
+    def each(kind, body):
+        for k, state in enumerate((masters, moments, variances)):
+            pltpu.make_async_copy(state[kind], buffers[4 * k + kind], sem_in.at[4 * k + kind]).wait()
+        pl.loop(0, CUTS)(body)
+        for k in range(3):
+            out = outs[5 * ((k + 2) % 3) + kind]
+            pltpu.make_async_copy(buffers[4 * k + kind], out, sem_out.at[4 * k + kind]).start()
+
+    def lanes(block):
+        return pl.ds(pl.multiple_of(block * LANES, LANES), LANES)
+
+    def reduce_body(cut):
+        for k in range(4):
+            update(3, (slice(96 * k, 96 * k + 96), lanes(cut)), cut, ROW_TWO + 96 * k, 96)
+
+    def expand_body(cut):
+        for k in range(4):
+            update(2, (slice(None), lanes(4 * cut + k)), cut, ROW_ONE + 96 * k, 96)
+
+    def joint_body(cut):
+        for k in range(3):
+            update(1, (slice(None), lanes(3 * cut + k)), cut, ROW_QKV + 96 * k, 96)
+
+    def square_body(cut):
+        for i, row in enumerate((ROW_P, ROW_O, ROW_H)):
+            update(0, (i, slice(None), lanes(cut)), cut, row, 96)
+
+    for kind, body in zip(order, (reduce_body, expand_body, joint_body, square_body)):
+        each(kind, body)
+    states = (state[4][...] for state in (masters, moments, variances))
+    for k, value in enumerate(adam(*states, table[:rows, :] * scale, vector_rate, 0.0)):
+        outs[5 * k + 4][...] = value
+    for k in range(3):
+        for kind in range(4):
+            out = outs[5 * ((k + 2) % 3) + kind]
+            pltpu.make_async_copy(buffers[4 * k + kind], out, sem_out.at[4 * k + kind]).wait()
+
+
+def adam_all(core, squares, table, grads, masters, moments, variances):
     smem = pl.BlockSpec(memory_space=pltpu.SMEM)
-    whole = pl.BlockSpec(memory_space=pltpu.VMEM)
-    blocks = [
-        pl.BlockSpec((3, 96, LANES), lambda i: (0, 0, i)),
-        pl.BlockSpec((96, 3 * LANES), lambda i: (0, i)),
-        pl.BlockSpec((96, 4 * LANES), lambda i: (0, i)),
-        pl.BlockSpec((384, LANES), lambda i: (0, i)),
-    ]
-    outs = [jax.ShapeDtypeStruct(master.shape, f32) for master in masters]
-    results = pl.pallas_call(
+    vmem = pl.BlockSpec(memory_space=pltpu.VMEM)
+    anywhere = pl.BlockSpec(memory_space=pl.ANY)
+    shapes = [jax.ShapeDtypeStruct(master.shape, f32) for master in masters]
+    loss, norm, *results = pl.pallas_call(
         adam_kernel,
-        grid=(CUTS,),
-        out_shape=outs * 3,
-        in_specs=[smem, smem, whole, whole] + blocks * 3,
-        out_specs=blocks * 3,
+        out_shape=[jax.ShapeDtypeStruct((1, 1), f32)] * 2 + shapes * 3,
+        in_specs=[smem] + [vmem] * (2 + len(grads)) + ([anywhere] * 4 + [vmem]) * 3,
+        out_specs=[smem] * 2 + ([anywhere] * 4 + [vmem]) * 3,
+        scratch_shapes=[pltpu.VMEM(shape.shape, f32) for shape in shapes[:4] * 3]
+        + [pltpu.SemaphoreType.DMA((12,))] * 2,
+        compiler_params=pltpu.CompilerParams(vmem_limit_bytes=56 * 1024 * 1024),
         name="adam",
-    )(core, factor, own, other, *masters, *moments, *variances)
-    return (results[:4], results[4:8], results[8:])
+    )(core, squares, table, *grads, *masters, *moments, *variances)
+    return loss.reshape(()), norm.reshape(()), results[:5], results[5:10], results[10:]
 
 
 def positions(slot_float, features):
@@ -474,27 +600,13 @@
     return lax.ppermute(value, "seq", [(i, i ^ k) for i in range(n_seq)])
 
 
-def dp_flip(value, k, n_dp):
-    return lax.ppermute(value, "dp", [(i, i ^ k) for i in range(n_dp)])
-
-
-def whole_image(pixels, block_mask, targets, n_seq):
-    images, length, features = pixels.shape
-    mask_rows = jnp.zeros((images, 16, features), bf16)
-    mask_rows = lax.dynamic_update_slice(mask_rows, block_mask.astype(bf16)[:, None, :], (0, 0, 0))
-    parcels = jnp.concatenate([pixels, targets, mask_rows], 1)
-    me = lax.axis_index("seq")
-
-    def parcel(k):
-        return lax.dynamic_index_in_dim(parcels, me ^ k, 0, keepdims=False)
-
-    got = jnp.stack([parcel(0)] + [seq_flip(parcel(k), k, n_seq) for k in range(1, n_seq)])
-    got = jnp.take(got, me ^ jnp.arange(n_seq), axis=0)
-    return (
-        got[:, :length].reshape(n_seq * length, features),
-        got[:, length : 2 * length].reshape(n_seq * length, features),
-        got[:, 2 * length, :length].reshape(n_seq * length).astype(f32),
-    )
+def hop(value, dp_k, seq_k, n_dp, n_seq):
+    pairs = [(dp * n_seq + seq, (dp ^ dp_k) * n_seq + (seq ^ seq_k)) for dp in range(n_dp) for seq in range(n_seq)]
+    return lax.ppermute(value, ("dp", "seq"), pairs)
+
+
+def tick(*values):
+    return lax.optimization_barrier(values)
 
 
 def ring_of(n_dp):
@@ -510,21 +622,27 @@
 def local(n_dp, n_seq, *args):
     pixels, block_mask, targets = args[:3]
     masters, moments, variances = args[3:8], args[8:13], args[13:18]
-    features = pixels.shape[2]
+    length, features = pixels.shape[1:]
     square, joint, expand, reduce, vectors = masters
     me, group = lax.axis_index("seq"), lax.axis_index("dp")
     ringed = n_dp == BLOCKS and n_seq == 4
-    core = me % 2 if ringed else jnp.zeros((), jnp.int32)
-    pix, target, mask = whole_image(pixels, block_mask, targets, n_seq)
-    pos = positions(jnp.arange(pix.shape[0]).astype(f32), features)
-    vectors_low = vectors.astype(bf16)
+    core, side = (me % 2, me // 2) if ringed else (jnp.zeros((), jnp.int32),) * 2
+    slots = me ^ jnp.arange(n_seq, dtype=jnp.int32)
+    slots_info = jnp.concatenate([slots, jnp.zeros(16 - n_seq, jnp.int32)])
+    eight = jnp.arange(8, dtype=jnp.int32)
+    first_info = jnp.stack([core, side] + [core] * 6).astype(jnp.int32)
+
     if ringed:
         ring = ring_of(n_dp)
         forward = [(ring[i], ring[(i + 1) % n_dp]) for i in range(n_dp)]
         backward = [(b, a) for a, b in forward]
-        place_of = jnp.argsort(jnp.array(ring)).astype(jnp.int32)
-        ring_array = jnp.array(ring, jnp.int32)
-        place = place_of[group]
+        place = jnp.argsort(jnp.array(ring)).astype(jnp.int32)[group]
+        blocks = jnp.array(ring, jnp.int32)[(place + eight) % n_dp]
+        base = jnp.stack([3 * core, 3 - 3 * core])
+        cuts = jnp.stack([base, base + 1 + side, base + 2 - side], 1).astype(jnp.int32)
+        info = jnp.concatenate([first_info, slots_info, eight, cuts.reshape(-1), jnp.zeros(10, jnp.int32), blocks])
+        shared, on_left, on_right = CUT + 8, CUT + 9, CUT + 10
+        pieces, vec_pieces, sources = [], [], []
 
         def ahead(value):
             return lax.ppermute(value, "dp", forward)
@@ -535,49 +653,87 @@
         def across(value):
             return seq_flip(value, 1, n_seq)
 
-        stacked = jnp.stack([vectors_low] + [dp_flip(vectors_low, k, n_dp) for k in range(1, n_dp)])
-        stacked = jnp.take(stacked, group ^ jnp.arange(n_dp), axis=0)
-        vec = stacked.transpose(1, 0, 2).reshape(vectors.shape[0], features).astype(f32)
-
-        slabs = pack(square, joint, expand, reduce)
-        mine = lax.dynamic_slice_in_dim(slabs, 3 * core, 3, 0)
-        sources, pieces = [slabs], [(0, cut, 24 + cut, 48, 0, ROWS) for cut in range(CUTS)]
-
-        def add_piece(value, swapped, distance, row, rows):
-            pieces.extend(
-                (len(sources), i, 32 + 3 * swapped + i, 48 + distance, row, rows) for i in range(3)
-            )
+        def trade(value):
+            return seq_flip(value, 2, n_seq)
+
+        def note(swapped, number, left, right):
+            for value, far, kinds in (
+                (left, n_dp - number, (shared, on_left)),
+                (right, number, (on_right, shared)),
+            ):
+                if not swapped:
+                    vec_pieces.append((len(sources), kinds.index(shared), ROWS, BLOCK + far))
+                pieces.extend((len(sources), i, kind + 3 * swapped, BLOCK + far) for i, kind in enumerate(kinds))
+                sources.append(value)
+
+        def note_trade(swapped, number, value):
+            for i, (far, kind) in enumerate(((n_dp - number, on_right), (number, on_left))):
+                pieces.append((len(sources), i, kind + 3 * swapped, BLOCK + far))
             sources.append(value)
 
-        left, right = mine, mine
-        for distance in range(1, 4):
-            left, right = ahead(left), behind(right)
-            for value, far in ((left, n_dp - distance), (right, distance)):
-                add_piece(value, 0, far, 0, ROWS)
-                add_piece(across(value), 1, far, 0, ROWS)
-        half = ROWS // 2
-        left, right = ahead(left[:, :half]), behind(right[:, half:])
-        for value, row in ((left, 0), (right, half)):
-            add_piece(value, 0, 4, row, half)
-            add_piece(across(value), 1, 4, row, half)
-        info = jnp.concatenate(
-            [
-                jnp.stack([core] + [core] * 7),
-                (place_of - place) % n_dp,
-                jnp.zeros(8, jnp.int32),
-                jnp.arange(8, dtype=jnp.int32),
-                jnp.stack([3 * core + i for i in range(3)] + [3 - 3 * core + i for i in range(3)] + [core] * 10),
-                ring_array[(place + jnp.arange(8)) % n_dp],
-                jnp.zeros(8, jnp.int32),
-            ]
-        ).astype(jnp.int32)
+        def in_turn(left, right, traded):
+            left, traded = tick(across(left), traded)
+            return left, across(right), across(traded)
+
+        def for_trade(left, right):
+            return jnp.stack([left[1], right[0]])
+
+        order = jnp.stack([cuts[0, 0], cuts[0, 1], cuts[0, 2], cuts[0, 0]])
+        slabs, left0, right0 = pack(order, square, joint, expand, reduce, vectors)
+        pieces.extend((0, cut, CUT + cut, BLOCK) for cut in range(CUTS))
+        vec_pieces.append((1, 0, ROWS, BLOCK))
+        sources.extend((slabs, left0))
+        parcels = list(make_parcels(slots, pixels, block_mask, targets))
+        left1, right1, *parcels[1:] = tick(
+            ahead(left0),
+            behind(right0),
+            *(seq_flip(parcels[k], k, n_seq) for k in range(1, n_seq)),
+        )
+        note(0, 1, left1, right1)
+        pos = positions(jnp.arange(n_seq * length).astype(f32), features)
+        left2, right2, trade1, left1, right1, pos = tick(
+            ahead(left1),
+            behind(right1),
+            trade(for_trade(left1, right1)),
+            across(left1),
+            across(right1),
+            pos,
+        )
+        note(1, 1, left1, right1)
+        note(0, 2, left2, right2)
+        note_trade(0, 1, trade1)
+        left3, right3, trade2, left2, right2, trade1 = tick(
+            ahead(left2), behind(right2), trade(for_trade(left2, right2)), *in_turn(left2, right2, trade1)
+        )
+        note(1, 2, left2, right2)
+        note(0, 3, left3, right3)
+        note_trade(1, 1, trade1)
+        note_trade(0, 2, trade2)
+        left4, right4, trade3, left3, right3, trade2, info = tick(
+            ahead(left3),
+            behind(right3[:1]),
+            trade(for_trade(left3, right3)),
+            *in_turn(left3, right3, trade2),
+            info,
+        )
+        note(1, 3, left3, right3)
+        note_trade(1, 2, trade2)
+        note_trade(0, 3, trade3)
+        far = BLOCK + n_dp // 2
+        vec_pieces.append((len(sources), 0, ROWS, far))
+        for swapped, values in enumerate(((left4, right4), (across(left4), across(right4)))):
+            for number, (value, kinds) in enumerate(zip(values, ((shared, on_left), (on_right,)))):
+                pieces.extend((len(sources) + number, i, kind + 3 * swapped, far) for i, kind in enumerate(kinds))
+            sources.extend(values)
+        note_trade(1, 3, across(trade3))
     else:
+        parcels = make_parcels(slots, pixels, block_mask, targets)
+        parcels = [parcels[0]] + [seq_flip(parcels[k], k, n_seq) for k in range(1, n_seq)]
+        pos = positions(jnp.arange(n_seq * length).astype(f32), features)
         gathered = [
             lax.all_gather(value.astype(bf16), "dp", axis=axis, tiled=True)
             for value, axis in zip(masters, (1, 0, 0, 0, 1))
         ]
-        vec = gathered[4].astype(f32)
-
         def cut_up(matrix):
             rows, columns = matrix.shape
             blocks = columns // (CUTS * LANES)
@@ -586,54 +742,119 @@
 
         order = (gathered[0][0], gathered[1], gathered[0][1], gathered[2], gathered[3], gathered[0][2])
         slabs = jnp.concatenate([cut_up(matrix) for matrix in order], 2)
-        sources = [slabs.reshape(CUTS * BLOCKS, ROWS, LANES)]
-        pieces = [(0, BLOCKS * cut + q, 24 + cut, 48 + q, 0, ROWS) for cut in range(CUTS) for q in range(BLOCKS)]
-        eight = jnp.arange(8, dtype=jnp.int32)
-        info = jnp.concatenate([eight * 0, eight, eight * 0, eight, eight, eight, eight, eight])
-
-    keep, send, vgrad, loss_rows = run_step(
-        info, pix, target, mask[:, None], pos, vec, vec[16:].reshape(1, -1), tuple(pieces), tuple(sources)
-    )
+        vec_slabs = gathered[4].reshape(vectors.shape[0], BLOCKS, features // BLOCKS).transpose(1, 0, 2)
+        vec_slabs = jnp.pad(vec_slabs, ((0, 0), (0, VEC_ROWS - vectors.shape[0]), (0, LANES - features // BLOCKS)))
+        sources = [slabs.reshape(CUTS * BLOCKS, ROWS, LANES), vec_slabs]
+        pieces = [(0, BLOCKS * cut + q, CUT + cut, BLOCK + q) for cut in range(CUTS) for q in range(BLOCKS)]
+        vec_pieces = [(1, q, 0, BLOCK + q) for q in range(BLOCKS)]
+        info = jnp.concatenate([first_info, slots_info, eight, jnp.zeros(16, jnp.int32), eight])
+
+    outs, vgrad = run_step(info, pos, tuple(parcels), tuple(pieces), tuple(vec_pieces), tuple(sources))
     rows = vectors.shape[0]
-    loss_part, count_part = jnp.sum(loss_rows), jnp.sum(mask)
+    n_whole = 2 * len(PLACES)
+    keeps, sends = outs[0:n_whole:2], outs[1:n_whole:2]
+    split_keeps, split_sends = outs[n_whole::2], outs[n_whole + 1 :: 2]
+
+    def join_halves(low, high):
+        cut = ROW_ONE // 2
+        return jnp.concatenate([low[..., :cut, :], high[..., :cut, :], low[..., cut:, :], high[..., cut:, :]], -2)
 
     if ringed:
-        got = across(send)
-
-        def partial_sum(r, part=slice(None)):
-            return keep[r][:, part].astype(f32) + got[r][:, part].astype(f32)
-
-        low_part, high_part = slice(0, half), slice(half, ROWS)
-        left = ahead(partial_sum(4, low_part).astype(bf16))
-        right = behind(partial_sum(4, high_part).astype(bf16))
-        left = jnp.concatenate([partial_sum(3, low_part) + left.astype(f32), partial_sum(3, high_part)], 1)
-        right = jnp.concatenate([partial_sum(5, low_part), partial_sum(5, high_part) + right.astype(f32)], 1)
-        for r in (2, 1, 0):
-            left, right = ahead(left.astype(bf16)).astype(f32), behind(right.astype(bf16)).astype(f32)
-            if r:
-                left, right = left + partial_sum(r), right + partial_sum(8 - r)
-        own = (partial_sum(0) + left + right).astype(bf16)
-        other_chip = seq_flip(own, 2, n_seq)
-        own = (own.astype(f32) + other_chip.astype(f32)).astype(bf16)
-        other = across(own)
-
-        extra = jnp.stack([jnp.full((features,), loss_part), jnp.full((features,), count_part)])
-        small = jnp.concatenate([vgrad[:rows], extra]).reshape(rows + 2, n_dp, -1).transpose(1, 0, 2)
-        for k in (1, 2):
-            small = small + seq_flip(small, k, n_seq)
-
-        def row_of(k):
-            return lax.dynamic_index_in_dim(small, group ^ k, 0, keepdims=False)
-
-        small = tree_sum([row_of(0)] + [dp_flip(row_of(k), k, n_dp) for k in range(1, n_dp)])
-        vector_grad, loss_sum, count = small[:rows], small[rows, 0], small[rows + 1, 0]
-        squares = (
-            jnp.sum(jnp.square(own.astype(f32))) + jnp.sum(jnp.square(other.astype(f32))) + jnp.sum(vector_grad**2)
-        )
-        squares = jnp.full((1, LANES), squares)
-        squares = tree_sum([squares] + [dp_flip(squares, k, n_dp) for k in range(1, n_dp)])[0, 0]
+        def rounded(*values):
+            return sum(value.astype(f32) for value in values).astype(bf16)
+
+        def low_half(value):
+            return jnp.pad(value.astype(f32), ((0, 1), (0, 0), (0, 0)))
+
+        def high_half(value):
+            return jnp.pad(value.astype(f32), ((1, 0), (0, 0), (0, 0)))
+
+        small = vgrad.reshape(-1, n_dp, features // n_dp).transpose(1, 0, 2)
+        opposite, split_first, next_got, small, small_more, send_rest, split_send_rest = tick(
+            rounded(keeps[0], across(sends[0])),
+            rounded(split_keeps[0], across(split_sends[0])),
+            across(sends[1]),
+            small,
+            across(small),
+            sends[2],
+            split_sends[1],
+        )
+        small = small + small_more
+        whole, split = {}, dict(zip((4, 3, 5), split_first[:, 0]))
+        left, right, pair_first, whole_next, got_rest, split_rest = tick(
+            ahead(opposite[0, :1]),
+            behind(opposite[0, 1:]),
+            trade(split_first[:, 1]),
+            rounded(keeps[1], next_got),
+            across(send_rest),
+            rounded(split_keeps[1], across(split_send_rest)),
+        )
+        whole.update(zip((3, 5), whole_next))
+        split.update(zip((2, 6, 1, 7, 0), split_rest[:, 0]))
+        pair = dict(zip((4, 3, 5), pair_first))
+        left, right, split_left, pair_rest, whole_rest, small, small_more = tick(
+            ahead(rounded(whole[3], low_half(left))),
+            behind(rounded(whole[5], high_half(right))),
+            ahead(rounded(split[4], pair[4])),
+            trade(split_rest[:, 1]),
+            rounded(keeps[2], got_rest),
+            small,
+            trade(small),
+        )
+        pair.update(zip((2, 6, 1, 7, 0), pair_rest))
+        whole.update(zip((2, 6, 1, 7, 0), whole_rest))
+        small = small + small_more
+        left, right, split_left, split_right, small, small_more = tick(
+            ahead(rounded(whole[2], left)),
+            behind(rounded(whole[6], right)),
+            ahead(rounded(split[3], pair[3], split_left)),
+            behind(rounded(split[5], pair[5])),
+            small,
+            hop(small, 1, 0, n_dp, n_seq),
+        )
+        small = small + small_more
+        left, right, split_left, split_right, small, small_more = tick(
+            ahead(rounded(whole[1], left)),
+            behind(rounded(whole[7], right)),
+            ahead(rounded(split[2], pair[2], split_left)),
+            behind(rounded(split[6], pair[6], split_right)),
+            small,
+            hop(small, 2, 0, n_dp, n_seq),
+        )
+        small = small + small_more
+        own = rounded(whole[0], left, right)
+        own, other_chip, split_left, split_right, small, small_more = tick(
+            own,
+            trade(own),
+            ahead(rounded(split[1], pair[1], split_left)),
+            behind(rounded(split[7], pair[7], split_right)),
+            small,
+            hop(small, 4, 0, n_dp, n_seq),
+        )
+        small = lax.dynamic_index_in_dim(small + small_more, group, 0, keepdims=False)
+        split_own, own, other_chip, small = tick(
+            rounded(split[0], pair[0], split_left, split_right), own, other_chip, small
+        )
+        own = rounded(own, other_chip)
+        squares = jnp.sum(jnp.square(own.astype(f32))) + 0.5 * jnp.sum(small[:rows] ** 2)
+        own, split_own, pair_own, other, squares = tick(own, split_own, trade(split_own), across(own), squares)
+        split_own = join_halves(
+            jnp.where(side == 0, split_own, pair_own), jnp.where(side == 0, pair_own, split_own)
+        )
+        split_other = across(split_own)
+        squares = jnp.full((1, LANES), squares + jnp.sum(jnp.square(split_own.astype(f32))))
+        for hops in (((0, 0), (0, 1), (1, 0), (1, 1)), ((0, 0), (2, 0), (4, 0), (6, 0))):
+            squares = tree_sum([squares] + [hop(squares, *ks, n_dp, n_seq) for ks in hops[1:]])
     else:
-        canonical = jnp.concatenate([keep, send], 1).transpose(1, 0, 2, 3)
+        def by_place(groups, values):
+            spread = dict(zip((r for places in groups for r in places), jnp.concatenate(values)))
+            return jnp.stack([spread[r] for r in range(BLOCKS)])
+
+        def three(whole, split):
+            split = by_place(SPLIT_PLACES, split)
+            return jnp.concatenate([by_place(PLACES, whole), join_halves(split[:, 0], split[:, 1])[:, None]], 1)
+
+        canonical = jnp.concatenate([three(keeps, split_keeps), three(sends, split_sends)], 1).transpose(1, 0, 2, 3)
 
         def join(row, end, blocks):
             part = canonical[:, :, row:end].astype(f32).reshape(CUTS, BLOCKS, blocks, -1, LANES)
@@ -653,25 +874,21 @@
         grads = lax.psum(grads, "seq")
         vector_grad = grads[4]
         squares = lax.psum(sum(jnp.sum(grad * grad) for grad in grads), "dp")
-        loss_sum, count = lax.psum((loss_part, count_part), ("dp", "seq"))
-
-    norm = jnp.sqrt(squares) / count
-    factor = clip_limit / jnp.maximum(norm, clip_limit) / count
+        loss_sum, count = lax.psum((vgrad[rows, 0], vgrad[rows + 1, 0]), ("dp", "seq"))
+
     if ringed:
-        new = adam_all(
-            core.reshape(1), factor.reshape(1), own, other, masters[:4], moments[:4], variances[:4]
-        )
+        shared_grads = (own, split_own, other, split_other)
+        loss, norm, *new = adam_all(core.reshape(1), squares, small, shared_grads, masters, moments, variances)
     else:
+        loss, norm = loss_sum / count, jnp.sqrt(squares) / count
+        factor = clip_limit / jnp.maximum(norm, clip_limit) / count
+        rates = ((matrix_rate, weight_decay),) * 4 + ((vector_rate, 0.0),)
         updated = [
-            adam(master, moment, variance, grad * factor, matrix_rate, weight_decay)
-            for master, moment, variance, grad in zip(masters[:4], moments, variances, grads)
+            adam(master, moment, variance, grad * factor, *rate)
+            for master, moment, variance, grad, rate in zip(masters, moments, variances, grads, rates)
         ]
         new = tuple(zip(*updated))
-    last = adam(vectors, moments[4], variances[4], vector_grad * factor, vector_rate, 0.0)
-    outs = []
-    for kind in range(4):
-        outs.extend((new[0][kind], new[1][kind], new[2][kind]))
-    return (loss_sum / count, norm, *outs, *last)
+    return (loss, norm, *(new[k][kind] for kind in range(5) for k in range(3)))
 
 
 def solution(mesh):

time: 344 us -> 279 us (0.81)
  waiting for transfers between devices: 176 us -> 141 us
  local copies, waits for them, and re-layouts: 20.8 us -> 6.59 us
  starting transfers between devices: 61.3 us -> 47.2 us
  between operations: 8.13 us -> 3.42 us
  Pallas kernels: 61.3 us -> 65.7 us
    ppermute x8 -> x12, waiting for transfers between devices: 84.3 us -> 14.9 us  [ahead(): return lax.ppermute(value, 'dp', forward)]
    ppermute x21 -> x9, starting transfers between devices: 36.3 us -> 8.83 us  [hop(): return lax.ppermute(value, ('dp', 'seq'), pairs)]
    ppermute x16 -> x30, waiting for transfers between devices: 39.4 us -> 63.9 us  [seq_flip(): return lax.ppermute(value, 'seq', [(i, i ^ k) for i in range(n_seq)])]
    ppermute x21 -> x9, waiting for transfers between devices: 17.9 us -> 42 us  [hop(): return lax.ppermute(value, ('dp', 'seq'), pairs)]
    ppermute x8 -> x11, waiting for transfers between devices: 34.1 us -> 20.2 us  [behind(): return lax.ppermute(value, 'dp', backward)]
    ppermute x8 -> x12, starting transfers between devices: 7.54 us -> 16.2 us  [ahead(): return lax.ppermute(value, 'dp', forward)]
    ppermute x16 -> x30, starting transfers between devices: 7.18 us -> 12.5 us  [seq_flip(): return lax.ppermute(value, 'seq', [(i, i ^ k) for i in range(n_seq)])]
    pallas_call x3 -> x4, Pallas kernels: 61.3 us -> 65.7 us  [the longest x1 47.9 us: run_step(): pl.pallas_call(partial(step_kernel, pieces, vec_pieces, (len(parcels), le...]
  transfers between devices with their start and end apart: 53 -> 62, of which waited for: 22 -> 29; matrix products, arithmetic and copies ran while one was open for 8% -> 5% of each run, Pallas kernels for 0% -> 1%
where the time goes in v2:
time: 279 us; the launch traced here: 278 us
  waiting for transfers between devices  141 us (51%)
  Pallas kernels  65.7 us (24%)
  starting transfers between devices  47.2 us (17%)
  other arithmetic  14.4 us (5%)
  local copies, waits for them, and re-layouts  6.59 us (2%)
  between operations  3.42 us (1%)
    ppermute x30, waiting for transfers between devices, seq_flip(): return lax.ppermute(value, 'seq', [(i, i ^ k) for i in range(n_seq)])  63.9 us
    pallas_call x1, Pallas kernels, run_step(): pl.pallas_call(partial(step_kernel, pieces, vec_pieces, (len(parcels), le...  47.9 us
    ppermute x9, waiting for transfers between devices, hop(): return lax.ppermute(value, ('dp', 'seq'), pairs)  42 us
    ppermute x11, waiting for transfers between devices, behind(): return lax.ppermute(value, 'dp', backward)  20.2 us
    ppermute x12, starting transfers between devices, ahead(): return lax.ppermute(value, 'dp', forward)  16.2 us
    ppermute x12, waiting for transfers between devices, ahead(): return lax.ppermute(value, 'dp', forward)  14.9 us
    ppermute x30, starting transfers between devices, seq_flip(): return lax.ppermute(value, 'seq', [(i, i ^ k) for i in range(n_seq)])  12.5 us
    pallas_call x1, Pallas kernels, adam_all(): pl.pallas_call(adam_kernel, out_shape=[jax.ShapeDtypeStruct((1, 1), f32)]...  11.6 us
  transfers between devices with their start and end apart: 62, of which 29 were waited for; matrix products, arithmetic and copies ran while one was open for 5% of the time, Pallas kernels for 1%

profile of v2, /device:TPU:0, one launch (start us, length us, event | category | flops | bytes accessed | tf_op | source)
XLA Modules:
  0.0 278.4 jit_solution(6053313873937666498)
XLA Ops:
  1.4 4.2 %pack.1 = (bf16[6,1344,128]{2,1,0:T(8,128)(2,1)}, bf16[2,1376,128]{2,1,0:T(8,128)(2,1)}, bf16[2,1376,128]{2,1,0:T(8,128)(2,1)}) custom-call(s32[4]{0:T(128)} %pad_add_fusion.2.chosen, f32[3,96,768]{2,1,0:T(8,128)} %refs_0_.1, f32[96,2304]{1,0:T(8,128)} %refs_1_.1, f32[96,3072]{1,0:T(8,128)} %refs_2_.1, f32[384,768]{1,0:T(8,128)} %refs_3_.1, f32[20,96]{1,0:T(8,128)} %refs_4_.1), custom_call_target="tpu_custom_call" | custom-call | tf_op jit(solution)/shard_map/pack/pallas_call | solution.py:463
  5.5 3.0 %collective-permute-start.1 = (bf16[2,1376,128]{2,1,0:T(8,128)(2,1)}, bf16[2,1376,128]{2,1,0:T(8,128)(2,1)S(1)}, u32[]{:S(2)}, u32[]{:S(2)}) collective-permute-start(bf16[2,1376,128]{2,1,0:T(8,128)(2,1)} %get-tuple-element.129), channel_id=1, source_target_pairs={{8,0},{16,8},{24,16},{28,24},{20,28},{12,20},{4,12},{0,4},{9,1},{1... | collective-permute-start | bytes 2113544 | tf_op jit(solution)/shard_map/ppermute | solution.py:651
  9.1 2.1 parcels.1
  11.2 1.9 collective-permute-start.3
  13.3 6.5 %collective-permute-done.3.refs_4_ = bf16[144,768]{1,0:T(8,128)(2,1)S(1)} collective-permute-done((bf16[144,768]{1,0:T(8,128)(2,1)}, bf16[144,768]{1,0:T(8,128)(2,1)S(1)}, u32[]{:S(2)}, u32[]{:S(2)}) %collective-permute-start.3) | collective-permute-done | bytes 221216 | tf_op jit(solution)/shard_map/ppermute | solution.py:600
  19.7 4.2 %collective-permute-done.4.refs_5_ = bf16[144,768]{1,0:T(8,128)(2,1)S(1)} collective-permute-done((bf16[144,768]{1,0:T(8,128)(2,1)}, bf16[144,768]{1,0:T(8,128)(2,1)S(1)}, u32[]{:S(2)}, u32[]{:S(2)}) %collective-permute-start.4) | collective-permute-done | bytes 221216 | tf_op jit(solution)/shard_map/ppermute | solution.py:600
  24.6 1.4 collective-permute-done.refs_8_
  26.1 1.6 collective-permute-start.7
  28.4 1.5 collective-permute-start.6
  30.0 3.8 %fusion.8.refs_1_ = f32[256,768]{1,0:T(8,128)} fusion(f32[768]{0:T(1024)S(1)} %fusion.30, f32[256]{0:T(256)S(1)} %iota_convert_fusion, pred[768]{0:T(1024)(128)(4,1)S(1)} %fusion.25), kind=kLoop, calls=%fused_computation.26 | loop fusion | flops 393216 | bytes 791296 | tf_op jit(solution)/shard_map/jit(_where)/select_n | solution.py:596
  33.8 9.1 %collective-permute-done.7.refs_14_ = bf16[2,1376,128]{2,1,0:T(8,128)(2,1)S(1)} collective-permute-done((bf16[2,1376,128]{2,1,0:T(8,128)(2,1)S(1)}, bf16[2,1376,128]{2,1,0:T(8,128)(2,1)S(1)}, u32[]{:S(2)}, u32[]{:S(2)}) %collective-permute-start.7) | collective-permute-done | bytes 704544 | tf_op jit(solution)/shard_map/ppermute | solution.py:600
  42.9 3.0 %collective-permute-done.5.refs_12_ = bf16[2,1376,128]{2,1,0:T(8,128)(2,1)S(1)} collective-permute-done((bf16[2,1376,128]{2,1,0:T(8,128)(2,1)S(1)}, bf16[2,1376,128]{2,1,0:T(8,128)(2,1)S(1)}, u32[]{:S(2)}, u32[]{:S(2)}) %collective-permute-start.5) | collective-permute-done | bytes 704544 | tf_op jit(solution)/shard_map/ppermute | solution.py:648
  46.8 1.4 collective-permute-start.10
  50.0 17.2 %collective-permute-done.12.refs_20_ = bf16[2,1376,128]{2,1,0:T(8,128)(2,1)} collective-permute-done((bf16[2,1376,128]{2,1,0:T(8,128)(2,1)S(1)}, bf16[2,1376,128]{2,1,0:T(8,128)(2,1)}, u32[]{:S(2)}, u32[]{:S(2)}) %collective-permute-start.12) | collective-permute-done | bytes 704544 | tf_op jit(solution)/shard_map/ppermute | solution.py:600
  68.8 1.3 collective-permute-start.16
  71.0 1.1 collective-permute-start.17
  74.9 6.8 %collective-permute-done.17.refs_26_ = bf16[1,1376,128]{2,1,0:T(8,128)(2,1)S(1)} collective-permute-done((bf16[1,1376,128]{2,1,0:T(8,128)(2,1)S(1)}, bf16[1,1376,128]{2,1,0:T(8,128)(2,1)S(1)}, u32[]{:S(2)}, u32[]{:S(2)}) %collective-permute-start.17) | collective-permute-done | bytes 352288 | tf_op jit(solution)/shard_map/ppermute | solution.py:651
  81.7 6.3 %collective-permute-done.18.refs_24_ = bf16[2,1376,128]{2,1,0:T(8,128)(2,1)} collective-permute-done((bf16[2,1376,128]{2,1,0:T(8,128)(2,1)S(1)}, bf16[2,1376,128]{2,1,0:T(8,128)(2,1)}, u32[]{:S(2)}, u32[]{:S(2)}) %collective-permute-start.18) | collective-permute-done | bytes 704544 | tf_op jit(solution)/shard_map/ppermute | solution.py:600
  88.6 3.3 %collective-permute-done.23.refs_28_ = bf16[1,1376,128]{2,1,0:T(8,128)(2,1)S(1)} collective-permute-done((bf16[1,1376,128]{2,1,0:T(8,128)(2,1)S(1)}, bf16[1,1376,128]{2,1,0:T(8,128)(2,1)S(1)}, u32[]{:S(2)}, u32[]{:S(2)}) %collective-permute-start.23) | collective-permute-done | bytes 352288 | tf_op jit(solution)/shard_map/ppermute | solution.py:600
  93.1 47.9 %step.1 = (bf16[1,2,1344,128]{3,2,1,0:T(8,128)(2,1)}, bf16[1,2,1344,128]{3,2,1,0:T(8,128)(2,1)}, bf16[2,2,1344,128]{3,2,1,0:T(8,128)(2,1)}, bf16[2,2,1344,128]{3...) custom-call(s32[56]{0:T(128)} %concatenate.20.refs_0_, ...), custom_call_target="tpu_custom_call" | custom-call | tf_op jit(solution)/shard_map/step/pallas_call | solution.py:394
  143.5 1.6 add_convert_fusion.5
  145.1 1.7 collective-permute-done.26
  149.2 1.6 collective-permute-start.31
  151.1 4.6 %collective-permute-done.33 = bf16[5,2,672,128]{3,2,1,0:T(8,128)(2,1)S(1)} collective-permute-done((bf16[5,2,672,128]{3,2,1,0:T(8,128)(2,1)}, bf16[5,2,672,128]{3,2,1,0:T(8,128)(2,1)S(1)}, u32[]{:S(2)}, u32[]{:S(2)}) %collective-permute-start.33) | collective-permute-done | bytes 1720352 | tf_op jit(solution)/shard_map/ppermute | solution.py:600
  155.7 1.6 collective-permute-start.29
  158.4 7.5 %collective-permute-done.29 = bf16[1,1344,128]{2,1,0:T(8,128)(2,1)S(1)} collective-permute-done((bf16[1,1344,128]{2,1,0:T(8,128)(2,1)S(1)}, bf16[1,1344,128]{2,1,0:T(8,128)(2,1)S(1)}, u32[]{:S(2)}, u32[]{:S(2)}) %collective-permute-start.29) | collective-permute-done | bytes 344096 | tf_op jit(solution)/shard_map/ppermute | solution.py:648
  165.9 1.6 collective-permute-start.36
  169.0 1.6 collective-permute-start.34
  171.6 1.4 collective-permute-done.36
  173.0 11.7 %collective-permute-done.35 = bf16[2,1344,128]{2,1,0:T(8,128)(2,1)S(1)} collective-permute-done((bf16[2,1344,128]{2,1,0:T(8,128)(2,1)S(1)}, bf16[2,1344,128]{2,1,0:T(8,128)(2,1)S(1)}, u32[]{:S(2)}, u32[]{:S(2)}) %collective-permute-start.35) | collective-permute-done | bytes 688160 | tf_op jit(solution)/shard_map/ppermute | solution.py:651
  184.6 1.6 collective-permute-done.34
  186.3 1.4 collective-permute-done.37
  188.6 1.6 collective-permute-start.39
  190.8 1.6 collective-permute-start.41
  192.9 16.7 %collective-permute-done.43 = f32[8,24,96]{2,1,0:T(8,128)S(1)} collective-permute-done((f32[8,24,96]{2,1,0:T(8,128)S(1)}, f32[8,24,96]{2,1,0:T(8,128)S(1)}, u32[]{:S(2)}, u32[]{:S(2)}) %collective-permute-start.43) | collective-permute-done | bytes 73760 | tf_op jit(solution)/shard_map/ppermute | solution.py:605
  210.3 1.7 collective-permute-start.44
  212.5 1.7 collective-permute-start.46
  214.3 16.1 %collective-permute-done.48 = f32[8,24,96]{2,1,0:T(8,128)S(1)} collective-permute-done((f32[8,24,96]{2,1,0:T(8,128)S(1)}, f32[8,24,96]{2,1,0:T(8,128)S(1)}, u32[]{:S(2)}, u32[]{:S(2)}) %collective-permute-start.48) | collective-permute-done | bytes 73760 | tf_op jit(solution)/shard_map/ppermute | solution.py:605
  232.0 1.4 collective-permute-start.50
  233.4 1.6 collective-permute-start.52
  235.0 4.0 %collective-permute-done.52 = f32[8,24,96]{2,1,0:T(8,128)S(1)} collective-permute-done((f32[8,24,96]{2,1,0:T(8,128)S(1)}, f32[8,24,96]{2,1,0:T(8,128)S(1)}, u32[]{:S(2)}, u32[]{:S(2)}) %collective-permute-start.52) | collective-permute-done | bytes 73760 | tf_op jit(solution)/shard_map/ppermute | solution.py:605
  239.0 5.0 %collective-permute-done.49 = bf16[2,1344,128]{2,1,0:T(8,128)(2,1)S(1)} collective-permute-done((bf16[2,1344,128]{2,1,0:T(8,128)(2,1)S(1)}, bf16[2,1344,128]{2,1,0:T(8,128)(2,1)S(1)}, u32[]{:S(2)}, u32[]{:S(2)}) %collective-permute-start.49) | collective-permute-done | bytes 688160 | tf_op jit(solution)/shard_map/ppermute | solution.py:600
  247.7 4.2 %collective-permute-done.53 = bf16[672,128]{1,0:T(8,128)(2,1)S(1)} collective-permute-done((bf16[672,128]{1,0:T(8,128)(2,1)S(1)}, bf16[672,128]{1,0:T(8,128)(2,1)S(1)}, u32[]{:S(2)}, u32[]{:S(2)}) %collective-permute-start.53) | collective-permute-done | bytes 172064 | tf_op jit(solution)/shard_map/ppermute | solution.py:600
  254.5 1.1 collective-permute-start.55
  255.7 1.4 collective-permute-done.56
  257.4 3.4 %collective-permute-start.60 = (f32[1,128]{1,0:T(1,128)S(1)}, f32[1,128]{1,0:T(1,128)S(1)}, u32[]{:S(2)}, u32[]{:S(2)}) collective-permute-start(f32[1,128]{1,0:T(1,128)S(1)} %add_add_fusion.1), channel_id=1, source_target_pairs={{0,24},{1,25},{2,26},{3,27},{4,28},{5,29},{6,30},{7,31},{8,16},{9,... | collective-permute-start | bytes 1544 | tf_op jit(solution)/shard_map/ppermute | solution.py:605
  262.9 2.5 collective-permute-done.59
  266.6 11.6 %adam.1 = (f32[1,1]{1,0:T(1,128)}, f32[1,1]{1,0:T(1,128)}, f32[3,96,768]{2,1,0:T(8,128)}, f32[96,2304]{1,0:T(8,128)}, f32[96,3072]{1,0:T(8,128)}, /*index=5*/f32...) custom-call(s32[1]{0:T(128)} %bitcast.core, ...), custom_call_target="tpu_custom_call" | custom-call | tf_op jit(solution)/shard_map/adam/pallas_call | solution.py:579
  (210 shorter events, 33.9 us)
Async XLA Ops:
  5.5 19.0 %collective-permute-start.1 = (bf16[2,1376,128]{2,1,0:T(8,128)(2,1)}, bf16[2,1376,128]{2,1,0:T(8,128)(2,1)S(1)}, u32[]{:S(2)}, u32[]{:S(2)}) collective-permute-start(bf16[2,1376,128]{2,1,0:T(8,128)(2,1)} %get-tuple-element.129), channel_id=1, source_target_pairs={{8,0},{16,8},{24,16},{28,24},{20,28},{12,20},{4,12},{0,4},{9,1},{1... | collective-permute-start | bytes 2113544 | tf_op jit(solution)/shard_map/ppermute | solution.py:651
  8.5 17.5 %collective-permute-start = (bf16[2,1376,128]{2,1,0:T(8,128)(2,1)}, bf16[2,1376,128]{2,1,0:T(8,128)(2,1)S(1)}, u32[]{:S(2)}, u32[]{:S(2)}) collective-permute-start(bf16[2,1376,128]{2,1,0:T(8,128)(2,1)} %get-tuple-element.128.refs_7_), channel_id=1, source_target_pairs={{0,8},{8,16},{16,24},{24,28},{28,20},{20,12},{12,4},{4,0},{1,9},{9... | collective-permute-start | bytes 2113544 | tf_op jit(solution)/shard_map/ppermute | solution.py:648
  11.2 8.5 %collective-permute-start.3 = (bf16[144,768]{1,0:T(8,128)(2,1)}, bf16[144,768]{1,0:T(8,128)(2,1)S(1)}, u32[]{:S(2)}, u32[]{:S(2)}) collective-permute-start(bf16[144,768]{1,0:T(8,128)(2,1)} %get-tuple-element.131), channel_id=1, source_target_pairs={{0,2},{1,3},{2,0},{3,1},{4,6},{5,7},{6,4},{7,5},{8,10},{9,11},{10,... | collective-permute-start | bytes 663560 | tf_op jit(solution)/shard_map/ppermute | solution.py:600
  13.2 10.8 %collective-permute-start.4 = (bf16[144,768]{1,0:T(8,128)(2,1)}, bf16[144,768]{1,0:T(8,128)(2,1)S(1)}, u32[]{:S(2)}, u32[]{:S(2)}) collective-permute-start(bf16[144,768]{1,0:T(8,128)(2,1)} %get-tuple-element.132), channel_id=1, source_target_pairs={{0,3},{1,2},{2,1},{3,0},{4,7},{5,6},{6,5},{7,4},{8,11},{9,10},{10,... | collective-permute-start | bytes 663560 | tf_op jit(solution)/shard_map/ppermute | solution.py:600
  26.1 16.8 %collective-permute-start.7 = (bf16[2,1376,128]{2,1,0:T(8,128)(2,1)S(1)}, bf16[2,1376,128]{2,1,0:T(8,128)(2,1)S(1)}, u32[]{:S(2)}, u32[]{:S(2)}) collective-permute-start(bf16[2,1376,128]{2,1,0:T(8,128)(2,1)S(1)} %pad_maximum_fusion), channel_id=1, source_target_pairs={{0,2},{1,3},{2,0},{3,1},{4,6},{5,7},{6,4},{7,5},{8,10},{9,11},{10,... | collective-permute-start | bytes 2113544 | tf_op jit(solution)/shard_map/ppermute | solution.py:600
  27.7 15.2 %collective-permute-start.8 = (bf16[2,1376,128]{2,1,0:T(8,128)(2,1)S(1)}, bf16[2,1376,128]{2,1,0:T(8,128)(2,1)S(1)}, u32[]{:S(2)}, u32[]{:S(2)}) collective-permute-start(bf16[2,1376,128]{2,1,0:T(8,128)(2,1)S(1)} %collective-permute-done.refs_8_), channel_id=1, source_target_pairs={{0,1},{1,0},{2,3},{3,2},{4,5},{5,4},{6,7},{7,6},{8,9},{9,8},{10,11... | collective-permute-start | bytes 2113544 | tf_op jit(solution)/shard_map/ppermute | solution.py:600
  27.7 18.2 %collective-permute-start.5 = (bf16[2,1376,128]{2,1,0:T(8,128)(2,1)S(1)}, bf16[2,1376,128]{2,1,0:T(8,128)(2,1)S(1)}, u32[]{:S(2)}, u32[]{:S(2)}) collective-permute-start(bf16[2,1376,128]{2,1,0:T(8,128)(2,1)S(1)} %collective-permute-done.refs_8_), channel_id=1, source_target_pairs={{0,8},{8,16},{16,24},{24,28},{28,20},{20,12},{12,4},{4,0},{1,9},{9... | collective-permute-start | bytes 2113544 | tf_op jit(solution)/shard_map/ppermute | solution.py:648
  28.3 17.6 %collective-permute-start.9 = (bf16[2,1376,128]{2,1,0:T(8,128)(2,1)S(1)}, bf16[2,1376,128]{2,1,0:T(8,128)(2,1)S(1)}, u32[]{:S(2)}, u32[]{:S(2)}) collective-permute-start(bf16[2,1376,128]{2,1,0:T(8,128)(2,1)S(1)} %collective-permute-done.1.refs_9_), channel_id=1, source_target_pairs={{0,1},{1,0},{2,3},{3,2},{4,5},{5,4},{6,7},{7,6},{8,9},{9,8},{10,11... | collective-permute-start | bytes 2113544 | tf_op jit(solution)/shard_map/ppermute | solution.py:600
  28.4 18.0 %collective-permute-start.6 = (bf16[2,1376,128]{2,1,0:T(8,128)(2,1)S(1)}, bf16[2,1376,128]{2,1,0:T(8,128)(2,1)S(1)}, u32[]{:S(2)}, u32[]{:S(2)}) collective-permute-start(bf16[2,1376,128]{2,1,0:T(8,128)(2,1)S(1)} %collective-permute-done.1.refs_9_), channel_id=1, source_target_pairs={{8,0},{16,8},{24,16},{28,24},{20,28},{12,20},{4,12},{0,4},{9,1},{1... | collective-permute-start | bytes 2113544 | tf_op jit(solution)/shard_map/ppermute | solution.py:651
  46.8 20.4 %collective-permute-start.10 = (bf16[2,1376,128]{2,1,0:T(8,128)(2,1)S(1)}, bf16[2,1376,128]{2,1,0:T(8,128)(2,1)S(1)}, u32[]{:S(2)}, u32[]{:S(2)}) collective-permute-start(bf16[2,1376,128]{2,1,0:T(8,128)(2,1)S(1)} %collective-permute-done.5.refs_12_), channel_id=1, source_target_pairs={{0,8},{8,16},{16,24},{24,28},{28,20},{20,12},{12,4},{4,0},{1,9},{9... | collective-permute-start | bytes 2113544 | tf_op jit(solution)/shard_map/ppermute | solution.py:648
  48.2 19.0 %collective-permute-start.14 = (bf16[2,1376,128]{2,1,0:T(8,128)(2,1)S(1)}, bf16[2,1376,128]{2,1,0:T(8,128)(2,1)S(1)}, u32[]{:S(2)}, u32[]{:S(2)}) collective-permute-start(bf16[2,1376,128]{2,1,0:T(8,128)(2,1)S(1)} %collective-permute-done.6.refs_13_), channel_id=1, source_target_pairs={{0,1},{1,0},{2,3},{3,2},{4,5},{5,4},{6,7},{7,6},{8,9},{9,8},{10,11... | collective-permute-start | bytes 2113544 | tf_op jit(solution)/shard_map/ppermute | solution.py:600
  48.5 18.7 %collective-permute-start.11 = (bf16[2,1376,128]{2,1,0:T(8,128)(2,1)S(1)}, bf16[2,1376,128]{2,1,0:T(8,128)(2,1)S(1)}, u32[]{:S(2)}, u32[]{:S(2)}) collective-permute-start(bf16[2,1376,128]{2,1,0:T(8,128)(2,1)S(1)} %collective-permute-done.6.refs_13_), channel_id=1, source_target_pairs={{8,0},{16,8},{24,16},{28,24},{20,28},{12,20},{4,12},{0,4},{9,1},{1... | collective-permute-start | bytes 2113544 | tf_op jit(solution)/shard_map/ppermute | solution.py:651
  49.3 17.9 %collective-permute-start.12 = (bf16[2,1376,128]{2,1,0:T(8,128)(2,1)S(1)}, bf16[2,1376,128]{2,1,0:T(8,128)(2,1)}, u32[]{:S(2)}, u32[]{:S(2)}) collective-permute-start(bf16[2,1376,128]{2,1,0:T(8,128)(2,1)S(1)} %pad_maximum_fusion.1), channel_id=1, source_target_pairs={{0,2},{1,3},{2,0},{3,1},{4,6},{5,7},{6,4},{7,5},{8,10},{9,11},{10,... | collective-permute-start | bytes 2113544 | tf_op jit(solution)/shard_map/ppermute | solution.py:600
  49.9 17.3 %collective-permute-start.15 = (bf16[2,1376,128]{2,1,0:T(8,128)(2,1)S(1)}, bf16[2,1376,128]{2,1,0:T(8,128)(2,1)S(1)}, u32[]{:S(2)}, u32[]{:S(2)}) collective-permute-start(bf16[2,1376,128]{2,1,0:T(8,128)(2,1)S(1)} %collective-permute-done.7.refs_14_), channel_id=1, source_target_pairs={{0,1},{1,0},{2,3},{3,2},{4,5},{5,4},{6,7},{7,6},{8,9},{9,8},{10,11... | collective-permute-start | bytes 2113544 | tf_op jit(solution)/shard_map/ppermute | solution.py:600
  68.2 19.7 %collective-permute-start.20 = (bf16[2,1376,128]{2,1,0:T(8,128)(2,1)S(1)}, bf16[2,1376,128]{2,1,0:T(8,128)(2,1)}, u32[]{:S(2)}, u32[]{:S(2)}) collective-permute-start(bf16[2,1376,128]{2,1,0:T(8,128)(2,1)S(1)} %collective-permute-done.11.refs_18_), channel_id=1, source_target_pairs={{0,1},{1,0},{2,3},{3,2},{4,5},{5,4},{6,7},{7,6},{8,9},{9,8},{10,11... | collective-permute-start | bytes 2113544 | tf_op jit(solution)/shard_map/ppermute | solution.py:600
  68.8 19.1 %collective-permute-start.16 = (bf16[2,1376,128]{2,1,0:T(8,128)(2,1)S(1)}, bf16[2,1376,128]{2,1,0:T(8,128)(2,1)}, u32[]{:S(2)}, u32[]{:S(2)}) collective-permute-start(bf16[2,1376,128]{2,1,0:T(8,128)(2,1)S(1)} %collective-permute-done.10.refs_17_), channel_id=1, source_target_pairs={{0,8},{8,16},{16,24},{24,28},{28,20},{20,12},{12,4},{4,0},{1,9},{9... | collective-permute-start | bytes 2113544 | tf_op jit(solution)/shard_map/ppermute | solution.py:648
  70.3 17.6 %collective-permute-start.18 = (bf16[2,1376,128]{2,1,0:T(8,128)(2,1)S(1)}, bf16[2,1376,128]{2,1,0:T(8,128)(2,1)}, u32[]{:S(2)}, u32[]{:S(2)}) collective-permute-start(bf16[2,1376,128]{2,1,0:T(8,128)(2,1)S(1)} %pad_maximum_fusion.2), channel_id=1, source_target_pairs={{0,2},{1,3},{2,0},{3,1},{4,6},{5,7},{6,4},{7,5},{8,10},{9,11},{10,... | collective-permute-start | bytes 2113544 | tf_op jit(solution)/shard_map/ppermute | solution.py:600
  71.0 16.9 %collective-permute-start.21 = (bf16[2,1376,128]{2,1,0:T(8,128)(2,1)}, bf16[2,1376,128]{2,1,0:T(8,128)(2,1)}, u32[]{:S(2)}, u32[]{:S(2)}) collective-permute-start(bf16[2,1376,128]{2,1,0:T(8,128)(2,1)} %collective-permute-done.12.refs_20_), channel_id=1, source_target_pairs={{0,1},{1,0},{2,3},{3,2},{4,5},{5,4},{6,7},{7,6},{8,9},{9,8},{10,11... | collective-permute-start | bytes 2113544 | tf_op jit(solution)/shard_map/ppermute | solution.py:600
  71.0 10.6 %collective-permute-start.17 = (bf16[1,1376,128]{2,1,0:T(8,128)(2,1)S(1)}, bf16[1,1376,128]{2,1,0:T(8,128)(2,1)S(1)}, u32[]{:S(2)}, u32[]{:S(2)}) collective-permute-start(bf16[1,1376,128]{2,1,0:T(8,128)(2,1)S(1)} %slice.81), channel_id=1, source_target_pairs={{8,0},{16,8},{24,16},{28,24},{20,28},{12,20},{4,12},{0,4},{9,1},{1... | collective-permute-start | bytes 1056776 | tf_op jit(solution)/shard_map/ppermute | solution.py:651
  141.2 6.0 %collective-permute-start.27 = (bf16[2,2,1344,128]{3,2,1,0:T(8,128)(2,1)}, bf16[2,2,1344,128]{3,2,1,0:T(8,128)(2,1)S(1)}, u32[]{:S(2)}, u32[]{:S(2)}) collective-permute-start(bf16[2,2,1344,128]{3,2,1,0:T(8,128)(2,1)} %get-tuple-element.168), channel_id=1, source_target_pairs={{0,1},{1,0},{2,3},{3,2},{4,5},{5,4},{6,7},{7,6},{8,9},{9,8},{10,11... | collective-permute-start | bytes 4128776 | tf_op jit(solution)/shard_map/ppermute | solution.py:600
  147.1 18.7 %collective-permute-start.32 = (bf16[5,2,1344,128]{3,2,1,0:T(8,128)(2,1)S(1)}, bf16[5,2,1344,128]{3,2,1,0:T(8,128)(2,1)S(1)}, u32[]{:S(2)}, u32[]{:S(2)}) collective-permute-start(bf16[5,2,1344,128]{3,2,1,0:T(8,128)(2,1)S(1)} %copy-done.31), channel_id=1, source_target_pairs={{0,1},{1,0},{2,3},{3,2},{4,5},{5,4},{6,7},{7,6},{8,9},{9,8},{10,11... | collective-permute-start | bytes 10321928 | tf_op jit(solution)/shard_map/ppermute | solution.py:600
  147.3 8.4 %collective-permute-start.33 = (bf16[5,2,672,128]{3,2,1,0:T(8,128)(2,1)}, bf16[5,2,672,128]{3,2,1,0:T(8,128)(2,1)S(1)}, u32[]{:S(2)}, u32[]{:S(2)}) collective-permute-start(bf16[5,2,672,128]{3,2,1,0:T(8,128)(2,1)} %get-tuple-element.178), channel_id=1, source_target_pairs={{0,1},{1,0},{2,3},{3,2},{4,5},{5,4},{6,7},{7,6},{8,9},{9,8},{10,11... | collective-permute-start | bytes 5160968 | tf_op jit(solution)/shard_map/ppermute | solution.py:600
  147.7 23.8 %collective-permute-start.38 = (f32[8,24,96]{2,1,0:T(8,128)S(1)}, f32[8,24,96]{2,1,0:T(8,128)S(1)}, u32[]{:S(2)}, u32[]{:S(2)}) collective-permute-start(f32[8,24,96]{2,1,0:T(8,128)S(1)} %add.251), channel_id=1, source_target_pairs={{0,2},{1,3},{2,0},{3,1},{4,6},{5,7},{6,4},{7,5},{8,10},{9,11},{10,... | collective-permute-start | bytes 221192 | tf_op jit(solution)/shard_map/ppermute | solution.py:600
  148.5 9.9 %collective-permute-start.30 = (bf16[1,1344,128]{2,1,0:T(8,128)(2,1)S(1)}, bf16[1,1344,128]{2,1,0:T(8,128)(2,1)S(1)}, u32[]{:S(2)}, u32[]{:S(2)}) collective-permute-start(bf16[1,1344,128]{2,1,0:T(8,128)(2,1)S(1)} %get-tuple-element.257), channel_id=1, source_target_pairs={{8,0},{16,8},{24,16},{28,24},{20,28},{12,20},{4,12},{0,4},{9,1},{1... | collective-permute-start | bytes 1032200 | tf_op jit(solution)/shard_map/ppermute | solution.py:651
  149.2 16.7 %collective-permute-start.31 = (bf16[3,672,128]{2,1,0:T(8,128)(2,1)S(1)}, bf16[3,672,128]{2,1,0:T(8,128)(2,1)S(1)}, u32[]{:S(2)}, u32[]{:S(2)}) collective-permute-start(bf16[3,672,128]{2,1,0:T(8,128)(2,1)S(1)} %slice_bitcast_fusion.1), channel_id=1, source_target_pairs={{0,2},{1,3},{2,0},{3,1},{4,6},{5,7},{6,4},{7,5},{8,10},{9,11},{10,... | collective-permute-start | bytes 1548296 | tf_op jit(solution)/shard_map/ppermute | solution.py:600
  155.7 10.1 %collective-permute-start.29 = (bf16[1,1344,128]{2,1,0:T(8,128)(2,1)S(1)}, bf16[1,1344,128]{2,1,0:T(8,128)(2,1)S(1)}, u32[]{:S(2)}, u32[]{:S(2)}) collective-permute-start(bf16[1,1344,128]{2,1,0:T(8,128)(2,1)S(1)} %get-tuple-element.258), channel_id=1, source_target_pairs={{0,8},{8,16},{16,24},{24,28},{28,20},{20,12},{12,4},{4,0},{1,9},{9... | collective-permute-start | bytes 1032200 | tf_op jit(solution)/shard_map/ppermute | solution.py:648
  165.9 7.1 %collective-permute-start.36 = (bf16[672,128]{1,0:T(8,128)(2,1)S(1)}, bf16[672,128]{1,0:T(8,128)(2,1)S(1)}, u32[]{:S(2)}, u32[]{:S(2)}) collective-permute-start(bf16[672,128]{1,0:T(8,128)(2,1)S(1)} %fusion.23), channel_id=1, source_target_pairs={{0,8},{8,16},{16,24},{24,28},{28,20},{20,12},{12,4},{4,0},{1,9},{9... | collective-permute-start | bytes 516104 | tf_op jit(solution)/shard_map/ppermute | solution.py:648
  167.6 20.1 %collective-permute-start.37 = (bf16[5,672,128]{2,1,0:T(8,128)(2,1)S(1)}, bf16[5,672,128]{2,1,0:T(8,128)(2,1)S(1)}, u32[]{:S(2)}, u32[]{:S(2)}) collective-permute-start(bf16[5,672,128]{2,1,0:T(8,128)(2,1)S(1)} %slice_bitcast_fusion), channel_id=1, source_target_pairs={{0,2},{1,3},{2,0},{3,1},{4,6},{5,7},{6,4},{7,5},{8,10},{9,11},{10,... | collective-permute-start | bytes 2580488 | tf_op jit(solution)/shard_map/ppermute | solution.py:600
  168.5 16.1 %collective-permute-start.35 = (bf16[2,1344,128]{2,1,0:T(8,128)(2,1)S(1)}, bf16[2,1344,128]{2,1,0:T(8,128)(2,1)S(1)}, u32[]{:S(2)}, u32[]{:S(2)}) collective-permute-start(bf16[2,1344,128]{2,1,0:T(8,128)(2,1)S(1)} %get-tuple-element.255), channel_id=1, source_target_pairs={{8,0},{16,8},{24,16},{28,24},{20,28},{12,20},{4,12},{0,4},{9,1},{1... | collective-permute-start | bytes 2064392 | tf_op jit(solution)/shard_map/ppermute | solution.py:651
  169.0 17.2 %collective-permute-start.34 = (bf16[2,1344,128]{2,1,0:T(8,128)(2,1)S(1)}, bf16[2,1344,128]{2,1,0:T(8,128)(2,1)S(1)}, u32[]{:S(2)}, u32[]{:S(2)}) collective-permute-start(bf16[2,1344,128]{2,1,0:T(8,128)(2,1)S(1)} %get-tuple-element.256), channel_id=1, source_target_pairs={{0,8},{8,16},{16,24},{24,28},{28,20},{20,12},{12,4},{4,0},{1,9},{9... | collective-permute-start | bytes 2064392 | tf_op jit(solution)/shard_map/ppermute | solution.py:648
  188.1 21.5 %collective-permute-start.40 = (bf16[2,1344,128]{2,1,0:T(8,128)(2,1)S(1)}, bf16[2,1344,128]{2,1,0:T(8,128)(2,1)S(1)}, u32[]{:S(2)}, u32[]{:S(2)}) collective-permute-start(bf16[2,1344,128]{2,1,0:T(8,128)(2,1)S(1)} %get-tuple-element.247), channel_id=1, source_target_pairs={{8,0},{16,8},{24,16},{28,24},{20,28},{12,20},{4,12},{0,4},{9,1},{1... | collective-permute-start | bytes 2064392 | tf_op jit(solution)/shard_map/ppermute | solution.py:651
  188.6 21.0 %collective-permute-start.39 = (bf16[2,1344,128]{2,1,0:T(8,128)(2,1)S(1)}, bf16[2,1344,128]{2,1,0:T(8,128)(2,1)S(1)}, u32[]{:S(2)}, u32[]{:S(2)}) collective-permute-start(bf16[2,1344,128]{2,1,0:T(8,128)(2,1)S(1)} %get-tuple-element.248), channel_id=1, source_target_pairs={{0,8},{8,16},{16,24},{24,28},{28,20},{20,12},{12,4},{4,0},{1,9},{9... | collective-permute-start | bytes 2064392 | tf_op jit(solution)/shard_map/ppermute | solution.py:648
  190.3 19.3 %collective-permute-start.42 = (bf16[672,128]{1,0:T(8,128)(2,1)S(1)}, bf16[672,128]{1,0:T(8,128)(2,1)S(1)}, u32[]{:S(2)}, u32[]{:S(2)}) collective-permute-start(bf16[672,128]{1,0:T(8,128)(2,1)S(1)} %get-tuple-element.253), channel_id=1, source_target_pairs={{8,0},{16,8},{24,16},{28,24},{20,28},{12,20},{4,12},{0,4},{9,1},{1... | collective-permute-start | bytes 516104 | tf_op jit(solution)/shard_map/ppermute | solution.py:651
  190.8 18.8 %collective-permute-start.41 = (bf16[672,128]{1,0:T(8,128)(2,1)S(1)}, bf16[672,128]{1,0:T(8,128)(2,1)S(1)}, u32[]{:S(2)}, u32[]{:S(2)}) collective-permute-start(bf16[672,128]{1,0:T(8,128)(2,1)S(1)} %get-tuple-element.254), channel_id=1, source_target_pairs={{0,8},{8,16},{16,24},{24,28},{28,20},{20,12},{12,4},{4,0},{1,9},{9... | collective-permute-start | bytes 516104 | tf_op jit(solution)/shard_map/ppermute | solution.py:648
  192.4 17.2 %collective-permute-start.43 = (f32[8,24,96]{2,1,0:T(8,128)S(1)}, f32[8,24,96]{2,1,0:T(8,128)S(1)}, u32[]{:S(2)}, u32[]{:S(2)}) collective-permute-start(f32[8,24,96]{2,1,0:T(8,128)S(1)} %add.258), channel_id=1, source_target_pairs={{0,4},{1,5},{2,6},{3,7},{4,0},{5,1},{6,2},{7,3},{8,12},{9,13},{10,... | collective-permute-start | bytes 221192 | tf_op jit(solution)/shard_map/ppermute | solution.py:605
  210.0 20.5 %collective-permute-start.45 = (bf16[2,1344,128]{2,1,0:T(8,128)(2,1)S(1)}, bf16[2,1344,128]{2,1,0:T(8,128)(2,1)S(1)}, u32[]{:S(2)}, u32[]{:S(2)}) collective-permute-start(bf16[2,1344,128]{2,1,0:T(8,128)(2,1)S(1)} %get-tuple-element.245), channel_id=1, source_target_pairs={{8,0},{16,8},{24,16},{28,24},{20,28},{12,20},{4,12},{0,4},{9,1},{1... | collective-permute-start | bytes 2064392 | tf_op jit(solution)/shard_map/ppermute | solution.py:651
  210.3 20.2 %collective-permute-start.44 = (bf16[2,1344,128]{2,1,0:T(8,128)(2,1)S(1)}, bf16[2,1344,128]{2,1,0:T(8,128)(2,1)S(1)}, u32[]{:S(2)}, u32[]{:S(2)}) collective-permute-start(bf16[2,1344,128]{2,1,0:T(8,128)(2,1)S(1)} %get-tuple-element.246), channel_id=1, source_target_pairs={{0,8},{8,16},{16,24},{24,28},{28,20},{20,12},{12,4},{4,0},{1,9},{9... | collective-permute-start | bytes 2064392 | tf_op jit(solution)/shard_map/ppermute | solution.py:648
  212.2 18.3 %collective-permute-start.47 = (bf16[672,128]{1,0:T(8,128)(2,1)S(1)}, bf16[672,128]{1,0:T(8,128)(2,1)S(1)}, u32[]{:S(2)}, u32[]{:S(2)}) collective-permute-start(bf16[672,128]{1,0:T(8,128)(2,1)S(1)} %get-tuple-element.251), channel_id=1, source_target_pairs={{8,0},{16,8},{24,16},{28,24},{20,28},{12,20},{4,12},{0,4},{9,1},{1... | collective-permute-start | bytes 516104 | tf_op jit(solution)/shard_map/ppermute | solution.py:651
  212.5 18.0 %collective-permute-start.46 = (bf16[672,128]{1,0:T(8,128)(2,1)S(1)}, bf16[672,128]{1,0:T(8,128)(2,1)S(1)}, u32[]{:S(2)}, u32[]{:S(2)}) collective-permute-start(bf16[672,128]{1,0:T(8,128)(2,1)S(1)} %get-tuple-element.252), channel_id=1, source_target_pairs={{0,8},{8,16},{16,24},{24,28},{28,20},{20,12},{12,4},{4,0},{1,9},{9... | collective-permute-start | bytes 516104 | tf_op jit(solution)/shard_map/ppermute | solution.py:648
  214.3 16.2 %collective-permute-start.48 = (f32[8,24,96]{2,1,0:T(8,128)S(1)}, f32[8,24,96]{2,1,0:T(8,128)S(1)}, u32[]{:S(2)}, u32[]{:S(2)}) collective-permute-start(f32[8,24,96]{2,1,0:T(8,128)S(1)} %add.265), channel_id=1, source_target_pairs={{0,8},{1,9},{2,10},{3,11},{4,12},{5,13},{6,14},{7,15},{8,0},{9,1},... | collective-permute-start | bytes 221192 | tf_op jit(solution)/shard_map/ppermute | solution.py:605
  230.8 13.3 %collective-permute-start.49 = (bf16[2,1344,128]{2,1,0:T(8,128)(2,1)S(1)}, bf16[2,1344,128]{2,1,0:T(8,128)(2,1)S(1)}, u32[]{:S(2)}, u32[]{:S(2)}) collective-permute-start(bf16[2,1344,128]{2,1,0:T(8,128)(2,1)S(1)} %fusion.5), channel_id=1, source_target_pairs={{0,2},{1,3},{2,0},{3,1},{4,6},{5,7},{6,4},{7,5},{8,10},{9,11},{10,... | collective-permute-start | bytes 2064392 | tf_op jit(solution)/shard_map/ppermute | solution.py:600
  231.3 7.7 %collective-permute-start.51 = (bf16[672,128]{1,0:T(8,128)(2,1)S(1)}, bf16[672,128]{1,0:T(8,128)(2,1)S(1)}, u32[]{:S(2)}, u32[]{:S(2)}) collective-permute-start(bf16[672,128]{1,0:T(8,128)(2,1)S(1)} %get-tuple-element.249), channel_id=1, source_target_pairs={{8,0},{16,8},{24,16},{28,24},{20,28},{12,20},{4,12},{0,4},{9,1},{1... | collective-permute-start | bytes 516104 | tf_op jit(solution)/shard_map/ppermute | solution.py:651
  232.0 7.0 %collective-permute-start.50 = (bf16[672,128]{1,0:T(8,128)(2,1)S(1)}, bf16[672,128]{1,0:T(8,128)(2,1)S(1)}, u32[]{:S(2)}, u32[]{:S(2)}) collective-permute-start(bf16[672,128]{1,0:T(8,128)(2,1)S(1)} %get-tuple-element.250), channel_id=1, source_target_pairs={{0,8},{8,16},{16,24},{24,28},{28,20},{20,12},{12,4},{4,0},{1,9},{9... | collective-permute-start | bytes 516104 | tf_op jit(solution)/shard_map/ppermute | solution.py:648
  233.4 5.6 %collective-permute-start.52 = (f32[8,24,96]{2,1,0:T(8,128)S(1)}, f32[8,24,96]{2,1,0:T(8,128)S(1)}, u32[]{:S(2)}, u32[]{:S(2)}) collective-permute-start(f32[8,24,96]{2,1,0:T(8,128)S(1)} %add.272), channel_id=1, source_target_pairs={{0,16},{1,17},{2,18},{3,19},{4,20},{5,21},{6,22},{7,23},{8,24},{9,... | collective-permute-start | bytes 221192 | tf_op jit(solution)/shard_map/ppermute | solution.py:605
  245.1 6.8 %collective-permute-start.54 = (bf16[2,1344,128]{2,1,0:T(8,128)(2,1)S(1)}, bf16[2,1344,128]{2,1,0:T(8,128)(2,1)S(1)}, u32[]{:S(2)}, u32[]{:S(2)}) collective-permute-start(bf16[2,1344,128]{2,1,0:T(8,128)(2,1)S(1)} %get-tuple-element.220.own), channel_id=1, source_target_pairs={{0,1},{1,0},{2,3},{3,2},{4,5},{5,4},{6,7},{7,6},{8,9},{9,8},{10,11... | collective-permute-start | bytes 2064392 | tf_op jit(solution)/shard_map/ppermute | solution.py:600
  245.1 6.8 %collective-permute-start.53 = (bf16[672,128]{1,0:T(8,128)(2,1)S(1)}, bf16[672,128]{1,0:T(8,128)(2,1)S(1)}, u32[]{:S(2)}, u32[]{:S(2)}) collective-permute-start(bf16[672,128]{1,0:T(8,128)(2,1)S(1)} %fusion.22), channel_id=1, source_target_pairs={{0,2},{1,3},{2,0},{3,1},{4,6},{5,7},{6,4},{7,5},{8,10},{9,11},{10,... | collective-permute-start | bytes 516104 | tf_op jit(solution)/shard_map/ppermute | solution.py:600
  255.7 10.2 %collective-permute-start.61 = (bf16[1344,128]{1,0:T(8,128)(2,1)S(1)}, bf16[1344,128]{1,0:T(8,128)(2,1)S(1)}, u32[]{:S(2)}, u32[]{:S(2)}) collective-permute-start(bf16[1344,128]{1,0:T(8,128)(2,1)S(1)} %get-tuple-element.240.split_own), channel_id=1, source_target_pairs={{0,1},{1,0},{2,3},{3,2},{4,5},{5,4},{6,7},{7,6},{8,9},{9,8},{10,11... | collective-permute-start | bytes 1032200 | tf_op jit(solution)/shard_map/ppermute | solution.py:600
  257.4 5.4 %collective-permute-start.60 = (f32[1,128]{1,0:T(1,128)S(1)}, f32[1,128]{1,0:T(1,128)S(1)}, u32[]{:S(2)}, u32[]{:S(2)}) collective-permute-start(f32[1,128]{1,0:T(1,128)S(1)} %add_add_fusion.1), channel_id=1, source_target_pairs={{0,24},{1,25},{2,26},{3,27},{4,28},{5,29},{6,30},{7,31},{8,16},{9,... | collective-permute-start | bytes 1544 | tf_op jit(solution)/shard_map/ppermute | solution.py:605
  (47 other events, 286.5 us)

commit v3 on v2

--- a/solution.py
+++ b/solution.py
@@ -72,7 +72,8 @@
     parcels, sources = refs[2 : 2 + n_parts], refs[2 + n_parts : 2 + sum(n_refs)]
     *outs, vgrad = refs[2 + sum(n_refs) : 3 + sum(n_refs) + OUTS]
     w, vec_blocks, vec, pix, target, mask_rows, mask, bias, *refs = refs[3 + sum(n_refs) + OUTS :]
-    (x0, x1, x2, branch, mlp, work, qkv, probs, attn, slope, act, hid, low, sem_in, sem_part, sem_out) = refs
+    (x0, x1, x2, branch, mlp, work, qkv, probs, inverses, attn, slope, act, hid, low, *sems) = refs
+    sem_in, sem_part, sem_out = sems
     length, width = pix.shape
     part = length // n_parts
     pairs = width // 256
@@ -188,20 +189,25 @@
             value = nn(low[...], jnp.concatenate(parts[2 * j : 2 * j + 2], 1)) + shift[:, 256 * j : 256 * j + 256]
             qkv[i, :, 256 * j : 256 * j + 256] = value.astype(bf16)
 
+    def half_lanes(half):
+        return lower_half if half == 0 else jnp.logical_not(lower_half)
+
     @pl.loop(0, HEADS // 2)
     def _(i):
         c = cols(i, LANES)
-        query, key, value = qkv[0, :, c], qkv[1, :, c], qkv[2, :, c]
+        query, key, value = qkv[0, :, c] * 0.125, qkv[1, :, c], qkv[2, :, c]
         outs = []
         for half in range(2):
-            chosen = lower_half if half == 0 else jnp.logical_not(lower_half)
-            scores = nt(jnp.where(chosen, query, jnp.zeros_like(query)), key) * 0.125
+            chosen = half_lanes(half)
+            scores = nt(jnp.where(chosen, query, jnp.zeros_like(query)), key)
             scores = jnp.where(key_valid, scores, -1e30)
-            shifted = jnp.exp(scores - jnp.max(scores, -1, keepdims=True))
-            p = shifted * (1.0 / jnp.sum(shifted, -1, keepdims=True))
-            probs[2 * i + half] = p
-            outs.append(nn(p.astype(bf16), value))
-        attn[:, c] = jnp.where(lower_half, outs[0], outs[1]).astype(bf16)
+            weights = jnp.exp(scores - jnp.max(scores, -1, keepdims=True)).astype(bf16)
+            probs[2 * i + half] = weights
+            outs.append(nn(weights, jnp.where(chosen, value, jnp.ones_like(value))))
+        total = pltpu.roll(jnp.where(lower_half, outs[1], outs[0]), LANES // 2, 1)
+        inverse = 1.0 / total
+        inverses[:, c] = inverse
+        attn[:, c] = (jnp.where(lower_half, outs[0], outs[1]) * inverse).astype(bf16)
 
     @pl.loop(0, pairs)
     def _(i):
@@ -322,20 +328,30 @@
     def _(i):
         put_pair(i, ROW_O, nn(flipped, hid[:, cols(i)]))
 
+    lane = lax.broadcasted_iota(jnp.int32, (1, LANES), 1)
+
     @pl.loop(0, HEADS // 2)
     def _(i):
         c = cols(i, LANES)
         query, key, value = qkv[0, :, c], qkv[1, :, c], qkv[2, :, c]
-        out_grad = low[:, c]
+        out_grad, inverse = low[:, c].astype(f32), inverses[:, c]
+        product = out_grad * attn[:, c].astype(f32)
+        scaled_query = (query.astype(f32) * inverse).astype(bf16)
+        scaled_grad = (out_grad * inverse).astype(bf16)
         outs = []
         for half in range(2):
-            chosen = lower_half if half == 0 else jnp.logical_not(lower_half)
-            p = probs[2 * i + half]
-            dp = nt(jnp.where(chosen, out_grad, jnp.zeros_like(out_grad)), value)
-            ds = (p * (dp - jnp.sum(p * dp, -1, keepdims=True))).astype(bf16)
-            outs.append((nn(ds, key), tn(ds, query), tn(p.astype(bf16), out_grad)))
+            chosen = half_lanes(half)
+            spare = LANES // 2 * (1 - half)
+            sums = jnp.sum(jnp.where(chosen, product, 0.0), -1, keepdims=True)
+            rough = sums.astype(bf16).astype(f32)
+            fine = jnp.where(lane == spare, rough, jnp.where(lane == spare + 1, sums - rough, 0.0))
+            left = jnp.where(chosen, out_grad, fine).astype(bf16)
+            minus = jnp.where(jnp.logical_or(lane == spare, lane == spare + 1), -1.0, 0.0).astype(bf16)
+            weights = probs[2 * i + half]
+            ds = (weights.astype(f32) * nt(left, jnp.where(chosen, value, minus))).astype(bf16)
+            outs.append((nn(ds, key), tn(ds, scaled_query), tn(weights, scaled_grad)))
         dq, dk, dv = (jnp.where(lower_half, one, two) for one, two in zip(*outs))
-        dq, dk = (dq * 0.125, dk * 0.125)
+        dq, dk = (dq * inverse * 0.125, dk * 0.125)
         vgrad[5:6, c] = column_sum(dq)
         vgrad[6:7, c] = column_sum(dv)
         qkv[0, :, c], qkv[1, :, c], qkv[2, :, c] = (dq.astype(bf16), dk.astype(bf16), dv.astype(bf16))
@@ -420,7 +436,8 @@
             big,
             big,
             pltpu.VMEM((3, length, width), bf16),
-            pltpu.VMEM((HEADS, length, length), f32),
+            pltpu.VMEM((HEADS, length, length), bf16),
+            big,
             small,
             pltpu.VMEM((length, hidden), f32),
             pltpu.VMEM((length, hidden), bf16),
@@ -508,8 +525,16 @@
 def adam_kernel(core, squares, table, own, split_own, other, split_other, *refs):
     masters, moments, variances = refs[:5], refs[5:10], refs[10:15]
     loss_out, norm_out, *outs = refs[15:32]
-    buffers, sem_in, sem_out = refs[32:44], *refs[44:]
+    buffers, grads, sem_in, sem_out = refs[32:44], *refs[44:]
     order = (3, 2, 1, 0)
+    here, there = 3 * core[0], 3 - 3 * core[0]
+    for value, place in (
+        (own, pl.ds(here, 2)),
+        (split_own, here + 2),
+        (other, pl.ds(there, 2)),
+        (split_other, there + 2),
+    ):
+        pltpu.make_async_copy(value, grads.at[place], sem_in.at[12]).start()
     for kind in order:
         for k, state in enumerate((masters, moments, variances)):
             pltpu.make_async_copy(state[kind], buffers[4 * k + kind], sem_in.at[4 * k + kind]).start()
@@ -517,20 +542,24 @@
     count = table[rows + 1 : rows + 2, 0:1]
     norm = jnp.sqrt(squares[0:1, 0:1]) / count
     scale = clip_limit / jnp.maximum(norm, clip_limit) / count
+    grad_scale = (1.0 - beta_one) * scale
+    square_scale = (1.0 - beta_two) / (1.0 - beta_one) ** 2
+    root_scale = (1.0 - beta_two**adam_step) ** -0.5
+    step_scale = matrix_rate / (1.0 - beta_one**adam_step)
+    keep_scale = 1.0 - matrix_rate * weight_decay
     loss_out[0, 0] = (table[rows : rows + 1, 0:1] / count)[0, 0]
     norm_out[0, 0] = norm[0, 0]
 
-    def grad_of(cut, row, rows):
-        mine = cut // 3 == core[0]
-        index, part = jnp.minimum(lax.rem(cut, 3), 1), slice(row, row + rows)
-        grad = jnp.where(mine, own[index, part, :], other[index, part, :])
-        split = jnp.where(mine, split_own[part, :], split_other[part, :])
-        return jnp.where(lax.rem(cut, 3) == 2, split, grad).astype(f32) * scale
+    pltpu.make_async_copy(grads, grads, sem_in.at[12]).wait()
 
     def update(kind, where, cut, row, rows):
-        states = (buffers[4 * k + kind][where] for k in range(3))
-        values = adam(*states, grad_of(cut, row, rows), matrix_rate, weight_decay)
-        for k, value in zip((1, 2, 0), values):
+        weight, moment, variance = (buffers[4 * k + kind][where] for k in range(3))
+        part = grads[cut, row : row + rows, :].astype(f32) * grad_scale
+        moment = beta_one * moment + part
+        variance = beta_two * variance + (square_scale * part) * part
+        divisor = (root_scale * variance) * lax.rsqrt(variance) + adam_eps
+        step = (step_scale * moment) * lax.rsqrt(divisor * divisor)
+        for k, value in enumerate((keep_scale * weight - step, moment, variance)):
             buffers[4 * k + kind][where] = value
 
     def each(kind, body):
@@ -579,10 +608,14 @@
     loss, norm, *results = pl.pallas_call(
         adam_kernel,
         out_shape=[jax.ShapeDtypeStruct((1, 1), f32)] * 2 + shapes * 3,
-        in_specs=[smem] + [vmem] * (2 + len(grads)) + ([anywhere] * 4 + [vmem]) * 3,
+        in_specs=[smem] + [vmem] * 2 + [anywhere] * len(grads) + ([anywhere] * 4 + [vmem]) * 3,
         out_specs=[smem] * 2 + ([anywhere] * 4 + [vmem]) * 3,
         scratch_shapes=[pltpu.VMEM(shape.shape, f32) for shape in shapes[:4] * 3]
-        + [pltpu.SemaphoreType.DMA((12,))] * 2,
+        + [
+            pltpu.VMEM((CUTS, ROWS, LANES), bf16),
+            pltpu.SemaphoreType.DMA((13,)),
+            pltpu.SemaphoreType.DMA((12,)),
+        ],
         compiler_params=pltpu.CompilerParams(vmem_limit_bytes=56 * 1024 * 1024),
         name="adam",
     )(core, squares, table, *grads, *masters, *moments, *variances)
@@ -763,6 +796,8 @@
         def rounded(*values):
             return sum(value.astype(f32) for value in values).astype(bf16)
 
+        half = ROWS // 4
+
         def low_half(value):
             return jnp.pad(value.astype(f32), ((0, 1), (0, 0), (0, 0)))
 
@@ -781,45 +816,52 @@
         )
         small = small + small_more
         whole, split = {}, dict(zip((4, 3, 5), split_first[:, 0]))
-        left, right, pair_first, whole_next, got_rest, split_rest = tick(
+        left, right, pair_first, whole_next, got_rest, split_rest, small = tick(
             ahead(opposite[0, :1]),
             behind(opposite[0, 1:]),
             trade(split_first[:, 1]),
             rounded(keeps[1], next_got),
             across(send_rest),
             rounded(split_keeps[1], across(split_send_rest)),
+            small,
         )
         whole.update(zip((3, 5), whole_next))
         split.update(zip((2, 6, 1, 7, 0), split_rest[:, 0]))
         pair = dict(zip((4, 3, 5), pair_first))
-        left, right, split_left, pair_rest, whole_rest, small, small_more = tick(
+        pair_next, small = tick(trade(split_rest[:2, 1]), small)
+        left, right, split_left, split_right, pair_next, whole_rest, split_rest, small, small_more = tick(
             ahead(rounded(whole[3], low_half(left))),
             behind(rounded(whole[5], high_half(right))),
-            ahead(rounded(split[4], pair[4])),
-            trade(split_rest[:, 1]),
+            ahead(rounded(split[4][:half], pair[4][:half])),
+            behind(rounded(split[4][half:], pair[4][half:])),
+            pair_next,
             rounded(keeps[2], got_rest),
+            split_rest,
             small,
             trade(small),
         )
-        pair.update(zip((2, 6, 1, 7, 0), pair_rest))
+        pair.update(zip((2, 6), pair_next))
         whole.update(zip((2, 6, 1, 7, 0), whole_rest))
-        small = small + small_more
-        left, right, split_left, split_right, small, small_more = tick(
+        small = jnp.take(small + small_more, group ^ jnp.array([0, 4, 2, 6, 1, 5, 3, 7]), axis=0)
+        pair_rest, small = tick(trade(split_rest[2:, 1]), small)
+        left, right, split_left, split_right, pair_rest, small, small_more = tick(
             ahead(rounded(whole[2], left)),
             behind(rounded(whole[6], right)),
-            ahead(rounded(split[3], pair[3], split_left)),
-            behind(rounded(split[5], pair[5])),
-            small,
-            hop(small, 1, 0, n_dp, n_seq),
-        )
+            ahead(rounded(split[3], pair[3], jnp.pad(split_left.astype(f32), ((0, half), (0, 0))))),
+            behind(rounded(split[5], pair[5], jnp.pad(split_right.astype(f32), ((half, 0), (0, 0))))),
+            pair_rest,
+            small[:4],
+            hop(small[4:], 1, 0, n_dp, n_seq),
+        )
+        pair.update(zip((1, 7, 0), pair_rest))
         small = small + small_more
         left, right, split_left, split_right, small, small_more = tick(
             ahead(rounded(whole[1], left)),
             behind(rounded(whole[7], right)),
             ahead(rounded(split[2], pair[2], split_left)),
             behind(rounded(split[6], pair[6], split_right)),
-            small,
-            hop(small, 2, 0, n_dp, n_seq),
+            small[:2],
+            hop(small[2:], 2, 0, n_dp, n_seq),
         )
         small = small + small_more
         own = rounded(whole[0], left, right)
@@ -828,10 +870,10 @@
             trade(own),
             ahead(rounded(split[1], pair[1], split_left)),
             behind(rounded(split[7], pair[7], split_right)),
-            small,
-            hop(small, 4, 0, n_dp, n_seq),
-        )
-        small = lax.dynamic_index_in_dim(small + small_more, group, 0, keepdims=False)
+            small[0],
+            hop(small[1], 4, 0, n_dp, n_seq),
+        )
+        small = small + small_more
         split_own, own, other_chip, small = tick(
             rounded(split[0], pair[0], split_left, split_right), own, other_chip, small
         )
@@ -843,8 +885,8 @@
         )
         split_other = across(split_own)
         squares = jnp.full((1, LANES), squares + jnp.sum(jnp.square(split_own.astype(f32))))
-        for hops in (((0, 0), (0, 1), (1, 0), (1, 1)), ((0, 0), (2, 0), (4, 0), (6, 0))):
-            squares = tree_sum([squares] + [hop(squares, *ks, n_dp, n_seq) for ks in hops[1:]])
+        for hops in (((0, 1), (1, 0), (1, 1)), ((2, 0), (4, 0), (6, 0))):
+            squares = tree_sum([squares] + [hop(squares, *ks, n_dp, n_seq) for ks in hops])
     else:
         def by_place(groups, values):
             spread = dict(zip((r for places in groups for r in places), jnp.concatenate(values)))

time: 279 us -> 275 us (0.986)
  waiting for transfers between devices: 141 us -> 128 us
  other arithmetic: 14.4 us -> 21.4 us
  local copies, waits for them, and re-layouts: 6.59 us -> 10.6 us
  Pallas kernels: 65.7 us -> 62.9 us
    ppermute x9, waiting for transfers between devices: 42 us -> 21 us  [hop(): return lax.ppermute(value, ('dp', 'seq'), pairs)]
    ppermute x30 -> x31, waiting for transfers between devices: 63.9 us -> 73.6 us  [seq_flip(): return lax.ppermute(value, 'seq', [(i, i ^ k) for i in range(n_seq)])]
    ppermute x11 -> x12, waiting for transfers between devices: 20.2 us -> 13.4 us  [behind(): return lax.ppermute(value, 'dp', backward)]
    convert_element_type x14, other arithmetic: 5.44 us -> 11.6 us  [rounded(): return sum((value.astype(f32) for value in values)).astype(bf16)]
    ppermute x12, waiting for transfers between devices: 14.9 us -> 19.5 us  [ahead(): return lax.ppermute(value, 'dp', forward)]
    ppermute x11 -> x12, starting transfers between devices: 9.72 us -> 8.36 us  [behind(): return lax.ppermute(value, 'dp', backward)]
    ppermute x30 -> x31, starting transfers between devices: 12.5 us -> 13.1 us  [seq_flip(): return lax.ppermute(value, 'seq', [(i, i ^ k) for i in range(n_seq)])]
  transfers between devices with their start and end apart: 62 -> 64, of which waited for: 29 -> 32; matrix products, arithmetic and copies ran while one was open for 5% -> 7% of each run, Pallas kernels for 1% -> 1%
where the time goes in v3:
time: 275 us; the launch traced here: 274 us
  waiting for transfers between devices  128 us (47%)
  Pallas kernels  62.9 us (23%)
  starting transfers between devices  48.5 us (18%)
  other arithmetic  21.4 us (8%)
  local copies, waits for them, and re-layouts  10.6 us (4%)
  between operations  3.43 us (1%)
    ppermute x31, waiting for transfers between devices, seq_flip(): return lax.ppermute(value, 'seq', [(i, i ^ k) for i in range(n_seq)])  73.6 us
    pallas_call x1, Pallas kernels, run_step(): pl.pallas_call(partial(step_kernel, pieces, vec_pieces, (len(parcels), le...  46.3 us
    ppermute x9, waiting for transfers between devices, hop(): return lax.ppermute(value, ('dp', 'seq'), pairs)  21 us
    ppermute x12, waiting for transfers between devices, ahead(): return lax.ppermute(value, 'dp', forward)  19.5 us
    ppermute x12, starting transfers between devices, ahead(): return lax.ppermute(value, 'dp', forward)  17.6 us
    ppermute x12, waiting for transfers between devices, behind(): return lax.ppermute(value, 'dp', backward)  13.4 us
    ppermute x31, starting transfers between devices, seq_flip(): return lax.ppermute(value, 'seq', [(i, i ^ k) for i in range(n_seq)])  13.1 us
    convert_element_type x14, other arithmetic, rounded(): return sum((value.astype(f32) for value in values)).astype(bf16)  11.6 us
  transfers between devices with their start and end apart: 64, of which 32 were waited for; matrix products, arithmetic and copies ran while one was open for 7% of the time, Pallas kernels for 1%

profile of v3, /device:TPU:0, one launch (start us, length us, event | category | flops | bytes accessed | tf_op | source)
XLA Modules:
  0.0 274.3 jit_solution(719243934344942017)
XLA Ops:
  1.4 4.2 %pack.1 = (bf16[6,1344,128]{2,1,0:T(8,128)(2,1)}, bf16[2,1376,128]{2,1,0:T(8,128)(2,1)}, bf16[2,1376,128]{2,1,0:T(8,128)(2,1)}) custom-call(s32[4]{0:T(128)} %pad_add_fusion.2.chosen, f32[3,96,768]{2,1,0:T(8,128)} %refs_0_.1, f32[96,2304]{1,0:T(8,128)} %refs_1_.1, f32[96,3072]{1,0:T(8,128)} %refs_2_.1, f32[384,768]{1,0:T(8,128)} %refs_3_.1, f32[20,96]{1,0:T(8,128)} %refs_4_.1), custom_call_target="tpu_custom_call" | custom-call | tf_op jit(solution)/shard_map/pack/pallas_call | solution.py:480
  5.5 3.1 %collective-permute-start = (bf16[2,1376,128]{2,1,0:T(8,128)(2,1)}, bf16[2,1376,128]{2,1,0:T(8,128)(2,1)S(1)}, u32[]{:S(2)}, u32[]{:S(2)}) collective-permute-start(bf16[2,1376,128]{2,1,0:T(8,128)(2,1)} %get-tuple-element.136.refs_7_), channel_id=1, source_target_pairs={{0,8},{8,16},{16,24},{24,28},{28,20},{20,12},{12,4},{4,0},{1,9},{9... | collective-permute-start | bytes 2113544 | tf_op jit(solution)/shard_map/ppermute | solution.py:681
  9.1 2.1 parcels.1
  11.2 1.9 collective-permute-start.3
  13.3 6.5 %collective-permute-done.3.refs_4_ = bf16[144,768]{1,0:T(8,128)(2,1)S(1)} collective-permute-done((bf16[144,768]{1,0:T(8,128)(2,1)}, bf16[144,768]{1,0:T(8,128)(2,1)S(1)}, u32[]{:S(2)}, u32[]{:S(2)}) %collective-permute-start.3) | collective-permute-done | bytes 221216 | tf_op jit(solution)/shard_map/ppermute | solution.py:633
  19.7 4.2 %collective-permute-done.4.refs_5_ = bf16[144,768]{1,0:T(8,128)(2,1)S(1)} collective-permute-done((bf16[144,768]{1,0:T(8,128)(2,1)}, bf16[144,768]{1,0:T(8,128)(2,1)S(1)}, u32[]{:S(2)}, u32[]{:S(2)}) %collective-permute-start.4) | collective-permute-done | bytes 221216 | tf_op jit(solution)/shard_map/ppermute | solution.py:633
  26.2 1.6 collective-permute-start.7
  27.7 1.6 collective-permute-start.5
  30.3 3.8 %fusion.8.refs_1_ = f32[256,768]{1,0:T(8,128)} fusion(f32[768]{0:T(1024)S(1)} %fusion.31, f32[256]{0:T(256)S(1)} %iota_convert_fusion, pred[768]{0:T(1024)(128)(4,1)S(1)} %fusion.26), kind=kLoop, calls=%fused_computation.26 | loop fusion | flops 393216 | bytes 791296 | tf_op jit(solution)/shard_map/jit(_where)/select_n | solution.py:629
  34.1 8.8 %collective-permute-done.7.refs_14_ = bf16[2,1376,128]{2,1,0:T(8,128)(2,1)S(1)} collective-permute-done((bf16[2,1376,128]{2,1,0:T(8,128)(2,1)S(1)}, bf16[2,1376,128]{2,1,0:T(8,128)(2,1)S(1)}, u32[]{:S(2)}, u32[]{:S(2)}) %collective-permute-start.7) | collective-permute-done | bytes 704544 | tf_op jit(solution)/shard_map/ppermute | solution.py:633
  42.9 1.5 collective-permute-done.5.refs_12_
  47.4 1.6 collective-permute-start.10
  50.6 17.5 %collective-permute-done.12.refs_20_ = bf16[2,1376,128]{2,1,0:T(8,128)(2,1)} collective-permute-done((bf16[2,1376,128]{2,1,0:T(8,128)(2,1)S(1)}, bf16[2,1376,128]{2,1,0:T(8,128)(2,1)}, u32[]{:S(2)}, u32[]{:S(2)}) %collective-permute-start.12) | collective-permute-done | bytes 704544 | tf_op jit(solution)/shard_map/ppermute | solution.py:633
  69.1 1.6 collective-permute-start.16
  75.3 7.4 %collective-permute-done.17.refs_26_ = bf16[1,1376,128]{2,1,0:T(8,128)(2,1)S(1)} collective-permute-done((bf16[1,1376,128]{2,1,0:T(8,128)(2,1)S(1)}, bf16[1,1376,128]{2,1,0:T(8,128)(2,1)S(1)}, u32[]{:S(2)}, u32[]{:S(2)}) %collective-permute-start.17) | collective-permute-done | bytes 352288 | tf_op jit(solution)/shard_map/ppermute | solution.py:684
  82.7 6.6 %collective-permute-done.18.refs_24_ = bf16[2,1376,128]{2,1,0:T(8,128)(2,1)} collective-permute-done((bf16[2,1376,128]{2,1,0:T(8,128)(2,1)S(1)}, bf16[2,1376,128]{2,1,0:T(8,128)(2,1)}, u32[]{:S(2)}, u32[]{:S(2)}) %collective-permute-start.18) | collective-permute-done | bytes 704544 | tf_op jit(solution)/shard_map/ppermute | solution.py:633
  90.0 3.3 %collective-permute-done.23.refs_28_ = bf16[1,1376,128]{2,1,0:T(8,128)(2,1)S(1)} collective-permute-done((bf16[1,1376,128]{2,1,0:T(8,128)(2,1)S(1)}, bf16[1,1376,128]{2,1,0:T(8,128)(2,1)S(1)}, u32[]{:S(2)}, u32[]{:S(2)}) %collective-permute-start.23) | collective-permute-done | bytes 352288 | tf_op jit(solution)/shard_map/ppermute | solution.py:633
  94.6 46.3 %step.1 = (bf16[1,2,1344,128]{3,2,1,0:T(8,128)(2,1)}, bf16[1,2,1344,128]{3,2,1,0:T(8,128)(2,1)}, bf16[2,2,1344,128]{3,2,1,0:T(8,128)(2,1)}, bf16[2,2,1344,128]{3...) custom-call(s32[56]{0:T(128)} %concatenate.20.refs_0_, ...), custom_call_target="tpu_custom_call" | custom-call | tf_op jit(solution)/shard_map/step/pallas_call | solution.py:410
  143.4 1.6 add_convert_fusion.5
  145.1 1.7 collective-permute-done.26
  147.7 1.6 collective-permute-start.29
  150.8 4.8 %collective-permute-done.33 = bf16[5,2,672,128]{3,2,1,0:T(8,128)(2,1)S(1)} collective-permute-done((bf16[5,2,672,128]{3,2,1,0:T(8,128)(2,1)}, bf16[5,2,672,128]{3,2,1,0:T(8,128)(2,1)S(1)}, u32[]{:S(2)}, u32[]{:S(2)}) %collective-permute-start.33) | collective-permute-done | bytes 1720352 | tf_op jit(solution)/shard_map/ppermute | solution.py:633
  156.2 1.7 collective-permute-done.29
  159.2 4.0 %collective-permute-done.31 = bf16[3,672,128]{2,1,0:T(8,128)(2,1)S(1)} collective-permute-done((bf16[3,672,128]{2,1,0:T(8,128)(2,1)S(1)}, bf16[3,672,128]{2,1,0:T(8,128)(2,1)S(1)}, u32[]{:S(2)}, u32[]{:S(2)}) %collective-permute-start.31) | collective-permute-done | bytes 516128 | tf_op jit(solution)/shard_map/ppermute | solution.py:633
  163.8 1.6 collective-permute-start.36
  166.1 1.6 collective-permute-start.34
  168.2 3.8 %collective-permute-done.38 = bf16[2,672,128]{2,1,0:T(8,128)(2,1)S(1)} collective-permute-done((bf16[2,672,128]{2,1,0:T(8,128)(2,1)S(1)}, bf16[2,672,128]{2,1,0:T(8,128)(2,1)S(1)}, u32[]{:S(2)}, u32[]{:S(2)}) %collective-permute-start.38) | collective-permute-done | bytes 344096 | tf_op jit(solution)/shard_map/ppermute | solution.py:633
  173.6 2.9 %collective-permute-done.39 = f32[8,24,96]{2,1,0:T(8,128)S(1)} collective-permute-done((f32[8,24,96]{2,1,0:T(8,128)S(1)}, f32[8,24,96]{2,1,0:T(8,128)S(1)}, u32[]{:S(2)}, u32[]{:S(2)}) %collective-permute-start.39) | collective-permute-done | bytes 73760 | tf_op jit(solution)/shard_map/ppermute | solution.py:633
  176.5 5.7 %collective-permute-done.34 = bf16[2,1344,128]{2,1,0:T(8,128)(2,1)S(1)} collective-permute-done((bf16[2,1344,128]{2,1,0:T(8,128)(2,1)S(1)}, bf16[2,1344,128]{2,1,0:T(8,128)(2,1)S(1)}, u32[]{:S(2)}, u32[]{:S(2)}) %collective-permute-start.34) | collective-permute-done | bytes 688160 | tf_op jit(solution)/shard_map/ppermute | solution.py:681
  184.4 1.5 collective-permute-start.44
  185.9 1.4 fusion.4
  187.3 1.5 collective-permute-start.40
  190.2 1.5 collective-permute-start.42
  192.9 1.4 gather_fusion.1
  194.4 1.6 collective-permute-done.44
  196.6 10.0 %collective-permute-done.42 = bf16[672,128]{1,0:T(8,128)(2,1)} collective-permute-done((bf16[672,128]{1,0:T(8,128)(2,1)}, bf16[672,128]{1,0:T(8,128)(2,1)}, u32[]{:S(2)}, u32[]{:S(2)}) %collective-permute-start.42) | collective-permute-done | bytes 172064 | tf_op jit(solution)/shard_map/ppermute | solution.py:681
  207.3 1.8 fusion
  215.2 12.2 %collective-permute-done.50 = f32[2,24,96]{2,1,0:T(8,128)S(1)} collective-permute-done((f32[2,24,96]{2,1,0:T(8,128)S(1)}, f32[2,24,96]{2,1,0:T(8,128)S(1)}, u32[]{:S(2)}, u32[]{:S(2)}) %collective-permute-start.50) | collective-permute-done | bytes 18464 | tf_op jit(solution)/shard_map/ppermute | solution.py:638
  229.9 1.7 collective-permute-start.53
  231.6 1.9 collective-permute-start.54
  233.5 3.6 %collective-permute-done.54 = f32[24,96]{1,0:T(8,128)S(1)} collective-permute-done((f32[24,96]{1,0:T(8,128)S(1)}, f32[24,96]{1,0:T(8,128)S(1)}, u32[]{:S(2)}, u32[]{:S(2)}) %collective-permute-start.54) | collective-permute-done | bytes 9248 | tf_op jit(solution)/shard_map/ppermute | solution.py:638
  237.1 3.3 %collective-permute-done.51 = bf16[2,1344,128]{2,1,0:T(8,128)(2,1)S(1)} collective-permute-done((bf16[2,1344,128]{2,1,0:T(8,128)(2,1)S(1)}, bf16[2,1344,128]{2,1,0:T(8,128)(2,1)S(1)}, u32[]{:S(2)}, u32[]{:S(2)}) %collective-permute-start.51) | collective-permute-done | bytes 688160 | tf_op jit(solution)/shard_map/ppermute | solution.py:633
  244.8 4.3 %collective-permute-done.55 = bf16[672,128]{1,0:T(8,128)(2,1)S(1)} collective-permute-done((bf16[672,128]{1,0:T(8,128)(2,1)S(1)}, bf16[672,128]{1,0:T(8,128)(2,1)S(1)}, u32[]{:S(2)}, u32[]{:S(2)}) %collective-permute-start.55) | collective-permute-done | bytes 172064 | tf_op jit(solution)/shard_map/ppermute | solution.py:633
  250.7 1.5 collective-permute-start.58
  255.2 1.5 collective-permute-start.60
  257.1 2.5 collective-permute-start.62
  259.6 1.5 collective-permute-done.61
  263.8 10.3 %adam.1 = (f32[1,1]{1,0:T(1,128)}, f32[1,1]{1,0:T(1,128)}, f32[3,96,768]{2,1,0:T(8,128)}, f32[96,2304]{1,0:T(8,128)}, f32[96,3072]{1,0:T(8,128)}, /*index=5*/f32...) custom-call(s32[1]{0:T(128)} %bitcast.core, ...), custom_call_target="tpu_custom_call" | custom-call | tf_op jit(solution)/shard_map/adam/pallas_call | solution.py:608
  (232 shorter events, 51.2 us)
Async XLA Ops:
  5.5 19.0 %collective-permute-start = (bf16[2,1376,128]{2,1,0:T(8,128)(2,1)}, bf16[2,1376,128]{2,1,0:T(8,128)(2,1)S(1)}, u32[]{:S(2)}, u32[]{:S(2)}) collective-permute-start(bf16[2,1376,128]{2,1,0:T(8,128)(2,1)} %get-tuple-element.136.refs_7_), channel_id=1, source_target_pairs={{0,8},{8,16},{16,24},{24,28},{28,20},{20,12},{12,4},{4,0},{1,9},{9... | collective-permute-start | bytes 2113544 | tf_op jit(solution)/shard_map/ppermute | solution.py:681
  8.6 17.5 %collective-permute-start.1 = (bf16[2,1376,128]{2,1,0:T(8,128)(2,1)}, bf16[2,1376,128]{2,1,0:T(8,128)(2,1)S(1)}, u32[]{:S(2)}, u32[]{:S(2)}) collective-permute-start(bf16[2,1376,128]{2,1,0:T(8,128)(2,1)} %get-tuple-element.137), channel_id=1, source_target_pairs={{8,0},{16,8},{24,16},{28,24},{20,28},{12,20},{4,12},{0,4},{9,1},{1... | collective-permute-start | bytes 2113544 | tf_op jit(solution)/shard_map/ppermute | solution.py:684
  11.2 8.5 %collective-permute-start.3 = (bf16[144,768]{1,0:T(8,128)(2,1)}, bf16[144,768]{1,0:T(8,128)(2,1)S(1)}, u32[]{:S(2)}, u32[]{:S(2)}) collective-permute-start(bf16[144,768]{1,0:T(8,128)(2,1)} %get-tuple-element.139), channel_id=1, source_target_pairs={{0,2},{1,3},{2,0},{3,1},{4,6},{5,7},{6,4},{7,5},{8,10},{9,11},{10,... | collective-permute-start | bytes 663560 | tf_op jit(solution)/shard_map/ppermute | solution.py:633
  13.1 10.8 %collective-permute-start.4 = (bf16[144,768]{1,0:T(8,128)(2,1)}, bf16[144,768]{1,0:T(8,128)(2,1)S(1)}, u32[]{:S(2)}, u32[]{:S(2)}) collective-permute-start(bf16[144,768]{1,0:T(8,128)(2,1)} %get-tuple-element.140), channel_id=1, source_target_pairs={{0,3},{1,2},{2,1},{3,0},{4,7},{5,6},{6,5},{7,4},{8,11},{9,10},{10,... | collective-permute-start | bytes 663560 | tf_op jit(solution)/shard_map/ppermute | solution.py:633
  26.2 16.7 %collective-permute-start.7 = (bf16[2,1376,128]{2,1,0:T(8,128)(2,1)S(1)}, bf16[2,1376,128]{2,1,0:T(8,128)(2,1)S(1)}, u32[]{:S(2)}, u32[]{:S(2)}) collective-permute-start(bf16[2,1376,128]{2,1,0:T(8,128)(2,1)S(1)} %pad_maximum_fusion), channel_id=1, source_target_pairs={{0,2},{1,3},{2,0},{3,1},{4,6},{5,7},{6,4},{7,5},{8,10},{9,11},{10,... | collective-permute-start | bytes 2113544 | tf_op jit(solution)/shard_map/ppermute | solution.py:633
  27.7 16.6 %collective-permute-start.5 = (bf16[2,1376,128]{2,1,0:T(8,128)(2,1)S(1)}, bf16[2,1376,128]{2,1,0:T(8,128)(2,1)S(1)}, u32[]{:S(2)}, u32[]{:S(2)}) collective-permute-start(bf16[2,1376,128]{2,1,0:T(8,128)(2,1)S(1)} %collective-permute-done.refs_8_), channel_id=1, source_target_pairs={{0,8},{8,16},{16,24},{24,28},{28,20},{20,12},{12,4},{4,0},{1,9},{9... | collective-permute-start | bytes 2113544 | tf_op jit(solution)/shard_map/ppermute | solution.py:681
  29.3 16.3 %collective-permute-start.6 = (bf16[2,1376,128]{2,1,0:T(8,128)(2,1)S(1)}, bf16[2,1376,128]{2,1,0:T(8,128)(2,1)S(1)}, u32[]{:S(2)}, u32[]{:S(2)}) collective-permute-start(bf16[2,1376,128]{2,1,0:T(8,128)(2,1)S(1)} %collective-permute-done.1.refs_9_), channel_id=1, source_target_pairs={{8,0},{16,8},{24,16},{28,24},{20,28},{12,20},{4,12},{0,4},{9,1},{1... | collective-permute-start | bytes 2113544 | tf_op jit(solution)/shard_map/ppermute | solution.py:684
  29.8 15.9 %collective-permute-start.8 = (bf16[2,1376,128]{2,1,0:T(8,128)(2,1)S(1)}, bf16[2,1376,128]{2,1,0:T(8,128)(2,1)S(1)}, u32[]{:S(2)}, u32[]{:S(2)}) collective-permute-start(bf16[2,1376,128]{2,1,0:T(8,128)(2,1)S(1)} %collective-permute-done.refs_8_), channel_id=1, source_target_pairs={{0,1},{1,0},{2,3},{3,2},{4,5},{5,4},{6,7},{7,6},{8,9},{9,8},{10,11... | collective-permute-start | bytes 2113544 | tf_op jit(solution)/shard_map/ppermute | solution.py:633
  29.8 15.9 %collective-permute-start.9 = (bf16[2,1376,128]{2,1,0:T(8,128)(2,1)S(1)}, bf16[2,1376,128]{2,1,0:T(8,128)(2,1)S(1)}, u32[]{:S(2)}, u32[]{:S(2)}) collective-permute-start(bf16[2,1376,128]{2,1,0:T(8,128)(2,1)S(1)} %collective-permute-done.1.refs_9_), channel_id=1, source_target_pairs={{0,1},{1,0},{2,3},{3,2},{4,5},{5,4},{6,7},{7,6},{8,9},{9,8},{10,11... | collective-permute-start | bytes 2113544 | tf_op jit(solution)/shard_map/ppermute | solution.py:633
  47.4 20.6 %collective-permute-start.10 = (bf16[2,1376,128]{2,1,0:T(8,128)(2,1)S(1)}, bf16[2,1376,128]{2,1,0:T(8,128)(2,1)S(1)}, u32[]{:S(2)}, u32[]{:S(2)}) collective-permute-start(bf16[2,1376,128]{2,1,0:T(8,128)(2,1)S(1)} %collective-permute-done.5.refs_12_), channel_id=1, source_target_pairs={{0,8},{8,16},{16,24},{24,28},{28,20},{20,12},{12,4},{4,0},{1,9},{9... | collective-permute-start | bytes 2113544 | tf_op jit(solution)/shard_map/ppermute | solution.py:681
  49.1 19.0 %collective-permute-start.11 = (bf16[2,1376,128]{2,1,0:T(8,128)(2,1)S(1)}, bf16[2,1376,128]{2,1,0:T(8,128)(2,1)S(1)}, u32[]{:S(2)}, u32[]{:S(2)}) collective-permute-start(bf16[2,1376,128]{2,1,0:T(8,128)(2,1)S(1)} %collective-permute-done.6.refs_13_), channel_id=1, source_target_pairs={{8,0},{16,8},{24,16},{28,24},{20,28},{12,20},{4,12},{0,4},{9,1},{1... | collective-permute-start | bytes 2113544 | tf_op jit(solution)/shard_map/ppermute | solution.py:684
  49.6 18.5 %collective-permute-start.14 = (bf16[2,1376,128]{2,1,0:T(8,128)(2,1)S(1)}, bf16[2,1376,128]{2,1,0:T(8,128)(2,1)S(1)}, u32[]{:S(2)}, u32[]{:S(2)}) collective-permute-start(bf16[2,1376,128]{2,1,0:T(8,128)(2,1)S(1)} %collective-permute-done.6.refs_13_), channel_id=1, source_target_pairs={{0,1},{1,0},{2,3},{3,2},{4,5},{5,4},{6,7},{7,6},{8,9},{9,8},{10,11... | collective-permute-start | bytes 2113544 | tf_op jit(solution)/shard_map/ppermute | solution.py:633
  49.7 18.4 %collective-permute-start.12 = (bf16[2,1376,128]{2,1,0:T(8,128)(2,1)S(1)}, bf16[2,1376,128]{2,1,0:T(8,128)(2,1)}, u32[]{:S(2)}, u32[]{:S(2)}) collective-permute-start(bf16[2,1376,128]{2,1,0:T(8,128)(2,1)S(1)} %pad_maximum_fusion.1), channel_id=1, source_target_pairs={{0,2},{1,3},{2,0},{3,1},{4,6},{5,7},{6,4},{7,5},{8,10},{9,11},{10,... | collective-permute-start | bytes 2113544 | tf_op jit(solution)/shard_map/ppermute | solution.py:633
  50.3 17.8 %collective-permute-start.15 = (bf16[2,1376,128]{2,1,0:T(8,128)(2,1)S(1)}, bf16[2,1376,128]{2,1,0:T(8,128)(2,1)S(1)}, u32[]{:S(2)}, u32[]{:S(2)}) collective-permute-start(bf16[2,1376,128]{2,1,0:T(8,128)(2,1)S(1)} %collective-permute-done.7.refs_14_), channel_id=1, source_target_pairs={{0,1},{1,0},{2,3},{3,2},{4,5},{5,4},{6,7},{7,6},{8,9},{9,8},{10,11... | collective-permute-start | bytes 2113544 | tf_op jit(solution)/shard_map/ppermute | solution.py:633
  69.1 20.2 %collective-permute-start.16 = (bf16[2,1376,128]{2,1,0:T(8,128)(2,1)S(1)}, bf16[2,1376,128]{2,1,0:T(8,128)(2,1)}, u32[]{:S(2)}, u32[]{:S(2)}) collective-permute-start(bf16[2,1376,128]{2,1,0:T(8,128)(2,1)S(1)} %collective-permute-done.10.refs_17_), channel_id=1, source_target_pairs={{0,8},{8,16},{16,24},{24,28},{28,20},{20,12},{12,4},{4,0},{1,9},{9... | collective-permute-start | bytes 2113544 | tf_op jit(solution)/shard_map/ppermute | solution.py:681
  70.8 18.6 %collective-permute-start.20 = (bf16[2,1376,128]{2,1,0:T(8,128)(2,1)S(1)}, bf16[2,1376,128]{2,1,0:T(8,128)(2,1)}, u32[]{:S(2)}, u32[]{:S(2)}) collective-permute-start(bf16[2,1376,128]{2,1,0:T(8,128)(2,1)S(1)} %collective-permute-done.11.refs_18_), channel_id=1, source_target_pairs={{0,1},{1,0},{2,3},{3,2},{4,5},{5,4},{6,7},{7,6},{8,9},{9,8},{10,11... | collective-permute-start | bytes 2113544 | tf_op jit(solution)/shard_map/ppermute | solution.py:633
  71.2 18.1 %collective-permute-start.18 = (bf16[2,1376,128]{2,1,0:T(8,128)(2,1)S(1)}, bf16[2,1376,128]{2,1,0:T(8,128)(2,1)}, u32[]{:S(2)}, u32[]{:S(2)}) collective-permute-start(bf16[2,1376,128]{2,1,0:T(8,128)(2,1)S(1)} %pad_maximum_fusion.2), channel_id=1, source_target_pairs={{0,2},{1,3},{2,0},{3,1},{4,6},{5,7},{6,4},{7,5},{8,10},{9,11},{10,... | collective-permute-start | bytes 2113544 | tf_op jit(solution)/shard_map/ppermute | solution.py:633
  71.8 17.5 %collective-permute-start.21 = (bf16[2,1376,128]{2,1,0:T(8,128)(2,1)}, bf16[2,1376,128]{2,1,0:T(8,128)(2,1)}, u32[]{:S(2)}, u32[]{:S(2)}) collective-permute-start(bf16[2,1376,128]{2,1,0:T(8,128)(2,1)} %collective-permute-done.12.refs_20_), channel_id=1, source_target_pairs={{0,1},{1,0},{2,3},{3,2},{4,5},{5,4},{6,7},{7,6},{8,9},{9,8},{10,11... | collective-permute-start | bytes 2113544 | tf_op jit(solution)/shard_map/ppermute | solution.py:633
  71.9 10.8 %collective-permute-start.17 = (bf16[1,1376,128]{2,1,0:T(8,128)(2,1)S(1)}, bf16[1,1376,128]{2,1,0:T(8,128)(2,1)S(1)}, u32[]{:S(2)}, u32[]{:S(2)}) collective-permute-start(bf16[1,1376,128]{2,1,0:T(8,128)(2,1)S(1)} %slice.122), channel_id=1, source_target_pairs={{8,0},{16,8},{24,16},{28,24},{20,28},{12,20},{4,12},{0,4},{9,1},{1... | collective-permute-start | bytes 1056776 | tf_op jit(solution)/shard_map/ppermute | solution.py:684
  141.1 6.0 %collective-permute-start.27 = (bf16[2,2,1344,128]{3,2,1,0:T(8,128)(2,1)}, bf16[2,2,1344,128]{3,2,1,0:T(8,128)(2,1)S(1)}, u32[]{:S(2)}, u32[]{:S(2)}) collective-permute-start(bf16[2,2,1344,128]{3,2,1,0:T(8,128)(2,1)} %get-tuple-element.176), channel_id=1, source_target_pairs={{0,1},{1,0},{2,3},{3,2},{4,5},{5,4},{6,7},{7,6},{8,9},{9,8},{10,11... | collective-permute-start | bytes 4128776 | tf_op jit(solution)/shard_map/ppermute | solution.py:633
  147.1 16.1 %collective-permute-start.32 = (bf16[5,2,1344,128]{3,2,1,0:T(8,128)(2,1)S(1)}, bf16[5,2,1344,128]{3,2,1,0:T(8,128)(2,1)S(1)}, u32[]{:S(2)}, u32[]{:S(2)}) collective-permute-start(bf16[5,2,1344,128]{3,2,1,0:T(8,128)(2,1)S(1)} %copy-done.36), channel_id=1, source_target_pairs={{0,1},{1,0},{2,3},{3,2},{4,5},{5,4},{6,7},{7,6},{8,9},{9,8},{10,11... | collective-permute-start | bytes 10321928 | tf_op jit(solution)/shard_map/ppermute | solution.py:633
  147.3 8.4 %collective-permute-start.33 = (bf16[5,2,672,128]{3,2,1,0:T(8,128)(2,1)}, bf16[5,2,672,128]{3,2,1,0:T(8,128)(2,1)S(1)}, u32[]{:S(2)}, u32[]{:S(2)}) collective-permute-start(bf16[5,2,672,128]{3,2,1,0:T(8,128)(2,1)} %get-tuple-element.186), channel_id=1, source_target_pairs={{0,1},{1,0},{2,3},{3,2},{4,5},{5,4},{6,7},{7,6},{8,9},{9,8},{10,11... | collective-permute-start | bytes 5160968 | tf_op jit(solution)/shard_map/ppermute | solution.py:633
  147.7 10.2 %collective-permute-start.29 = (bf16[1,1344,128]{2,1,0:T(8,128)(2,1)S(1)}, bf16[1,1344,128]{2,1,0:T(8,128)(2,1)S(1)}, u32[]{:S(2)}, u32[]{:S(2)}) collective-permute-start(bf16[1,1344,128]{2,1,0:T(8,128)(2,1)S(1)} %get-tuple-element.276), channel_id=1, source_target_pairs={{0,8},{8,16},{16,24},{24,28},{28,20},{20,12},{12,4},{4,0},{1,9},{9... | collective-permute-start | bytes 1032200 | tf_op jit(solution)/shard_map/ppermute | solution.py:681
  149.4 9.8 %collective-permute-start.30 = (bf16[1,1344,128]{2,1,0:T(8,128)(2,1)S(1)}, bf16[1,1344,128]{2,1,0:T(8,128)(2,1)S(1)}, u32[]{:S(2)}, u32[]{:S(2)}) collective-permute-start(bf16[1,1344,128]{2,1,0:T(8,128)(2,1)S(1)} %get-tuple-element.275), channel_id=1, source_target_pairs={{8,0},{16,8},{24,16},{28,24},{20,28},{12,20},{4,12},{0,4},{9,1},{1... | collective-permute-start | bytes 1032200 | tf_op jit(solution)/shard_map/ppermute | solution.py:684
  149.9 13.3 %collective-permute-start.31 = (bf16[3,672,128]{2,1,0:T(8,128)(2,1)S(1)}, bf16[3,672,128]{2,1,0:T(8,128)(2,1)S(1)}, u32[]{:S(2)}, u32[]{:S(2)}) collective-permute-start(bf16[3,672,128]{2,1,0:T(8,128)(2,1)S(1)} %slice_bitcast_fusion.1), channel_id=1, source_target_pairs={{0,2},{1,3},{2,0},{3,1},{4,6},{5,7},{6,4},{7,5},{8,10},{9,11},{10,... | collective-permute-start | bytes 1548296 | tf_op jit(solution)/shard_map/ppermute | solution.py:633
  163.2 8.7 %collective-permute-start.38 = (bf16[2,672,128]{2,1,0:T(8,128)(2,1)S(1)}, bf16[2,672,128]{2,1,0:T(8,128)(2,1)S(1)}, u32[]{:S(2)}, u32[]{:S(2)}) collective-permute-start(bf16[2,672,128]{2,1,0:T(8,128)(2,1)S(1)} %slice_bitcast_fusion.2), channel_id=1, source_target_pairs={{0,2},{1,3},{2,0},{3,1},{4,6},{5,7},{6,4},{7,5},{8,10},{9,11},{10,... | collective-permute-start | bytes 1032200 | tf_op jit(solution)/shard_map/ppermute | solution.py:633
  163.8 9.8 %collective-permute-start.36 = (bf16[336,128]{1,0:T(8,128)(2,1)S(1)}, bf16[336,128]{1,0:T(8,128)(2,1)S(1)}, u32[]{:S(2)}, u32[]{:S(2)}) collective-permute-start(bf16[336,128]{1,0:T(8,128)(2,1)S(1)} %get-tuple-element.272), channel_id=1, source_target_pairs={{0,8},{8,16},{16,24},{24,28},{28,20},{20,12},{12,4},{4,0},{1,9},{9... | collective-permute-start | bytes 258056 | tf_op jit(solution)/shard_map/ppermute | solution.py:681
  165.5 8.2 %collective-permute-start.37 = (bf16[336,128]{1,0:T(8,128)(2,1)S(1)}, bf16[336,128]{1,0:T(8,128)(2,1)S(1)}, u32[]{:S(2)}, u32[]{:S(2)}) collective-permute-start(bf16[336,128]{1,0:T(8,128)(2,1)S(1)} %get-tuple-element.271), channel_id=1, source_target_pairs={{8,0},{16,8},{24,16},{28,24},{20,28},{12,20},{4,12},{0,4},{9,1},{1... | collective-permute-start | bytes 258056 | tf_op jit(solution)/shard_map/ppermute | solution.py:684
  166.1 16.2 %collective-permute-start.34 = (bf16[2,1344,128]{2,1,0:T(8,128)(2,1)S(1)}, bf16[2,1344,128]{2,1,0:T(8,128)(2,1)S(1)}, u32[]{:S(2)}, u32[]{:S(2)}) collective-permute-start(bf16[2,1344,128]{2,1,0:T(8,128)(2,1)S(1)} %get-tuple-element.274), channel_id=1, source_target_pairs={{0,8},{8,16},{16,24},{24,28},{28,20},{20,12},{12,4},{4,0},{1,9},{9... | collective-permute-start | bytes 2064392 | tf_op jit(solution)/shard_map/ppermute | solution.py:681
  167.7 15.9 %collective-permute-start.35 = (bf16[2,1344,128]{2,1,0:T(8,128)(2,1)S(1)}, bf16[2,1344,128]{2,1,0:T(8,128)(2,1)S(1)}, u32[]{:S(2)}, u32[]{:S(2)}) collective-permute-start(bf16[2,1344,128]{2,1,0:T(8,128)(2,1)S(1)} %get-tuple-element.273), channel_id=1, source_target_pairs={{8,0},{16,8},{24,16},{28,24},{20,28},{12,20},{4,12},{0,4},{9,1},{1... | collective-permute-start | bytes 2064392 | tf_op jit(solution)/shard_map/ppermute | solution.py:684
  184.4 11.6 %collective-permute-start.44 = (bf16[3,672,128]{2,1,0:T(8,128)(2,1)}, bf16[3,672,128]{2,1,0:T(8,128)(2,1)}, u32[]{:S(2)}, u32[]{:S(2)}) collective-permute-start(bf16[3,672,128]{2,1,0:T(8,128)(2,1)} %slice_bitcast_fusion), channel_id=1, source_target_pairs={{0,2},{1,3},{2,0},{3,1},{4,6},{5,7},{6,4},{7,5},{8,10},{9,11},{10,... | collective-permute-start | bytes 1548296 | tf_op jit(solution)/shard_map/ppermute | solution.py:633
  187.3 20.0 %collective-permute-start.40 = (bf16[2,1344,128]{2,1,0:T(8,128)(2,1)}, bf16[2,1344,128]{2,1,0:T(8,128)(2,1)}, u32[]{:S(2)}, u32[]{:S(2)}) collective-permute-start(bf16[2,1344,128]{2,1,0:T(8,128)(2,1)} %get-tuple-element.264), channel_id=1, source_target_pairs={{0,8},{8,16},{16,24},{24,28},{28,20},{20,12},{12,4},{4,0},{1,9},{9... | collective-permute-start | bytes 2064392 | tf_op jit(solution)/shard_map/ppermute | solution.py:681
  188.9 18.5 %collective-permute-start.41 = (bf16[2,1344,128]{2,1,0:T(8,128)(2,1)}, bf16[2,1344,128]{2,1,0:T(8,128)(2,1)}, u32[]{:S(2)}, u32[]{:S(2)}) collective-permute-start(bf16[2,1344,128]{2,1,0:T(8,128)(2,1)} %get-tuple-element.263), channel_id=1, source_target_pairs={{8,0},{16,8},{24,16},{28,24},{20,28},{12,20},{4,12},{0,4},{9,1},{1... | collective-permute-start | bytes 2064392 | tf_op jit(solution)/shard_map/ppermute | solution.py:684
  190.2 16.4 %collective-permute-start.42 = (bf16[672,128]{1,0:T(8,128)(2,1)}, bf16[672,128]{1,0:T(8,128)(2,1)}, u32[]{:S(2)}, u32[]{:S(2)}) collective-permute-start(bf16[672,128]{1,0:T(8,128)(2,1)} %get-tuple-element.270), channel_id=1, source_target_pairs={{0,8},{8,16},{16,24},{24,28},{28,20},{20,12},{12,4},{4,0},{1,9},{9... | collective-permute-start | bytes 516104 | tf_op jit(solution)/shard_map/ppermute | solution.py:681
  191.7 15.6 %collective-permute-start.43 = (bf16[672,128]{1,0:T(8,128)(2,1)}, bf16[672,128]{1,0:T(8,128)(2,1)}, u32[]{:S(2)}, u32[]{:S(2)}) collective-permute-start(bf16[672,128]{1,0:T(8,128)(2,1)} %get-tuple-element.269), channel_id=1, source_target_pairs={{8,0},{16,8},{24,16},{28,24},{20,28},{12,20},{4,12},{0,4},{9,1},{1... | collective-permute-start | bytes 516104 | tf_op jit(solution)/shard_map/ppermute | solution.py:684
  196.1 11.2 %collective-permute-start.45 = (f32[4,24,96]{2,1,0:T(8,128)S(1)}, f32[4,24,96]{2,1,0:T(8,128)S(1)}, u32[]{:S(2)}, u32[]{:S(2)}) collective-permute-start(f32[4,24,96]{2,1,0:T(8,128)S(1)} %get-tuple-element.279), channel_id=1, source_target_pairs={{0,4},{1,5},{2,6},{3,7},{4,0},{5,1},{6,2},{7,3},{8,12},{9,13},{10,... | collective-permute-start | bytes 110600 | tf_op jit(solution)/shard_map/ppermute | solution.py:638
  209.1 18.3 %collective-permute-start.46 = (bf16[2,1344,128]{2,1,0:T(8,128)(2,1)S(1)}, bf16[2,1344,128]{2,1,0:T(8,128)(2,1)S(1)}, u32[]{:S(2)}, u32[]{:S(2)}) collective-permute-start(bf16[2,1344,128]{2,1,0:T(8,128)(2,1)S(1)} %get-tuple-element.262), channel_id=1, source_target_pairs={{0,8},{8,16},{16,24},{24,28},{28,20},{20,12},{12,4},{4,0},{1,9},{9... | collective-permute-start | bytes 2064392 | tf_op jit(solution)/shard_map/ppermute | solution.py:681
  209.9 17.6 %collective-permute-start.47 = (bf16[2,1344,128]{2,1,0:T(8,128)(2,1)S(1)}, bf16[2,1344,128]{2,1,0:T(8,128)(2,1)S(1)}, u32[]{:S(2)}, u32[]{:S(2)}) collective-permute-start(bf16[2,1344,128]{2,1,0:T(8,128)(2,1)S(1)} %get-tuple-element.261), channel_id=1, source_target_pairs={{8,0},{16,8},{24,16},{28,24},{20,28},{12,20},{4,12},{0,4},{9,1},{1... | collective-permute-start | bytes 2064392 | tf_op jit(solution)/shard_map/ppermute | solution.py:684
  212.4 15.1 %collective-permute-start.48 = (bf16[672,128]{1,0:T(8,128)(2,1)S(1)}, bf16[672,128]{1,0:T(8,128)(2,1)S(1)}, u32[]{:S(2)}, u32[]{:S(2)}) collective-permute-start(bf16[672,128]{1,0:T(8,128)(2,1)S(1)} %get-tuple-element.268), channel_id=1, source_target_pairs={{0,8},{8,16},{16,24},{24,28},{28,20},{20,12},{12,4},{4,0},{1,9},{9... | collective-permute-start | bytes 516104 | tf_op jit(solution)/shard_map/ppermute | solution.py:681
  213.1 14.4 %collective-permute-start.49 = (bf16[672,128]{1,0:T(8,128)(2,1)S(1)}, bf16[672,128]{1,0:T(8,128)(2,1)S(1)}, u32[]{:S(2)}, u32[]{:S(2)}) collective-permute-start(bf16[672,128]{1,0:T(8,128)(2,1)S(1)} %get-tuple-element.267), channel_id=1, source_target_pairs={{8,0},{16,8},{24,16},{28,24},{20,28},{12,20},{4,12},{0,4},{9,1},{1... | collective-permute-start | bytes 516104 | tf_op jit(solution)/shard_map/ppermute | solution.py:684
  214.5 13.0 %collective-permute-start.50 = (f32[2,24,96]{2,1,0:T(8,128)S(1)}, f32[2,24,96]{2,1,0:T(8,128)S(1)}, u32[]{:S(2)}, u32[]{:S(2)}) collective-permute-start(f32[2,24,96]{2,1,0:T(8,128)S(1)} %get-tuple-element.281), channel_id=1, source_target_pairs={{0,8},{1,9},{2,10},{3,11},{4,12},{5,13},{6,14},{7,15},{8,0},{9,1},... | collective-permute-start | bytes 55304 | tf_op jit(solution)/shard_map/ppermute | solution.py:638
  227.8 12.6 %collective-permute-start.51 = (bf16[2,1344,128]{2,1,0:T(8,128)(2,1)S(1)}, bf16[2,1344,128]{2,1,0:T(8,128)(2,1)S(1)}, u32[]{:S(2)}, u32[]{:S(2)}) collective-permute-start(bf16[2,1344,128]{2,1,0:T(8,128)(2,1)S(1)} %fusion.3), channel_id=1, source_target_pairs={{0,2},{1,3},{2,0},{3,1},{4,6},{5,7},{6,4},{7,5},{8,10},{9,11},{10,... | collective-permute-start | bytes 2064392 | tf_op jit(solution)/shard_map/ppermute | solution.py:633
  229.5 7.5 %collective-permute-start.52 = (bf16[672,128]{1,0:T(8,128)(2,1)S(1)}, bf16[672,128]{1,0:T(8,128)(2,1)S(1)}, u32[]{:S(2)}, u32[]{:S(2)}) collective-permute-start(bf16[672,128]{1,0:T(8,128)(2,1)S(1)} %get-tuple-element.266), channel_id=1, source_target_pairs={{0,8},{8,16},{16,24},{24,28},{28,20},{20,12},{12,4},{4,0},{1,9},{9... | collective-permute-start | bytes 516104 | tf_op jit(solution)/shard_map/ppermute | solution.py:681
  229.9 7.2 %collective-permute-start.53 = (bf16[672,128]{1,0:T(8,128)(2,1)S(1)}, bf16[672,128]{1,0:T(8,128)(2,1)S(1)}, u32[]{:S(2)}, u32[]{:S(2)}) collective-permute-start(bf16[672,128]{1,0:T(8,128)(2,1)S(1)} %get-tuple-element.265), channel_id=1, source_target_pairs={{8,0},{16,8},{24,16},{28,24},{20,28},{12,20},{4,12},{0,4},{9,1},{1... | collective-permute-start | bytes 516104 | tf_op jit(solution)/shard_map/ppermute | solution.py:684
  231.6 5.4 %collective-permute-start.54 = (f32[24,96]{1,0:T(8,128)S(1)}, f32[24,96]{1,0:T(8,128)S(1)}, u32[]{:S(2)}, u32[]{:S(2)}) collective-permute-start(f32[24,96]{1,0:T(8,128)S(1)} %get-tuple-element.283), channel_id=1, source_target_pairs={{0,16},{1,17},{2,18},{3,19},{4,20},{5,21},{6,22},{7,23},{8,24},{9,... | collective-permute-start | bytes 27656 | tf_op jit(solution)/shard_map/ppermute | solution.py:638
  242.3 6.8 %collective-permute-start.56 = (bf16[2,1344,128]{2,1,0:T(8,128)(2,1)S(1)}, bf16[2,1344,128]{2,1,0:T(8,128)(2,1)S(1)}, u32[]{:S(2)}, u32[]{:S(2)}) collective-permute-start(bf16[2,1344,128]{2,1,0:T(8,128)(2,1)S(1)} %get-tuple-element.236.own), channel_id=1, source_target_pairs={{0,1},{1,0},{2,3},{3,2},{4,5},{5,4},{6,7},{7,6},{8,9},{9,8},{10,11... | collective-permute-start | bytes 2064392 | tf_op jit(solution)/shard_map/ppermute | solution.py:633
  242.3 6.8 %collective-permute-start.55 = (bf16[672,128]{1,0:T(8,128)(2,1)S(1)}, bf16[672,128]{1,0:T(8,128)(2,1)S(1)}, u32[]{:S(2)}, u32[]{:S(2)}) collective-permute-start(bf16[672,128]{1,0:T(8,128)(2,1)S(1)} %fusion.19), channel_id=1, source_target_pairs={{0,2},{1,3},{2,0},{3,1},{4,6},{5,7},{6,4},{7,5},{8,10},{9,11},{10,... | collective-permute-start | bytes 516104 | tf_op jit(solution)/shard_map/ppermute | solution.py:633
  252.6 10.5 %collective-permute-start.63 = (bf16[1344,128]{1,0:T(8,128)(2,1)S(1)}, bf16[1344,128]{1,0:T(8,128)(2,1)S(1)}, u32[]{:S(2)}, u32[]{:S(2)}) collective-permute-start(bf16[1344,128]{1,0:T(8,128)(2,1)S(1)} %get-tuple-element.256.split_own), channel_id=1, source_target_pairs={{0,1},{1,0},{2,3},{3,2},{4,5},{5,4},{6,7},{7,6},{8,9},{9,8},{10,11... | collective-permute-start | bytes 1032200 | tf_op jit(solution)/shard_map/ppermute | solution.py:633
  (54 other events, 335.3 us)

commit v4 on v3

--- a/solution.py
+++ b/solution.py
@@ -30,7 +30,7 @@
 ROW_P, ROW_QKV, ROW_O, ROW_ONE, ROW_TWO, ROW_H, ROWS = 0, 96, 384, 480, 864, 1248, 1344
 VEC_ROWS = 32
 PLACES = ((4,), (3, 5), (2, 6, 1, 7, 0))
-SPLIT_PLACES = ((4, 3, 5), (2, 6, 1, 7, 0))
+SPLIT_PLACES = ((4, 3), (5, 2, 6, 1, 7, 0))
 OUTS = 2 * len(PLACES) + 2 * len(SPLIT_PLACES)
 PART, CUT, BLOCK = 8, 24, 48
 
@@ -815,7 +815,7 @@
             split_sends[1],
         )
         small = small + small_more
-        whole, split = {}, dict(zip((4, 3, 5), split_first[:, 0]))
+        whole, split = {}, dict(zip((4, 3), split_first[:, 0]))
         left, right, pair_first, whole_next, got_rest, split_rest, small = tick(
             ahead(opposite[0, :1]),
             behind(opposite[0, 1:]),
@@ -826,9 +826,9 @@
             small,
         )
         whole.update(zip((3, 5), whole_next))
-        split.update(zip((2, 6, 1, 7, 0), split_rest[:, 0]))
-        pair = dict(zip((4, 3, 5), pair_first))
-        pair_next, small = tick(trade(split_rest[:2, 1]), small)
+        split.update(zip((5, 2, 6, 1, 7, 0), split_rest[:, 0]))
+        pair = dict(zip((4, 3), pair_first))
+        pair_next, small = tick(trade(split_rest[:3, 1]), small)
         left, right, split_left, split_right, pair_next, whole_rest, split_rest, small, small_more = tick(
             ahead(rounded(whole[3], low_half(left))),
             behind(rounded(whole[5], high_half(right))),
@@ -840,10 +840,10 @@
             small,
             trade(small),
         )
-        pair.update(zip((2, 6), pair_next))
+        pair.update(zip((5, 2, 6), pair_next))
         whole.update(zip((2, 6, 1, 7, 0), whole_rest))
         small = jnp.take(small + small_more, group ^ jnp.array([0, 4, 2, 6, 1, 5, 3, 7]), axis=0)
-        pair_rest, small = tick(trade(split_rest[2:, 1]), small)
+        pair_rest, small = tick(trade(split_rest[3:, 1]), small)
         left, right, split_left, split_right, pair_rest, small, small_more = tick(
             ahead(rounded(whole[2], left)),
             behind(rounded(whole[6], right)),

time: 275 us -> 273 us (level)
  waiting for transfers between devices: 128 us -> 125 us
    ppermute x12, waiting for transfers between devices: 19.5 us -> 16.2 us  [ahead(): return lax.ppermute(value, 'dp', forward)]
    convert_element_type x14 -> x15, other arithmetic: 11.6 us -> 12.3 us  [rounded(): return sum((value.astype(f32) for value in values)).astype(bf16)]
  transfers between devices with their start and end apart: 64 -> 64, of which waited for: 32 -> 32; matrix products, arithmetic and copies ran while one was open for 7% -> 8% of each run, Pallas kernels for 1% -> 1%
where the time goes in v4:
time: 273 us; the launch traced here: 272 us
  waiting for transfers between devices  125 us (46%)
  Pallas kernels  62.9 us (23%)
  starting transfers between devices  48.5 us (18%)
  other arithmetic  22.1 us (8%)
  local copies, waits for them, and re-layouts  10.3 us (4%)
  between operations  3.44 us (1%)
    ppermute x31, waiting for transfers between devices, seq_flip(): return lax.ppermute(value, 'seq', [(i, i ^ k) for i in range(n_seq)])  73.8 us
    pallas_call x1, Pallas kernels, run_step(): pl.pallas_call(partial(step_kernel, pieces, vec_pieces, (len(parcels), le...  46.4 us
    ppermute x9, waiting for transfers between devices, hop(): return lax.ppermute(value, ('dp', 'seq'), pairs)  22.1 us
    ppermute x12, starting transfers between devices, ahead(): return lax.ppermute(value, 'dp', forward)  17.5 us
    ppermute x12, waiting for transfers between devices, ahead(): return lax.ppermute(value, 'dp', forward)  16.2 us
    ppermute x31, starting transfers between devices, seq_flip(): return lax.ppermute(value, 'seq', [(i, i ^ k) for i in range(n_seq)])  13 us
    ppermute x12, waiting for transfers between devices, behind(): return lax.ppermute(value, 'dp', backward)  12.7 us
    convert_element_type x15, other arithmetic, rounded(): return sum((value.astype(f32) for value in values)).astype(bf16)  12.3 us
  transfers between devices with their start and end apart: 64, of which 32 were waited for; matrix products, arithmetic and copies ran while one was open for 8% of the time, Pallas kernels for 1%

profile of v4, /device:TPU:0, one launch (start us, length us, event | category | flops | bytes accessed | tf_op | source)
XLA Modules:
  0.0 272.2 jit_solution(6959549979536552568)
XLA Ops:
  1.4 4.2 %pack.1 = (bf16[6,1344,128]{2,1,0:T(8,128)(2,1)}, bf16[2,1376,128]{2,1,0:T(8,128)(2,1)}, bf16[2,1376,128]{2,1,0:T(8,128)(2,1)}) custom-call(s32[4]{0:T(128)} %pad_add_fusion.2.chosen, f32[3,96,768]{2,1,0:T(8,128)} %refs_0_.1, f32[96,2304]{1,0:T(8,128)} %refs_1_.1, f32[96,3072]{1,0:T(8,128)} %refs_2_.1, f32[384,768]{1,0:T(8,128)} %refs_3_.1, f32[20,96]{1,0:T(8,128)} %refs_4_.1), custom_call_target="tpu_custom_call" | custom-call | tf_op jit(solution)/shard_map/pack/pallas_call | solution.py:480
  5.5 3.1 %collective-permute-start = (bf16[2,1376,128]{2,1,0:T(8,128)(2,1)}, bf16[2,1376,128]{2,1,0:T(8,128)(2,1)S(1)}, u32[]{:S(2)}, u32[]{:S(2)}) collective-permute-start(bf16[2,1376,128]{2,1,0:T(8,128)(2,1)} %get-tuple-element.136.refs_7_), channel_id=1, source_target_pairs={{0,8},{8,16},{16,24},{24,28},{28,20},{20,12},{12,4},{4,0},{1,9},{9... | collective-permute-start | bytes 2113544 | tf_op jit(solution)/shard_map/ppermute | solution.py:681
  9.1 2.1 parcels.1
  11.2 1.9 collective-permute-start.3
  13.3 6.5 %collective-permute-done.3.refs_4_ = bf16[144,768]{1,0:T(8,128)(2,1)S(1)} collective-permute-done((bf16[144,768]{1,0:T(8,128)(2,1)}, bf16[144,768]{1,0:T(8,128)(2,1)S(1)}, u32[]{:S(2)}, u32[]{:S(2)}) %collective-permute-start.3) | collective-permute-done | bytes 221216 | tf_op jit(solution)/shard_map/ppermute | solution.py:633
  19.7 4.2 %collective-permute-done.4.refs_5_ = bf16[144,768]{1,0:T(8,128)(2,1)S(1)} collective-permute-done((bf16[144,768]{1,0:T(8,128)(2,1)}, bf16[144,768]{1,0:T(8,128)(2,1)S(1)}, u32[]{:S(2)}, u32[]{:S(2)}) %collective-permute-start.4) | collective-permute-done | bytes 221216 | tf_op jit(solution)/shard_map/ppermute | solution.py:633
  24.6 1.4 collective-permute-done.1.refs_9_
  26.2 1.6 collective-permute-start.7
  27.7 1.6 collective-permute-start.5
  30.3 3.8 %fusion.8.refs_1_ = f32[256,768]{1,0:T(8,128)} fusion(f32[768]{0:T(1024)S(1)} %fusion.31, f32[256]{0:T(256)S(1)} %iota_convert_fusion, pred[768]{0:T(1024)(128)(4,1)S(1)} %fusion.26), kind=kLoop, calls=%fused_computation.26 | loop fusion | flops 393216 | bytes 791296 | tf_op jit(solution)/shard_map/jit(_where)/select_n | solution.py:629
  34.1 8.8 %collective-permute-done.7.refs_14_ = bf16[2,1376,128]{2,1,0:T(8,128)(2,1)S(1)} collective-permute-done((bf16[2,1376,128]{2,1,0:T(8,128)(2,1)S(1)}, bf16[2,1376,128]{2,1,0:T(8,128)(2,1)S(1)}, u32[]{:S(2)}, u32[]{:S(2)}) %collective-permute-start.7) | collective-permute-done | bytes 704544 | tf_op jit(solution)/shard_map/ppermute | solution.py:633
  42.9 1.5 collective-permute-done.5.refs_12_
  47.5 1.6 collective-permute-start.10
  50.6 17.5 %collective-permute-done.12.refs_20_ = bf16[2,1376,128]{2,1,0:T(8,128)(2,1)} collective-permute-done((bf16[2,1376,128]{2,1,0:T(8,128)(2,1)S(1)}, bf16[2,1376,128]{2,1,0:T(8,128)(2,1)}, u32[]{:S(2)}, u32[]{:S(2)}) %collective-permute-start.12) | collective-permute-done | bytes 704544 | tf_op jit(solution)/shard_map/ppermute | solution.py:633
  69.1 1.6 collective-permute-start.16
  75.3 7.4 %collective-permute-done.17.refs_26_ = bf16[1,1376,128]{2,1,0:T(8,128)(2,1)S(1)} collective-permute-done((bf16[1,1376,128]{2,1,0:T(8,128)(2,1)S(1)}, bf16[1,1376,128]{2,1,0:T(8,128)(2,1)S(1)}, u32[]{:S(2)}, u32[]{:S(2)}) %collective-permute-start.17) | collective-permute-done | bytes 352288 | tf_op jit(solution)/shard_map/ppermute | solution.py:684
  82.7 6.6 %collective-permute-done.18.refs_24_ = bf16[2,1376,128]{2,1,0:T(8,128)(2,1)} collective-permute-done((bf16[2,1376,128]{2,1,0:T(8,128)(2,1)S(1)}, bf16[2,1376,128]{2,1,0:T(8,128)(2,1)}, u32[]{:S(2)}, u32[]{:S(2)}) %collective-permute-start.18) | collective-permute-done | bytes 704544 | tf_op jit(solution)/shard_map/ppermute | solution.py:633
  90.0 3.3 %collective-permute-done.23.refs_28_ = bf16[1,1376,128]{2,1,0:T(8,128)(2,1)S(1)} collective-permute-done((bf16[1,1376,128]{2,1,0:T(8,128)(2,1)S(1)}, bf16[1,1376,128]{2,1,0:T(8,128)(2,1)S(1)}, u32[]{:S(2)}, u32[]{:S(2)}) %collective-permute-start.23) | collective-permute-done | bytes 352288 | tf_op jit(solution)/shard_map/ppermute | solution.py:633
  94.5 46.4 %step.1 = (bf16[1,2,1344,128]{3,2,1,0:T(8,128)(2,1)}, bf16[1,2,1344,128]{3,2,1,0:T(8,128)(2,1)}, bf16[2,2,1344,128]{3,2,1,0:T(8,128)(2,1)}, bf16[2,2,1344,128]{3...) custom-call(s32[56]{0:T(128)} %concatenate.20.refs_0_, ...), custom_call_target="tpu_custom_call" | custom-call | tf_op jit(solution)/shard_map/step/pallas_call | solution.py:410
  143.3 1.4 add_convert_fusion.5
  144.7 1.5 collective-permute-done.26
  147.1 1.6 collective-permute-start.29
  150.2 5.3 %collective-permute-done.33 = bf16[6,2,672,128]{3,2,1,0:T(8,128)(2,1)S(1)} collective-permute-done((bf16[6,2,672,128]{3,2,1,0:T(8,128)(2,1)}, bf16[6,2,672,128]{3,2,1,0:T(8,128)(2,1)S(1)}, u32[]{:S(2)}, u32[]{:S(2)}) %collective-permute-start.33) | collective-permute-done | bytes 2064416 | tf_op jit(solution)/shard_map/ppermute | solution.py:633
  159.5 1.6 collective-permute-start.36
  161.8 1.6 collective-permute-start.34
  163.9 7.5 %collective-permute-done.38 = bf16[3,672,128]{2,1,0:T(8,128)(2,1)S(1)} collective-permute-done((bf16[3,672,128]{2,1,0:T(8,128)(2,1)S(1)}, bf16[3,672,128]{2,1,0:T(8,128)(2,1)S(1)}, u32[]{:S(2)}, u32[]{:S(2)}) %collective-permute-start.38) | collective-permute-done | bytes 516128 | tf_op jit(solution)/shard_map/ppermute | solution.py:633
  172.8 3.1 %collective-permute-done.39 = f32[8,24,96]{2,1,0:T(8,128)S(1)} collective-permute-done((f32[8,24,96]{2,1,0:T(8,128)S(1)}, f32[8,24,96]{2,1,0:T(8,128)S(1)}, u32[]{:S(2)}, u32[]{:S(2)}) %collective-permute-start.39) | collective-permute-done | bytes 73760 | tf_op jit(solution)/shard_map/ppermute | solution.py:633
  176.0 2.0 collective-permute-done.34
  180.1 1.5 collective-permute-start.44
  182.8 1.4 fusion.4
  184.3 1.6 collective-permute-start.40
  187.0 1.6 collective-permute-start.42
  189.2 1.4 gather_fusion.1
  192.3 10.9 %collective-permute-done.42 = bf16[672,128]{1,0:T(8,128)(2,1)} collective-permute-done((bf16[672,128]{1,0:T(8,128)(2,1)}, bf16[672,128]{1,0:T(8,128)(2,1)}, u32[]{:S(2)}, u32[]{:S(2)}) %collective-permute-start.42) | collective-permute-done | bytes 172064 | tf_op jit(solution)/shard_map/ppermute | solution.py:681
  203.7 1.7 fusion
  206.1 1.4 collective-permute-start.47
  209.5 1.4 collective-permute-start.49
  211.6 12.7 %collective-permute-done.50 = f32[2,24,96]{2,1,0:T(8,128)S(1)} collective-permute-done((f32[2,24,96]{2,1,0:T(8,128)S(1)}, f32[2,24,96]{2,1,0:T(8,128)S(1)}, u32[]{:S(2)}, u32[]{:S(2)}) %collective-permute-start.50) | collective-permute-done | bytes 18464 | tf_op jit(solution)/shard_map/ppermute | solution.py:638
  226.8 1.7 collective-permute-start.53
  228.6 2.1 collective-permute-start.54
  230.6 3.6 %collective-permute-done.54 = f32[24,96]{1,0:T(8,128)S(1)} collective-permute-done((f32[24,96]{1,0:T(8,128)S(1)}, f32[24,96]{1,0:T(8,128)S(1)}, u32[]{:S(2)}, u32[]{:S(2)}) %collective-permute-start.54) | collective-permute-done | bytes 9248 | tf_op jit(solution)/shard_map/ppermute | solution.py:638
  234.2 3.6 %collective-permute-done.51 = bf16[2,1344,128]{2,1,0:T(8,128)(2,1)S(1)} collective-permute-done((bf16[2,1344,128]{2,1,0:T(8,128)(2,1)S(1)}, bf16[2,1344,128]{2,1,0:T(8,128)(2,1)S(1)}, u32[]{:S(2)}, u32[]{:S(2)}) %collective-permute-start.51) | collective-permute-done | bytes 688160 | tf_op jit(solution)/shard_map/ppermute | solution.py:633
  242.3 4.4 %collective-permute-done.55 = bf16[672,128]{1,0:T(8,128)(2,1)S(1)} collective-permute-done((bf16[672,128]{1,0:T(8,128)(2,1)S(1)}, bf16[672,128]{1,0:T(8,128)(2,1)S(1)}, u32[]{:S(2)}, u32[]{:S(2)}) %collective-permute-start.55) | collective-permute-done | bytes 172064 | tf_op jit(solution)/shard_map/ppermute | solution.py:633
  248.3 1.4 collective-permute-start.58
  255.0 2.1 collective-permute-start.62
  257.2 1.4 collective-permute-done.61
  258.6 1.8 collective-permute-done.62
  261.7 10.3 %adam.1 = (f32[1,1]{1,0:T(1,128)}, f32[1,1]{1,0:T(1,128)}, f32[3,96,768]{2,1,0:T(8,128)}, f32[96,2304]{1,0:T(8,128)}, f32[96,3072]{1,0:T(8,128)}, /*index=5*/f32...) custom-call(s32[1]{0:T(128)} %bitcast.core, ...), custom_call_target="tpu_custom_call" | custom-call | tf_op jit(solution)/shard_map/adam/pallas_call | solution.py:608
  (231 shorter events, 49.9 us)
Async XLA Ops:
  5.5 19.0 %collective-permute-start = (bf16[2,1376,128]{2,1,0:T(8,128)(2,1)}, bf16[2,1376,128]{2,1,0:T(8,128)(2,1)S(1)}, u32[]{:S(2)}, u32[]{:S(2)}) collective-permute-start(bf16[2,1376,128]{2,1,0:T(8,128)(2,1)} %get-tuple-element.136.refs_7_), channel_id=1, source_target_pairs={{0,8},{8,16},{16,24},{24,28},{28,20},{20,12},{12,4},{4,0},{1,9},{9... | collective-permute-start | bytes 2113544 | tf_op jit(solution)/shard_map/ppermute | solution.py:681
  8.6 17.5 %collective-permute-start.1 = (bf16[2,1376,128]{2,1,0:T(8,128)(2,1)}, bf16[2,1376,128]{2,1,0:T(8,128)(2,1)S(1)}, u32[]{:S(2)}, u32[]{:S(2)}) collective-permute-start(bf16[2,1376,128]{2,1,0:T(8,128)(2,1)} %get-tuple-element.137), channel_id=1, source_target_pairs={{8,0},{16,8},{24,16},{28,24},{20,28},{12,20},{4,12},{0,4},{9,1},{1... | collective-permute-start | bytes 2113544 | tf_op jit(solution)/shard_map/ppermute | solution.py:684
  11.2 8.5 %collective-permute-start.3 = (bf16[144,768]{1,0:T(8,128)(2,1)}, bf16[144,768]{1,0:T(8,128)(2,1)S(1)}, u32[]{:S(2)}, u32[]{:S(2)}) collective-permute-start(bf16[144,768]{1,0:T(8,128)(2,1)} %get-tuple-element.139), channel_id=1, source_target_pairs={{0,2},{1,3},{2,0},{3,1},{4,6},{5,7},{6,4},{7,5},{8,10},{9,11},{10,... | collective-permute-start | bytes 663560 | tf_op jit(solution)/shard_map/ppermute | solution.py:633
  13.1 10.8 %collective-permute-start.4 = (bf16[144,768]{1,0:T(8,128)(2,1)}, bf16[144,768]{1,0:T(8,128)(2,1)S(1)}, u32[]{:S(2)}, u32[]{:S(2)}) collective-permute-start(bf16[144,768]{1,0:T(8,128)(2,1)} %get-tuple-element.140), channel_id=1, source_target_pairs={{0,3},{1,2},{2,1},{3,0},{4,7},{5,6},{6,5},{7,4},{8,11},{9,10},{10,... | collective-permute-start | bytes 663560 | tf_op jit(solution)/shard_map/ppermute | solution.py:633
  26.2 16.7 %collective-permute-start.7 = (bf16[2,1376,128]{2,1,0:T(8,128)(2,1)S(1)}, bf16[2,1376,128]{2,1,0:T(8,128)(2,1)S(1)}, u32[]{:S(2)}, u32[]{:S(2)}) collective-permute-start(bf16[2,1376,128]{2,1,0:T(8,128)(2,1)S(1)} %pad_maximum_fusion), channel_id=1, source_target_pairs={{0,2},{1,3},{2,0},{3,1},{4,6},{5,7},{6,4},{7,5},{8,10},{9,11},{10,... | collective-permute-start | bytes 2113544 | tf_op jit(solution)/shard_map/ppermute | solution.py:633
  27.7 16.6 %collective-permute-start.5 = (bf16[2,1376,128]{2,1,0:T(8,128)(2,1)S(1)}, bf16[2,1376,128]{2,1,0:T(8,128)(2,1)S(1)}, u32[]{:S(2)}, u32[]{:S(2)}) collective-permute-start(bf16[2,1376,128]{2,1,0:T(8,128)(2,1)S(1)} %collective-permute-done.refs_8_), channel_id=1, source_target_pairs={{0,8},{8,16},{16,24},{24,28},{28,20},{20,12},{12,4},{4,0},{1,9},{9... | collective-permute-start | bytes 2113544 | tf_op jit(solution)/shard_map/ppermute | solution.py:681
  29.3 16.3 %collective-permute-start.6 = (bf16[2,1376,128]{2,1,0:T(8,128)(2,1)S(1)}, bf16[2,1376,128]{2,1,0:T(8,128)(2,1)S(1)}, u32[]{:S(2)}, u32[]{:S(2)}) collective-permute-start(bf16[2,1376,128]{2,1,0:T(8,128)(2,1)S(1)} %collective-permute-done.1.refs_9_), channel_id=1, source_target_pairs={{8,0},{16,8},{24,16},{28,24},{20,28},{12,20},{4,12},{0,4},{9,1},{1... | collective-permute-start | bytes 2113544 | tf_op jit(solution)/shard_map/ppermute | solution.py:684
  29.8 15.9 %collective-permute-start.8 = (bf16[2,1376,128]{2,1,0:T(8,128)(2,1)S(1)}, bf16[2,1376,128]{2,1,0:T(8,128)(2,1)S(1)}, u32[]{:S(2)}, u32[]{:S(2)}) collective-permute-start(bf16[2,1376,128]{2,1,0:T(8,128)(2,1)S(1)} %collective-permute-done.refs_8_), channel_id=1, source_target_pairs={{0,1},{1,0},{2,3},{3,2},{4,5},{5,4},{6,7},{7,6},{8,9},{9,8},{10,11... | collective-permute-start | bytes 2113544 | tf_op jit(solution)/shard_map/ppermute | solution.py:633
  29.8 15.9 %collective-permute-start.9 = (bf16[2,1376,128]{2,1,0:T(8,128)(2,1)S(1)}, bf16[2,1376,128]{2,1,0:T(8,128)(2,1)S(1)}, u32[]{:S(2)}, u32[]{:S(2)}) collective-permute-start(bf16[2,1376,128]{2,1,0:T(8,128)(2,1)S(1)} %collective-permute-done.1.refs_9_), channel_id=1, source_target_pairs={{0,1},{1,0},{2,3},{3,2},{4,5},{5,4},{6,7},{7,6},{8,9},{9,8},{10,11... | collective-permute-start | bytes 2113544 | tf_op jit(solution)/shard_map/ppermute | solution.py:633
  47.5 20.6 %collective-permute-start.10 = (bf16[2,1376,128]{2,1,0:T(8,128)(2,1)S(1)}, bf16[2,1376,128]{2,1,0:T(8,128)(2,1)S(1)}, u32[]{:S(2)}, u32[]{:S(2)}) collective-permute-start(bf16[2,1376,128]{2,1,0:T(8,128)(2,1)S(1)} %collective-permute-done.5.refs_12_), channel_id=1, source_target_pairs={{0,8},{8,16},{16,24},{24,28},{28,20},{20,12},{12,4},{4,0},{1,9},{9... | collective-permute-start | bytes 2113544 | tf_op jit(solution)/shard_map/ppermute | solution.py:681
  49.1 19.0 %collective-permute-start.11 = (bf16[2,1376,128]{2,1,0:T(8,128)(2,1)S(1)}, bf16[2,1376,128]{2,1,0:T(8,128)(2,1)S(1)}, u32[]{:S(2)}, u32[]{:S(2)}) collective-permute-start(bf16[2,1376,128]{2,1,0:T(8,128)(2,1)S(1)} %collective-permute-done.6.refs_13_), channel_id=1, source_target_pairs={{8,0},{16,8},{24,16},{28,24},{20,28},{12,20},{4,12},{0,4},{9,1},{1... | collective-permute-start | bytes 2113544 | tf_op jit(solution)/shard_map/ppermute | solution.py:684
  49.6 18.5 %collective-permute-start.14 = (bf16[2,1376,128]{2,1,0:T(8,128)(2,1)S(1)}, bf16[2,1376,128]{2,1,0:T(8,128)(2,1)S(1)}, u32[]{:S(2)}, u32[]{:S(2)}) collective-permute-start(bf16[2,1376,128]{2,1,0:T(8,128)(2,1)S(1)} %collective-permute-done.6.refs_13_), channel_id=1, source_target_pairs={{0,1},{1,0},{2,3},{3,2},{4,5},{5,4},{6,7},{7,6},{8,9},{9,8},{10,11... | collective-permute-start | bytes 2113544 | tf_op jit(solution)/shard_map/ppermute | solution.py:633
  49.7 18.4 %collective-permute-start.12 = (bf16[2,1376,128]{2,1,0:T(8,128)(2,1)S(1)}, bf16[2,1376,128]{2,1,0:T(8,128)(2,1)}, u32[]{:S(2)}, u32[]{:S(2)}) collective-permute-start(bf16[2,1376,128]{2,1,0:T(8,128)(2,1)S(1)} %pad_maximum_fusion.1), channel_id=1, source_target_pairs={{0,2},{1,3},{2,0},{3,1},{4,6},{5,7},{6,4},{7,5},{8,10},{9,11},{10,... | collective-permute-start | bytes 2113544 | tf_op jit(solution)/shard_map/ppermute | solution.py:633
  50.3 17.8 %collective-permute-start.15 = (bf16[2,1376,128]{2,1,0:T(8,128)(2,1)S(1)}, bf16[2,1376,128]{2,1,0:T(8,128)(2,1)S(1)}, u32[]{:S(2)}, u32[]{:S(2)}) collective-permute-start(bf16[2,1376,128]{2,1,0:T(8,128)(2,1)S(1)} %collective-permute-done.7.refs_14_), channel_id=1, source_target_pairs={{0,1},{1,0},{2,3},{3,2},{4,5},{5,4},{6,7},{7,6},{8,9},{9,8},{10,11... | collective-permute-start | bytes 2113544 | tf_op jit(solution)/shard_map/ppermute | solution.py:633
  69.1 20.2 %collective-permute-start.16 = (bf16[2,1376,128]{2,1,0:T(8,128)(2,1)S(1)}, bf16[2,1376,128]{2,1,0:T(8,128)(2,1)}, u32[]{:S(2)}, u32[]{:S(2)}) collective-permute-start(bf16[2,1376,128]{2,1,0:T(8,128)(2,1)S(1)} %collective-permute-done.10.refs_17_), channel_id=1, source_target_pairs={{0,8},{8,16},{16,24},{24,28},{28,20},{20,12},{12,4},{4,0},{1,9},{9... | collective-permute-start | bytes 2113544 | tf_op jit(solution)/shard_map/ppermute | solution.py:681
  70.8 18.6 %collective-permute-start.20 = (bf16[2,1376,128]{2,1,0:T(8,128)(2,1)S(1)}, bf16[2,1376,128]{2,1,0:T(8,128)(2,1)}, u32[]{:S(2)}, u32[]{:S(2)}) collective-permute-start(bf16[2,1376,128]{2,1,0:T(8,128)(2,1)S(1)} %collective-permute-done.11.refs_18_), channel_id=1, source_target_pairs={{0,1},{1,0},{2,3},{3,2},{4,5},{5,4},{6,7},{7,6},{8,9},{9,8},{10,11... | collective-permute-start | bytes 2113544 | tf_op jit(solution)/shard_map/ppermute | solution.py:633
  71.2 18.1 %collective-permute-start.18 = (bf16[2,1376,128]{2,1,0:T(8,128)(2,1)S(1)}, bf16[2,1376,128]{2,1,0:T(8,128)(2,1)}, u32[]{:S(2)}, u32[]{:S(2)}) collective-permute-start(bf16[2,1376,128]{2,1,0:T(8,128)(2,1)S(1)} %pad_maximum_fusion.2), channel_id=1, source_target_pairs={{0,2},{1,3},{2,0},{3,1},{4,6},{5,7},{6,4},{7,5},{8,10},{9,11},{10,... | collective-permute-start | bytes 2113544 | tf_op jit(solution)/shard_map/ppermute | solution.py:633
  71.8 17.5 %collective-permute-start.21 = (bf16[2,1376,128]{2,1,0:T(8,128)(2,1)}, bf16[2,1376,128]{2,1,0:T(8,128)(2,1)}, u32[]{:S(2)}, u32[]{:S(2)}) collective-permute-start(bf16[2,1376,128]{2,1,0:T(8,128)(2,1)} %collective-permute-done.12.refs_20_), channel_id=1, source_target_pairs={{0,1},{1,0},{2,3},{3,2},{4,5},{5,4},{6,7},{7,6},{8,9},{9,8},{10,11... | collective-permute-start | bytes 2113544 | tf_op jit(solution)/shard_map/ppermute | solution.py:633
  71.9 10.8 %collective-permute-start.17 = (bf16[1,1376,128]{2,1,0:T(8,128)(2,1)S(1)}, bf16[1,1376,128]{2,1,0:T(8,128)(2,1)S(1)}, u32[]{:S(2)}, u32[]{:S(2)}) collective-permute-start(bf16[1,1376,128]{2,1,0:T(8,128)(2,1)S(1)} %slice.122), channel_id=1, source_target_pairs={{8,0},{16,8},{24,16},{28,24},{20,28},{12,20},{4,12},{0,4},{9,1},{1... | collective-permute-start | bytes 1056776 | tf_op jit(solution)/shard_map/ppermute | solution.py:684
  141.1 5.4 %collective-permute-start.27 = (bf16[2,2,1344,128]{3,2,1,0:T(8,128)(2,1)}, bf16[2,2,1344,128]{3,2,1,0:T(8,128)(2,1)S(1)}, u32[]{:S(2)}, u32[]{:S(2)}) collective-permute-start(bf16[2,2,1344,128]{3,2,1,0:T(8,128)(2,1)} %get-tuple-element.176), channel_id=1, source_target_pairs={{0,1},{1,0},{2,3},{3,2},{4,5},{5,4},{6,7},{7,6},{8,9},{9,8},{10,11... | collective-permute-start | bytes 4128776 | tf_op jit(solution)/shard_map/ppermute | solution.py:633
  146.5 12.4 %collective-permute-start.32 = (bf16[5,2,1344,128]{3,2,1,0:T(8,128)(2,1)S(1)}, bf16[5,2,1344,128]{3,2,1,0:T(8,128)(2,1)S(1)}, u32[]{:S(2)}, u32[]{:S(2)}) collective-permute-start(bf16[5,2,1344,128]{3,2,1,0:T(8,128)(2,1)S(1)} %copy-done.35), channel_id=1, source_target_pairs={{0,1},{1,0},{2,3},{3,2},{4,5},{5,4},{6,7},{7,6},{8,9},{9,8},{10,11... | collective-permute-start | bytes 10321928 | tf_op jit(solution)/shard_map/ppermute | solution.py:633
  146.7 8.9 %collective-permute-start.33 = (bf16[6,2,672,128]{3,2,1,0:T(8,128)(2,1)}, bf16[6,2,672,128]{3,2,1,0:T(8,128)(2,1)S(1)}, u32[]{:S(2)}, u32[]{:S(2)}) collective-permute-start(bf16[6,2,672,128]{3,2,1,0:T(8,128)(2,1)} %get-tuple-element.186), channel_id=1, source_target_pairs={{0,1},{1,0},{2,3},{3,2},{4,5},{5,4},{6,7},{7,6},{8,9},{9,8},{10,11... | collective-permute-start | bytes 6193160 | tf_op jit(solution)/shard_map/ppermute | solution.py:633
  147.1 10.2 %collective-permute-start.29 = (bf16[1,1344,128]{2,1,0:T(8,128)(2,1)S(1)}, bf16[1,1344,128]{2,1,0:T(8,128)(2,1)S(1)}, u32[]{:S(2)}, u32[]{:S(2)}) collective-permute-start(bf16[1,1344,128]{2,1,0:T(8,128)(2,1)S(1)} %get-tuple-element.274), channel_id=1, source_target_pairs={{0,8},{8,16},{16,24},{24,28},{28,20},{20,12},{12,4},{4,0},{1,9},{9... | collective-permute-start | bytes 1032200 | tf_op jit(solution)/shard_map/ppermute | solution.py:681
  148.7 9.8 %collective-permute-start.30 = (bf16[1,1344,128]{2,1,0:T(8,128)(2,1)S(1)}, bf16[1,1344,128]{2,1,0:T(8,128)(2,1)S(1)}, u32[]{:S(2)}, u32[]{:S(2)}) collective-permute-start(bf16[1,1344,128]{2,1,0:T(8,128)(2,1)S(1)} %get-tuple-element.273), channel_id=1, source_target_pairs={{8,0},{16,8},{24,16},{28,24},{20,28},{12,20},{4,12},{0,4},{9,1},{1... | collective-permute-start | bytes 1032200 | tf_op jit(solution)/shard_map/ppermute | solution.py:684
  149.2 9.6 %collective-permute-start.31 = (bf16[2,672,128]{2,1,0:T(8,128)(2,1)S(1)}, bf16[2,672,128]{2,1,0:T(8,128)(2,1)S(1)}, u32[]{:S(2)}, u32[]{:S(2)}) collective-permute-start(bf16[2,672,128]{2,1,0:T(8,128)(2,1)S(1)} %slice_bitcast_fusion.2), channel_id=1, source_target_pairs={{0,2},{1,3},{2,0},{3,1},{4,6},{5,7},{6,4},{7,5},{8,10},{9,11},{10,... | collective-permute-start | bytes 1032200 | tf_op jit(solution)/shard_map/ppermute | solution.py:633
  158.9 12.5 %collective-permute-start.38 = (bf16[3,672,128]{2,1,0:T(8,128)(2,1)S(1)}, bf16[3,672,128]{2,1,0:T(8,128)(2,1)S(1)}, u32[]{:S(2)}, u32[]{:S(2)}) collective-permute-start(bf16[3,672,128]{2,1,0:T(8,128)(2,1)S(1)} %slice_bitcast_fusion), channel_id=1, source_target_pairs={{0,2},{1,3},{2,0},{3,1},{4,6},{5,7},{6,4},{7,5},{8,10},{9,11},{10,... | collective-permute-start | bytes 1548296 | tf_op jit(solution)/shard_map/ppermute | solution.py:633
  159.5 13.3 %collective-permute-start.36 = (bf16[336,128]{1,0:T(8,128)(2,1)S(1)}, bf16[336,128]{1,0:T(8,128)(2,1)S(1)}, u32[]{:S(2)}, u32[]{:S(2)}) collective-permute-start(bf16[336,128]{1,0:T(8,128)(2,1)S(1)} %get-tuple-element.272), channel_id=1, source_target_pairs={{0,8},{8,16},{16,24},{24,28},{28,20},{20,12},{12,4},{4,0},{1,9},{9... | collective-permute-start | bytes 258056 | tf_op jit(solution)/shard_map/ppermute | solution.py:681
  161.2 11.7 %collective-permute-start.37 = (bf16[336,128]{1,0:T(8,128)(2,1)S(1)}, bf16[336,128]{1,0:T(8,128)(2,1)S(1)}, u32[]{:S(2)}, u32[]{:S(2)}) collective-permute-start(bf16[336,128]{1,0:T(8,128)(2,1)S(1)} %get-tuple-element.271), channel_id=1, source_target_pairs={{8,0},{16,8},{24,16},{28,24},{20,28},{12,20},{4,12},{0,4},{9,1},{1... | collective-permute-start | bytes 258056 | tf_op jit(solution)/shard_map/ppermute | solution.py:684
  161.8 16.2 %collective-permute-start.34 = (bf16[2,1344,128]{2,1,0:T(8,128)(2,1)S(1)}, bf16[2,1344,128]{2,1,0:T(8,128)(2,1)S(1)}, u32[]{:S(2)}, u32[]{:S(2)}) collective-permute-start(bf16[2,1344,128]{2,1,0:T(8,128)(2,1)S(1)} %get-tuple-element.270), channel_id=1, source_target_pairs={{0,8},{8,16},{16,24},{24,28},{28,20},{20,12},{12,4},{4,0},{1,9},{9... | collective-permute-start | bytes 2064392 | tf_op jit(solution)/shard_map/ppermute | solution.py:681
  163.4 15.9 %collective-permute-start.35 = (bf16[2,1344,128]{2,1,0:T(8,128)(2,1)S(1)}, bf16[2,1344,128]{2,1,0:T(8,128)(2,1)S(1)}, u32[]{:S(2)}, u32[]{:S(2)}) collective-permute-start(bf16[2,1344,128]{2,1,0:T(8,128)(2,1)S(1)} %get-tuple-element.269), channel_id=1, source_target_pairs={{8,0},{16,8},{24,16},{28,24},{20,28},{12,20},{4,12},{0,4},{9,1},{1... | collective-permute-start | bytes 2064392 | tf_op jit(solution)/shard_map/ppermute | solution.py:684
  180.1 11.6 %collective-permute-start.44 = (bf16[3,672,128]{2,1,0:T(8,128)(2,1)}, bf16[3,672,128]{2,1,0:T(8,128)(2,1)}, u32[]{:S(2)}, u32[]{:S(2)}) collective-permute-start(bf16[3,672,128]{2,1,0:T(8,128)(2,1)} %slice_bitcast_fusion.1), channel_id=1, source_target_pairs={{0,2},{1,3},{2,0},{3,1},{4,6},{5,7},{6,4},{7,5},{8,10},{9,11},{10,... | collective-permute-start | bytes 1548296 | tf_op jit(solution)/shard_map/ppermute | solution.py:633
  182.3 10.0 %collective-permute-start.43 = (bf16[672,128]{1,0:T(8,128)(2,1)}, bf16[672,128]{1,0:T(8,128)(2,1)}, u32[]{:S(2)}, u32[]{:S(2)}) collective-permute-start(bf16[672,128]{1,0:T(8,128)(2,1)} %fusion.21), channel_id=1, source_target_pairs={{8,0},{16,8},{24,16},{28,24},{20,28},{12,20},{4,12},{0,4},{9,1},{1... | collective-permute-start | bytes 516104 | tf_op jit(solution)/shard_map/ppermute | solution.py:684
  184.3 19.4 %collective-permute-start.40 = (bf16[2,1344,128]{2,1,0:T(8,128)(2,1)}, bf16[2,1344,128]{2,1,0:T(8,128)(2,1)}, u32[]{:S(2)}, u32[]{:S(2)}) collective-permute-start(bf16[2,1344,128]{2,1,0:T(8,128)(2,1)} %get-tuple-element.264), channel_id=1, source_target_pairs={{0,8},{8,16},{16,24},{24,28},{28,20},{20,12},{12,4},{4,0},{1,9},{9... | collective-permute-start | bytes 2064392 | tf_op jit(solution)/shard_map/ppermute | solution.py:681
  185.8 17.9 %collective-permute-start.41 = (bf16[2,1344,128]{2,1,0:T(8,128)(2,1)}, bf16[2,1344,128]{2,1,0:T(8,128)(2,1)}, u32[]{:S(2)}, u32[]{:S(2)}) collective-permute-start(bf16[2,1344,128]{2,1,0:T(8,128)(2,1)} %get-tuple-element.263), channel_id=1, source_target_pairs={{8,0},{16,8},{24,16},{28,24},{20,28},{12,20},{4,12},{0,4},{9,1},{1... | collective-permute-start | bytes 2064392 | tf_op jit(solution)/shard_map/ppermute | solution.py:684
  187.0 16.2 %collective-permute-start.42 = (bf16[672,128]{1,0:T(8,128)(2,1)}, bf16[672,128]{1,0:T(8,128)(2,1)}, u32[]{:S(2)}, u32[]{:S(2)}) collective-permute-start(bf16[672,128]{1,0:T(8,128)(2,1)} %fusion.23), channel_id=1, source_target_pairs={{0,8},{8,16},{16,24},{24,28},{28,20},{20,12},{12,4},{4,0},{1,9},{9... | collective-permute-start | bytes 516104 | tf_op jit(solution)/shard_map/ppermute | solution.py:681
  191.7 11.9 %collective-permute-start.45 = (f32[4,24,96]{2,1,0:T(8,128)S(1)}, f32[4,24,96]{2,1,0:T(8,128)S(1)}, u32[]{:S(2)}, u32[]{:S(2)}) collective-permute-start(f32[4,24,96]{2,1,0:T(8,128)S(1)} %get-tuple-element.277), channel_id=1, source_target_pairs={{0,4},{1,5},{2,6},{3,7},{4,0},{5,1},{6,2},{7,3},{8,12},{9,13},{10,... | collective-permute-start | bytes 110600 | tf_op jit(solution)/shard_map/ppermute | solution.py:638
  205.4 18.9 %collective-permute-start.46 = (bf16[2,1344,128]{2,1,0:T(8,128)(2,1)S(1)}, bf16[2,1344,128]{2,1,0:T(8,128)(2,1)S(1)}, u32[]{:S(2)}, u32[]{:S(2)}) collective-permute-start(bf16[2,1344,128]{2,1,0:T(8,128)(2,1)S(1)} %get-tuple-element.262), channel_id=1, source_target_pairs={{0,8},{8,16},{16,24},{24,28},{28,20},{20,12},{12,4},{4,0},{1,9},{9... | collective-permute-start | bytes 2064392 | tf_op jit(solution)/shard_map/ppermute | solution.py:681
  206.1 18.3 %collective-permute-start.47 = (bf16[2,1344,128]{2,1,0:T(8,128)(2,1)S(1)}, bf16[2,1344,128]{2,1,0:T(8,128)(2,1)S(1)}, u32[]{:S(2)}, u32[]{:S(2)}) collective-permute-start(bf16[2,1344,128]{2,1,0:T(8,128)(2,1)S(1)} %get-tuple-element.261), channel_id=1, source_target_pairs={{8,0},{16,8},{24,16},{28,24},{20,28},{12,20},{4,12},{0,4},{9,1},{1... | collective-permute-start | bytes 2064392 | tf_op jit(solution)/shard_map/ppermute | solution.py:684
  208.8 15.5 %collective-permute-start.48 = (bf16[672,128]{1,0:T(8,128)(2,1)S(1)}, bf16[672,128]{1,0:T(8,128)(2,1)S(1)}, u32[]{:S(2)}, u32[]{:S(2)}) collective-permute-start(bf16[672,128]{1,0:T(8,128)(2,1)S(1)} %get-tuple-element.268), channel_id=1, source_target_pairs={{0,8},{8,16},{16,24},{24,28},{28,20},{20,12},{12,4},{4,0},{1,9},{9... | collective-permute-start | bytes 516104 | tf_op jit(solution)/shard_map/ppermute | solution.py:681
  209.5 14.8 %collective-permute-start.49 = (bf16[672,128]{1,0:T(8,128)(2,1)S(1)}, bf16[672,128]{1,0:T(8,128)(2,1)S(1)}, u32[]{:S(2)}, u32[]{:S(2)}) collective-permute-start(bf16[672,128]{1,0:T(8,128)(2,1)S(1)} %get-tuple-element.267), channel_id=1, source_target_pairs={{8,0},{16,8},{24,16},{28,24},{20,28},{12,20},{4,12},{0,4},{9,1},{1... | collective-permute-start | bytes 516104 | tf_op jit(solution)/shard_map/ppermute | solution.py:684
  210.9 13.4 %collective-permute-start.50 = (f32[2,24,96]{2,1,0:T(8,128)S(1)}, f32[2,24,96]{2,1,0:T(8,128)S(1)}, u32[]{:S(2)}, u32[]{:S(2)}) collective-permute-start(f32[2,24,96]{2,1,0:T(8,128)S(1)} %get-tuple-element.279), channel_id=1, source_target_pairs={{0,8},{1,9},{2,10},{3,11},{4,12},{5,13},{6,14},{7,15},{8,0},{9,1},... | collective-permute-start | bytes 55304 | tf_op jit(solution)/shard_map/ppermute | solution.py:638
  224.6 13.2 %collective-permute-start.51 = (bf16[2,1344,128]{2,1,0:T(8,128)(2,1)S(1)}, bf16[2,1344,128]{2,1,0:T(8,128)(2,1)S(1)}, u32[]{:S(2)}, u32[]{:S(2)}) collective-permute-start(bf16[2,1344,128]{2,1,0:T(8,128)(2,1)S(1)} %fusion.3), channel_id=1, source_target_pairs={{0,2},{1,3},{2,0},{3,1},{4,6},{5,7},{6,4},{7,5},{8,10},{9,11},{10,... | collective-permute-start | bytes 2064392 | tf_op jit(solution)/shard_map/ppermute | solution.py:633
  226.5 7.7 %collective-permute-start.52 = (bf16[672,128]{1,0:T(8,128)(2,1)S(1)}, bf16[672,128]{1,0:T(8,128)(2,1)S(1)}, u32[]{:S(2)}, u32[]{:S(2)}) collective-permute-start(bf16[672,128]{1,0:T(8,128)(2,1)S(1)} %get-tuple-element.266), channel_id=1, source_target_pairs={{0,8},{8,16},{16,24},{24,28},{28,20},{20,12},{12,4},{4,0},{1,9},{9... | collective-permute-start | bytes 516104 | tf_op jit(solution)/shard_map/ppermute | solution.py:681
  226.8 7.4 %collective-permute-start.53 = (bf16[672,128]{1,0:T(8,128)(2,1)S(1)}, bf16[672,128]{1,0:T(8,128)(2,1)S(1)}, u32[]{:S(2)}, u32[]{:S(2)}) collective-permute-start(bf16[672,128]{1,0:T(8,128)(2,1)S(1)} %get-tuple-element.265), channel_id=1, source_target_pairs={{8,0},{16,8},{24,16},{28,24},{20,28},{12,20},{4,12},{0,4},{9,1},{1... | collective-permute-start | bytes 516104 | tf_op jit(solution)/shard_map/ppermute | solution.py:684
  228.6 5.6 %collective-permute-start.54 = (f32[24,96]{1,0:T(8,128)S(1)}, f32[24,96]{1,0:T(8,128)S(1)}, u32[]{:S(2)}, u32[]{:S(2)}) collective-permute-start(f32[24,96]{1,0:T(8,128)S(1)} %get-tuple-element.281), channel_id=1, source_target_pairs={{0,16},{1,17},{2,18},{3,19},{4,20},{5,21},{6,22},{7,23},{8,24},{9,... | collective-permute-start | bytes 27656 | tf_op jit(solution)/shard_map/ppermute | solution.py:638
  239.9 6.8 %collective-permute-start.56 = (bf16[2,1344,128]{2,1,0:T(8,128)(2,1)S(1)}, bf16[2,1344,128]{2,1,0:T(8,128)(2,1)S(1)}, u32[]{:S(2)}, u32[]{:S(2)}) collective-permute-start(bf16[2,1344,128]{2,1,0:T(8,128)(2,1)S(1)} %get-tuple-element.236.own), channel_id=1, source_target_pairs={{0,1},{1,0},{2,3},{3,2},{4,5},{5,4},{6,7},{7,6},{8,9},{9,8},{10,11... | collective-permute-start | bytes 2064392 | tf_op jit(solution)/shard_map/ppermute | solution.py:633
  239.9 6.8 %collective-permute-start.55 = (bf16[672,128]{1,0:T(8,128)(2,1)S(1)}, bf16[672,128]{1,0:T(8,128)(2,1)S(1)}, u32[]{:S(2)}, u32[]{:S(2)}) collective-permute-start(bf16[672,128]{1,0:T(8,128)(2,1)S(1)} %fusion.19), channel_id=1, source_target_pairs={{0,2},{1,3},{2,0},{3,1},{4,6},{5,7},{6,4},{7,5},{8,10},{9,11},{10,... | collective-permute-start | bytes 516104 | tf_op jit(solution)/shard_map/ppermute | solution.py:633
  250.2 10.8 %collective-permute-start.63 = (bf16[1344,128]{1,0:T(8,128)(2,1)S(1)}, bf16[1344,128]{1,0:T(8,128)(2,1)S(1)}, u32[]{:S(2)}, u32[]{:S(2)}) collective-permute-start(bf16[1344,128]{1,0:T(8,128)(2,1)S(1)} %get-tuple-element.256.split_own), channel_id=1, source_target_pairs={{0,1},{1,0},{2,3},{3,2},{4,5},{5,4},{6,7},{7,6},{8,9},{9,8},{10,11... | collective-permute-start | bytes 1032200 | tf_op jit(solution)/shard_map/ppermute | solution.py:633
  (53 other events, 343.0 us)

commit v5 on v4

--- a/solution.py
+++ b/solution.py
@@ -70,10 +70,10 @@
     info, pos = refs[:2]
     n_parts = n_refs[0]
     parcels, sources = refs[2 : 2 + n_parts], refs[2 + n_parts : 2 + sum(n_refs)]
-    *outs, vgrad = refs[2 + sum(n_refs) : 3 + sum(n_refs) + OUTS]
+    *outs, vgrad_out = refs[2 + sum(n_refs) : 3 + sum(n_refs) + OUTS]
     w, vec_blocks, vec, pix, target, mask_rows, mask, bias, *refs = refs[3 + sum(n_refs) + OUTS :]
     (x0, x1, x2, branch, mlp, work, qkv, probs, inverses, attn, slope, act, hid, low, *sems) = refs
-    sem_in, sem_part, sem_out = sems
+    vgrad, sem_in, sem_part, sem_out = sems
     length, width = pix.shape
     part = length // n_parts
     pairs = width // 256
@@ -393,6 +393,8 @@
         put_pair(i, ROW_P, nn(flipped, hid[:, cols(i)]))
 
     leave(0, *first)
+    for q in range(BLOCKS):
+        vgrad_out[q] = vgrad[:, 96 * q : 96 * q + 96]
     for number, out in enumerate(outs):
         for group, (begin, end) in enumerate((first, second)):
             lo, hi = out_rows(number, begin, end)
@@ -416,7 +418,7 @@
                 for places in SPLIT_PLACES
                 for _ in range(2)
             ),
-            jax.ShapeDtypeStruct((24, width), f32),
+            jax.ShapeDtypeStruct((BLOCKS, 24, width // BLOCKS), f32),
         ),
         in_specs=[pl.BlockSpec(memory_space=pltpu.SMEM)] + [vmem] + [anywhere] * (len(parcels) + len(sources)),
         out_specs=(*[anywhere] * OUTS, vmem),
@@ -443,6 +445,7 @@
             pltpu.VMEM((length, hidden), bf16),
             small,
             small,
+            pltpu.VMEM((24, width), f32),
             pltpu.SemaphoreType.DMA((2,)),
             pltpu.SemaphoreType.DMA((4,)),
             pltpu.SemaphoreType.DMA((OUTS, 2)),
@@ -804,7 +807,7 @@
         def high_half(value):
             return jnp.pad(value.astype(f32), ((1, 0), (0, 0), (0, 0)))
 
-        small = vgrad.reshape(-1, n_dp, features // n_dp).transpose(1, 0, 2)
+        small = vgrad
         opposite, split_first, next_got, small, small_more, send_rest, split_send_rest = tick(
             rounded(keeps[0], across(sends[0])),
             rounded(split_keeps[0], across(split_sends[0])),
@@ -896,6 +899,7 @@
             split = by_place(SPLIT_PLACES, split)
             return jnp.concatenate([by_place(PLACES, whole), join_halves(split[:, 0], split[:, 1])[:, None]], 1)
 
+        vgrad = vgrad.transpose(1, 0, 2).reshape(-1, features)
         canonical = jnp.concatenate([three(keeps, split_keeps), three(sends, split_sends)], 1).transpose(1, 0, 2, 3)
 
         def join(row, end, blocks):

time: 273 us -> 273 us (level)
  transfers between devices with their start and end apart: 64 -> 64, of which waited for: 32 -> 32; matrix products, arithmetic and copies ran while one was open for 8% -> 7% of each run, Pallas kernels for 1% -> 1%
where the time goes in v5:
time: 273 us; the launch traced here: 272 us
  waiting for transfers between devices  126 us (46%)
  Pallas kernels  62.9 us (23%)
  starting transfers between devices  48.5 us (18%)
  other arithmetic  22.1 us (8%)
  local copies, waits for them, and re-layouts  9.35 us (3%)
  between operations  3.44 us (1%)
    ppermute x31, waiting for transfers between devices, seq_flip(): return lax.ppermute(value, 'seq', [(i, i ^ k) for i in range(n_seq)])  74.8 us
    pallas_call x1, Pallas kernels, run_step(): pl.pallas_call(partial(step_kernel, pieces, vec_pieces, (len(parcels), le...  46.4 us
    ppermute x9, waiting for transfers between devices, hop(): return lax.ppermute(value, ('dp', 'seq'), pairs)  22.2 us
    ppermute x12, starting transfers between devices, ahead(): return lax.ppermute(value, 'dp', forward)  17.5 us
    ppermute x12, waiting for transfers between devices, ahead(): return lax.ppermute(value, 'dp', forward)  16.2 us
    ppermute x31, starting transfers between devices, seq_flip(): return lax.ppermute(value, 'seq', [(i, i ^ k) for i in range(n_seq)])  13 us
    ppermute x12, waiting for transfers between devices, behind(): return lax.ppermute(value, 'dp', backward)  12.7 us
    convert_element_type x15, other arithmetic, rounded(): return sum((value.astype(f32) for value in values)).astype(bf16)  12.3 us
  transfers between devices with their start and end apart: 64, of which 32 were waited for; matrix products, arithmetic and copies ran while one was open for 7% of the time, Pallas kernels for 1%

profile of v5, /device:TPU:0, one launch (start us, length us, event | category | flops | bytes accessed | tf_op | source)
XLA Modules:
  0.0 272.2 jit_solution(3401866127241467662)
XLA Ops:
  1.4 4.2 %pack.1 = (bf16[6,1344,128]{2,1,0:T(8,128)(2,1)}, bf16[2,1376,128]{2,1,0:T(8,128)(2,1)}, bf16[2,1376,128]{2,1,0:T(8,128)(2,1)}) custom-call(s32[4]{0:T(128)} %pad_add_fusion.2.chosen, f32[3,96,768]{2,1,0:T(8,128)} %refs_0_.1, f32[96,2304]{1,0:T(8,128)} %refs_1_.1, f32[96,3072]{1,0:T(8,128)} %refs_2_.1, f32[384,768]{1,0:T(8,128)} %refs_3_.1, f32[20,96]{1,0:T(8,128)} %refs_4_.1), custom_call_target="tpu_custom_call" | custom-call | tf_op jit(solution)/shard_map/pack/pallas_call | solution.py:483
  5.5 3.1 %collective-permute-start = (bf16[2,1376,128]{2,1,0:T(8,128)(2,1)}, bf16[2,1376,128]{2,1,0:T(8,128)(2,1)S(1)}, u32[]{:S(2)}, u32[]{:S(2)}) collective-permute-start(bf16[2,1376,128]{2,1,0:T(8,128)(2,1)} %get-tuple-element.136.refs_7_), channel_id=1, source_target_pairs={{0,8},{8,16},{16,24},{24,28},{28,20},{20,12},{12,4},{4,0},{1,9},{9... | collective-permute-start | bytes 2113544 | tf_op jit(solution)/shard_map/ppermute | solution.py:684
  9.1 2.1 parcels.1
  11.2 1.9 collective-permute-start.3
  13.3 6.5 %collective-permute-done.3.refs_4_ = bf16[144,768]{1,0:T(8,128)(2,1)S(1)} collective-permute-done((bf16[144,768]{1,0:T(8,128)(2,1)}, bf16[144,768]{1,0:T(8,128)(2,1)S(1)}, u32[]{:S(2)}, u32[]{:S(2)}) %collective-permute-start.3) | collective-permute-done | bytes 221216 | tf_op jit(solution)/shard_map/ppermute | solution.py:636
  19.7 4.2 %collective-permute-done.4.refs_5_ = bf16[144,768]{1,0:T(8,128)(2,1)S(1)} collective-permute-done((bf16[144,768]{1,0:T(8,128)(2,1)}, bf16[144,768]{1,0:T(8,128)(2,1)S(1)}, u32[]{:S(2)}, u32[]{:S(2)}) %collective-permute-start.4) | collective-permute-done | bytes 221216 | tf_op jit(solution)/shard_map/ppermute | solution.py:636
  24.6 1.4 collective-permute-done.1.refs_9_
  26.2 1.6 collective-permute-start.7
  27.7 1.6 collective-permute-start.5
  30.3 3.8 %fusion.8.refs_1_ = f32[256,768]{1,0:T(8,128)} fusion(f32[768]{0:T(1024)S(1)} %fusion.31, f32[256]{0:T(256)S(1)} %iota_convert_fusion, pred[768]{0:T(1024)(128)(4,1)S(1)} %fusion.26), kind=kLoop, calls=%fused_computation.26 | loop fusion | flops 393216 | bytes 791296 | tf_op jit(solution)/shard_map/jit(_where)/select_n | solution.py:632
  34.1 8.8 %collective-permute-done.7.refs_14_ = bf16[2,1376,128]{2,1,0:T(8,128)(2,1)S(1)} collective-permute-done((bf16[2,1376,128]{2,1,0:T(8,128)(2,1)S(1)}, bf16[2,1376,128]{2,1,0:T(8,128)(2,1)S(1)}, u32[]{:S(2)}, u32[]{:S(2)}) %collective-permute-start.7) | collective-permute-done | bytes 704544 | tf_op jit(solution)/shard_map/ppermute | solution.py:636
  42.9 1.5 collective-permute-done.5.refs_12_
  47.4 1.6 collective-permute-start.10
  50.6 17.5 %collective-permute-done.12.refs_20_ = bf16[2,1376,128]{2,1,0:T(8,128)(2,1)} collective-permute-done((bf16[2,1376,128]{2,1,0:T(8,128)(2,1)S(1)}, bf16[2,1376,128]{2,1,0:T(8,128)(2,1)}, u32[]{:S(2)}, u32[]{:S(2)}) %collective-permute-start.12) | collective-permute-done | bytes 704544 | tf_op jit(solution)/shard_map/ppermute | solution.py:636
  69.1 1.6 collective-permute-start.16
  75.3 7.4 %collective-permute-done.17.refs_26_ = bf16[1,1376,128]{2,1,0:T(8,128)(2,1)S(1)} collective-permute-done((bf16[1,1376,128]{2,1,0:T(8,128)(2,1)S(1)}, bf16[1,1376,128]{2,1,0:T(8,128)(2,1)S(1)}, u32[]{:S(2)}, u32[]{:S(2)}) %collective-permute-start.17) | collective-permute-done | bytes 352288 | tf_op jit(solution)/shard_map/ppermute | solution.py:687
  82.7 6.6 %collective-permute-done.18.refs_24_ = bf16[2,1376,128]{2,1,0:T(8,128)(2,1)} collective-permute-done((bf16[2,1376,128]{2,1,0:T(8,128)(2,1)S(1)}, bf16[2,1376,128]{2,1,0:T(8,128)(2,1)}, u32[]{:S(2)}, u32[]{:S(2)}) %collective-permute-start.18) | collective-permute-done | bytes 704544 | tf_op jit(solution)/shard_map/ppermute | solution.py:636
  90.0 3.3 %collective-permute-done.23.refs_28_ = bf16[1,1376,128]{2,1,0:T(8,128)(2,1)S(1)} collective-permute-done((bf16[1,1376,128]{2,1,0:T(8,128)(2,1)S(1)}, bf16[1,1376,128]{2,1,0:T(8,128)(2,1)S(1)}, u32[]{:S(2)}, u32[]{:S(2)}) %collective-permute-start.23) | collective-permute-done | bytes 352288 | tf_op jit(solution)/shard_map/ppermute | solution.py:636
  94.5 46.4 %step.1 = (bf16[1,2,1344,128]{3,2,1,0:T(8,128)(2,1)}, bf16[1,2,1344,128]{3,2,1,0:T(8,128)(2,1)}, bf16[2,2,1344,128]{3,2,1,0:T(8,128)(2,1)}, bf16[2,2,1344,128]{3...) custom-call(s32[56]{0:T(128)} %concatenate.20.refs_0_, ...), custom_call_target="tpu_custom_call" | custom-call | tf_op jit(solution)/shard_map/step/pallas_call | solution.py:412
  143.3 1.4 add_convert_fusion.5
  144.8 1.5 collective-permute-done.26
  147.2 1.6 collective-permute-start.29
  150.3 5.3 %collective-permute-done.33 = bf16[6,2,672,128]{3,2,1,0:T(8,128)(2,1)S(1)} collective-permute-done((bf16[6,2,672,128]{3,2,1,0:T(8,128)(2,1)}, bf16[6,2,672,128]{3,2,1,0:T(8,128)(2,1)S(1)}, u32[]{:S(2)}, u32[]{:S(2)}) %collective-permute-start.33) | collective-permute-done | bytes 2064416 | tf_op jit(solution)/shard_map/ppermute | solution.py:636
  159.6 1.6 collective-permute-start.36
  161.8 1.6 collective-permute-start.34
  163.9 7.5 %collective-permute-done.38 = bf16[3,672,128]{2,1,0:T(8,128)(2,1)S(1)} collective-permute-done((bf16[3,672,128]{2,1,0:T(8,128)(2,1)S(1)}, bf16[3,672,128]{2,1,0:T(8,128)(2,1)S(1)}, u32[]{:S(2)}, u32[]{:S(2)}) %collective-permute-start.38) | collective-permute-done | bytes 516128 | tf_op jit(solution)/shard_map/ppermute | solution.py:636
  172.9 3.1 %collective-permute-done.39 = f32[8,24,96]{2,1,0:T(8,128)S(1)} collective-permute-done((f32[8,24,96]{2,1,0:T(8,128)S(1)}, f32[8,24,96]{2,1,0:T(8,128)S(1)}, u32[]{:S(2)}, u32[]{:S(2)}) %collective-permute-start.39) | collective-permute-done | bytes 73760 | tf_op jit(solution)/shard_map/ppermute | solution.py:636
  176.0 2.1 collective-permute-done.34
  180.1 1.5 collective-permute-start.44
  182.8 1.4 fusion.4
  184.3 1.6 collective-permute-start.40
  187.0 1.6 collective-permute-start.42
  189.2 1.4 gather_fusion.1
  192.4 10.9 %collective-permute-done.42 = bf16[672,128]{1,0:T(8,128)(2,1)} collective-permute-done((bf16[672,128]{1,0:T(8,128)(2,1)}, bf16[672,128]{1,0:T(8,128)(2,1)}, u32[]{:S(2)}, u32[]{:S(2)}) %collective-permute-start.42) | collective-permute-done | bytes 172064 | tf_op jit(solution)/shard_map/ppermute | solution.py:684
  203.7 1.7 fusion
  206.1 1.4 collective-permute-start.47
  209.5 1.4 collective-permute-start.49
  211.6 12.7 %collective-permute-done.50 = f32[2,24,96]{2,1,0:T(8,128)S(1)} collective-permute-done((f32[2,24,96]{2,1,0:T(8,128)S(1)}, f32[2,24,96]{2,1,0:T(8,128)S(1)}, u32[]{:S(2)}, u32[]{:S(2)}) %collective-permute-start.50) | collective-permute-done | bytes 18464 | tf_op jit(solution)/shard_map/ppermute | solution.py:641
  226.9 1.7 collective-permute-start.53
  228.6 2.0 collective-permute-start.54
  230.7 3.6 %collective-permute-done.54 = f32[24,96]{1,0:T(8,128)S(1)} collective-permute-done((f32[24,96]{1,0:T(8,128)S(1)}, f32[24,96]{1,0:T(8,128)S(1)}, u32[]{:S(2)}, u32[]{:S(2)}) %collective-permute-start.54) | collective-permute-done | bytes 9248 | tf_op jit(solution)/shard_map/ppermute | solution.py:641
  234.2 3.6 %collective-permute-done.51 = bf16[2,1344,128]{2,1,0:T(8,128)(2,1)S(1)} collective-permute-done((bf16[2,1344,128]{2,1,0:T(8,128)(2,1)S(1)}, bf16[2,1344,128]{2,1,0:T(8,128)(2,1)S(1)}, u32[]{:S(2)}, u32[]{:S(2)}) %collective-permute-start.51) | collective-permute-done | bytes 688160 | tf_op jit(solution)/shard_map/ppermute | solution.py:636
  242.4 4.3 %collective-permute-done.55 = bf16[672,128]{1,0:T(8,128)(2,1)S(1)} collective-permute-done((bf16[672,128]{1,0:T(8,128)(2,1)S(1)}, bf16[672,128]{1,0:T(8,128)(2,1)S(1)}, u32[]{:S(2)}, u32[]{:S(2)}) %collective-permute-start.55) | collective-permute-done | bytes 172064 | tf_op jit(solution)/shard_map/ppermute | solution.py:636
  248.3 1.4 collective-permute-start.58
  255.0 2.1 collective-permute-start.62
  257.1 1.4 collective-permute-done.61
  258.6 1.8 collective-permute-done.62
  261.7 10.3 %adam.1 = (f32[1,1]{1,0:T(1,128)}, f32[1,1]{1,0:T(1,128)}, f32[3,96,768]{2,1,0:T(8,128)}, f32[96,2304]{1,0:T(8,128)}, f32[96,3072]{1,0:T(8,128)}, /*index=5*/f32...) custom-call(s32[1]{0:T(128)} %bitcast.core, ...), custom_call_target="tpu_custom_call" | custom-call | tf_op jit(solution)/shard_map/adam/pallas_call | solution.py:611
  (231 shorter events, 50.0 us)
Async XLA Ops:
  5.5 19.0 %collective-permute-start = (bf16[2,1376,128]{2,1,0:T(8,128)(2,1)}, bf16[2,1376,128]{2,1,0:T(8,128)(2,1)S(1)}, u32[]{:S(2)}, u32[]{:S(2)}) collective-permute-start(bf16[2,1376,128]{2,1,0:T(8,128)(2,1)} %get-tuple-element.136.refs_7_), channel_id=1, source_target_pairs={{0,8},{8,16},{16,24},{24,28},{28,20},{20,12},{12,4},{4,0},{1,9},{9... | collective-permute-start | bytes 2113544 | tf_op jit(solution)/shard_map/ppermute | solution.py:684
  8.6 17.5 %collective-permute-start.1 = (bf16[2,1376,128]{2,1,0:T(8,128)(2,1)}, bf16[2,1376,128]{2,1,0:T(8,128)(2,1)S(1)}, u32[]{:S(2)}, u32[]{:S(2)}) collective-permute-start(bf16[2,1376,128]{2,1,0:T(8,128)(2,1)} %get-tuple-element.137), channel_id=1, source_target_pairs={{8,0},{16,8},{24,16},{28,24},{20,28},{12,20},{4,12},{0,4},{9,1},{1... | collective-permute-start | bytes 2113544 | tf_op jit(solution)/shard_map/ppermute | solution.py:687
  11.2 8.5 %collective-permute-start.3 = (bf16[144,768]{1,0:T(8,128)(2,1)}, bf16[144,768]{1,0:T(8,128)(2,1)S(1)}, u32[]{:S(2)}, u32[]{:S(2)}) collective-permute-start(bf16[144,768]{1,0:T(8,128)(2,1)} %get-tuple-element.139), channel_id=1, source_target_pairs={{0,2},{1,3},{2,0},{3,1},{4,6},{5,7},{6,4},{7,5},{8,10},{9,11},{10,... | collective-permute-start | bytes 663560 | tf_op jit(solution)/shard_map/ppermute | solution.py:636
  13.1 10.8 %collective-permute-start.4 = (bf16[144,768]{1,0:T(8,128)(2,1)}, bf16[144,768]{1,0:T(8,128)(2,1)S(1)}, u32[]{:S(2)}, u32[]{:S(2)}) collective-permute-start(bf16[144,768]{1,0:T(8,128)(2,1)} %get-tuple-element.140), channel_id=1, source_target_pairs={{0,3},{1,2},{2,1},{3,0},{4,7},{5,6},{6,5},{7,4},{8,11},{9,10},{10,... | collective-permute-start | bytes 663560 | tf_op jit(solution)/shard_map/ppermute | solution.py:636
  26.2 16.7 %collective-permute-start.7 = (bf16[2,1376,128]{2,1,0:T(8,128)(2,1)S(1)}, bf16[2,1376,128]{2,1,0:T(8,128)(2,1)S(1)}, u32[]{:S(2)}, u32[]{:S(2)}) collective-permute-start(bf16[2,1376,128]{2,1,0:T(8,128)(2,1)S(1)} %pad_maximum_fusion), channel_id=1, source_target_pairs={{0,2},{1,3},{2,0},{3,1},{4,6},{5,7},{6,4},{7,5},{8,10},{9,11},{10,... | collective-permute-start | bytes 2113544 | tf_op jit(solution)/shard_map/ppermute | solution.py:636
  27.7 16.6 %collective-permute-start.5 = (bf16[2,1376,128]{2,1,0:T(8,128)(2,1)S(1)}, bf16[2,1376,128]{2,1,0:T(8,128)(2,1)S(1)}, u32[]{:S(2)}, u32[]{:S(2)}) collective-permute-start(bf16[2,1376,128]{2,1,0:T(8,128)(2,1)S(1)} %collective-permute-done.refs_8_), channel_id=1, source_target_pairs={{0,8},{8,16},{16,24},{24,28},{28,20},{20,12},{12,4},{4,0},{1,9},{9... | collective-permute-start | bytes 2113544 | tf_op jit(solution)/shard_map/ppermute | solution.py:684
  29.3 16.3 %collective-permute-start.6 = (bf16[2,1376,128]{2,1,0:T(8,128)(2,1)S(1)}, bf16[2,1376,128]{2,1,0:T(8,128)(2,1)S(1)}, u32[]{:S(2)}, u32[]{:S(2)}) collective-permute-start(bf16[2,1376,128]{2,1,0:T(8,128)(2,1)S(1)} %collective-permute-done.1.refs_9_), channel_id=1, source_target_pairs={{8,0},{16,8},{24,16},{28,24},{20,28},{12,20},{4,12},{0,4},{9,1},{1... | collective-permute-start | bytes 2113544 | tf_op jit(solution)/shard_map/ppermute | solution.py:687
  29.8 15.9 %collective-permute-start.8 = (bf16[2,1376,128]{2,1,0:T(8,128)(2,1)S(1)}, bf16[2,1376,128]{2,1,0:T(8,128)(2,1)S(1)}, u32[]{:S(2)}, u32[]{:S(2)}) collective-permute-start(bf16[2,1376,128]{2,1,0:T(8,128)(2,1)S(1)} %collective-permute-done.refs_8_), channel_id=1, source_target_pairs={{0,1},{1,0},{2,3},{3,2},{4,5},{5,4},{6,7},{7,6},{8,9},{9,8},{10,11... | collective-permute-start | bytes 2113544 | tf_op jit(solution)/shard_map/ppermute | solution.py:636
  29.8 15.9 %collective-permute-start.9 = (bf16[2,1376,128]{2,1,0:T(8,128)(2,1)S(1)}, bf16[2,1376,128]{2,1,0:T(8,128)(2,1)S(1)}, u32[]{:S(2)}, u32[]{:S(2)}) collective-permute-start(bf16[2,1376,128]{2,1,0:T(8,128)(2,1)S(1)} %collective-permute-done.1.refs_9_), channel_id=1, source_target_pairs={{0,1},{1,0},{2,3},{3,2},{4,5},{5,4},{6,7},{7,6},{8,9},{9,8},{10,11... | collective-permute-start | bytes 2113544 | tf_op jit(solution)/shard_map/ppermute | solution.py:636
  47.4 20.6 %collective-permute-start.10 = (bf16[2,1376,128]{2,1,0:T(8,128)(2,1)S(1)}, bf16[2,1376,128]{2,1,0:T(8,128)(2,1)S(1)}, u32[]{:S(2)}, u32[]{:S(2)}) collective-permute-start(bf16[2,1376,128]{2,1,0:T(8,128)(2,1)S(1)} %collective-permute-done.5.refs_12_), channel_id=1, source_target_pairs={{0,8},{8,16},{16,24},{24,28},{28,20},{20,12},{12,4},{4,0},{1,9},{9... | collective-permute-start | bytes 2113544 | tf_op jit(solution)/shard_map/ppermute | solution.py:684
  49.1 19.0 %collective-permute-start.11 = (bf16[2,1376,128]{2,1,0:T(8,128)(2,1)S(1)}, bf16[2,1376,128]{2,1,0:T(8,128)(2,1)S(1)}, u32[]{:S(2)}, u32[]{:S(2)}) collective-permute-start(bf16[2,1376,128]{2,1,0:T(8,128)(2,1)S(1)} %collective-permute-done.6.refs_13_), channel_id=1, source_target_pairs={{8,0},{16,8},{24,16},{28,24},{20,28},{12,20},{4,12},{0,4},{9,1},{1... | collective-permute-start | bytes 2113544 | tf_op jit(solution)/shard_map/ppermute | solution.py:687
  49.6 18.5 %collective-permute-start.14 = (bf16[2,1376,128]{2,1,0:T(8,128)(2,1)S(1)}, bf16[2,1376,128]{2,1,0:T(8,128)(2,1)S(1)}, u32[]{:S(2)}, u32[]{:S(2)}) collective-permute-start(bf16[2,1376,128]{2,1,0:T(8,128)(2,1)S(1)} %collective-permute-done.6.refs_13_), channel_id=1, source_target_pairs={{0,1},{1,0},{2,3},{3,2},{4,5},{5,4},{6,7},{7,6},{8,9},{9,8},{10,11... | collective-permute-start | bytes 2113544 | tf_op jit(solution)/shard_map/ppermute | solution.py:636
  49.7 18.4 %collective-permute-start.12 = (bf16[2,1376,128]{2,1,0:T(8,128)(2,1)S(1)}, bf16[2,1376,128]{2,1,0:T(8,128)(2,1)}, u32[]{:S(2)}, u32[]{:S(2)}) collective-permute-start(bf16[2,1376,128]{2,1,0:T(8,128)(2,1)S(1)} %pad_maximum_fusion.1), channel_id=1, source_target_pairs={{0,2},{1,3},{2,0},{3,1},{4,6},{5,7},{6,4},{7,5},{8,10},{9,11},{10,... | collective-permute-start | bytes 2113544 | tf_op jit(solution)/shard_map/ppermute | solution.py:636
  50.3 17.8 %collective-permute-start.15 = (bf16[2,1376,128]{2,1,0:T(8,128)(2,1)S(1)}, bf16[2,1376,128]{2,1,0:T(8,128)(2,1)S(1)}, u32[]{:S(2)}, u32[]{:S(2)}) collective-permute-start(bf16[2,1376,128]{2,1,0:T(8,128)(2,1)S(1)} %collective-permute-done.7.refs_14_), channel_id=1, source_target_pairs={{0,1},{1,0},{2,3},{3,2},{4,5},{5,4},{6,7},{7,6},{8,9},{9,8},{10,11... | collective-permute-start | bytes 2113544 | tf_op jit(solution)/shard_map/ppermute | solution.py:636
  69.1 20.2 %collective-permute-start.16 = (bf16[2,1376,128]{2,1,0:T(8,128)(2,1)S(1)}, bf16[2,1376,128]{2,1,0:T(8,128)(2,1)}, u32[]{:S(2)}, u32[]{:S(2)}) collective-permute-start(bf16[2,1376,128]{2,1,0:T(8,128)(2,1)S(1)} %collective-permute-done.10.refs_17_), channel_id=1, source_target_pairs={{0,8},{8,16},{16,24},{24,28},{28,20},{20,12},{12,4},{4,0},{1,9},{9... | collective-permute-start | bytes 2113544 | tf_op jit(solution)/shard_map/ppermute | solution.py:684
  70.8 18.6 %collective-permute-start.20 = (bf16[2,1376,128]{2,1,0:T(8,128)(2,1)S(1)}, bf16[2,1376,128]{2,1,0:T(8,128)(2,1)}, u32[]{:S(2)}, u32[]{:S(2)}) collective-permute-start(bf16[2,1376,128]{2,1,0:T(8,128)(2,1)S(1)} %collective-permute-done.11.refs_18_), channel_id=1, source_target_pairs={{0,1},{1,0},{2,3},{3,2},{4,5},{5,4},{6,7},{7,6},{8,9},{9,8},{10,11... | collective-permute-start | bytes 2113544 | tf_op jit(solution)/shard_map/ppermute | solution.py:636
  71.2 18.1 %collective-permute-start.18 = (bf16[2,1376,128]{2,1,0:T(8,128)(2,1)S(1)}, bf16[2,1376,128]{2,1,0:T(8,128)(2,1)}, u32[]{:S(2)}, u32[]{:S(2)}) collective-permute-start(bf16[2,1376,128]{2,1,0:T(8,128)(2,1)S(1)} %pad_maximum_fusion.2), channel_id=1, source_target_pairs={{0,2},{1,3},{2,0},{3,1},{4,6},{5,7},{6,4},{7,5},{8,10},{9,11},{10,... | collective-permute-start | bytes 2113544 | tf_op jit(solution)/shard_map/ppermute | solution.py:636
  71.8 17.5 %collective-permute-start.21 = (bf16[2,1376,128]{2,1,0:T(8,128)(2,1)}, bf16[2,1376,128]{2,1,0:T(8,128)(2,1)}, u32[]{:S(2)}, u32[]{:S(2)}) collective-permute-start(bf16[2,1376,128]{2,1,0:T(8,128)(2,1)} %collective-permute-done.12.refs_20_), channel_id=1, source_target_pairs={{0,1},{1,0},{2,3},{3,2},{4,5},{5,4},{6,7},{7,6},{8,9},{9,8},{10,11... | collective-permute-start | bytes 2113544 | tf_op jit(solution)/shard_map/ppermute | solution.py:636
  71.8 10.8 %collective-permute-start.17 = (bf16[1,1376,128]{2,1,0:T(8,128)(2,1)S(1)}, bf16[1,1376,128]{2,1,0:T(8,128)(2,1)S(1)}, u32[]{:S(2)}, u32[]{:S(2)}) collective-permute-start(bf16[1,1376,128]{2,1,0:T(8,128)(2,1)S(1)} %slice.122), channel_id=1, source_target_pairs={{8,0},{16,8},{24,16},{28,24},{20,28},{12,20},{4,12},{0,4},{9,1},{1... | collective-permute-start | bytes 1056776 | tf_op jit(solution)/shard_map/ppermute | solution.py:687
  141.1 5.4 %collective-permute-start.27 = (bf16[2,2,1344,128]{3,2,1,0:T(8,128)(2,1)}, bf16[2,2,1344,128]{3,2,1,0:T(8,128)(2,1)S(1)}, u32[]{:S(2)}, u32[]{:S(2)}) collective-permute-start(bf16[2,2,1344,128]{3,2,1,0:T(8,128)(2,1)} %get-tuple-element.176), channel_id=1, source_target_pairs={{0,1},{1,0},{2,3},{3,2},{4,5},{5,4},{6,7},{7,6},{8,9},{9,8},{10,11... | collective-permute-start | bytes 4128776 | tf_op jit(solution)/shard_map/ppermute | solution.py:636
  146.5 12.4 %collective-permute-start.32 = (bf16[5,2,1344,128]{3,2,1,0:T(8,128)(2,1)S(1)}, bf16[5,2,1344,128]{3,2,1,0:T(8,128)(2,1)S(1)}, u32[]{:S(2)}, u32[]{:S(2)}) collective-permute-start(bf16[5,2,1344,128]{3,2,1,0:T(8,128)(2,1)S(1)} %copy-done.36), channel_id=1, source_target_pairs={{0,1},{1,0},{2,3},{3,2},{4,5},{5,4},{6,7},{7,6},{8,9},{9,8},{10,11... | collective-permute-start | bytes 10321928 | tf_op jit(solution)/shard_map/ppermute | solution.py:636
  146.7 8.9 %collective-permute-start.33 = (bf16[6,2,672,128]{3,2,1,0:T(8,128)(2,1)}, bf16[6,2,672,128]{3,2,1,0:T(8,128)(2,1)S(1)}, u32[]{:S(2)}, u32[]{:S(2)}) collective-permute-start(bf16[6,2,672,128]{3,2,1,0:T(8,128)(2,1)} %get-tuple-element.186), channel_id=1, source_target_pairs={{0,1},{1,0},{2,3},{3,2},{4,5},{5,4},{6,7},{7,6},{8,9},{9,8},{10,11... | collective-permute-start | bytes 6193160 | tf_op jit(solution)/shard_map/ppermute | solution.py:636
  147.2 10.2 %collective-permute-start.29 = (bf16[1,1344,128]{2,1,0:T(8,128)(2,1)S(1)}, bf16[1,1344,128]{2,1,0:T(8,128)(2,1)S(1)}, u32[]{:S(2)}, u32[]{:S(2)}) collective-permute-start(bf16[1,1344,128]{2,1,0:T(8,128)(2,1)S(1)} %get-tuple-element.274), channel_id=1, source_target_pairs={{0,8},{8,16},{16,24},{24,28},{28,20},{20,12},{12,4},{4,0},{1,9},{9... | collective-permute-start | bytes 1032200 | tf_op jit(solution)/shard_map/ppermute | solution.py:684
  148.8 9.8 %collective-permute-start.30 = (bf16[1,1344,128]{2,1,0:T(8,128)(2,1)S(1)}, bf16[1,1344,128]{2,1,0:T(8,128)(2,1)S(1)}, u32[]{:S(2)}, u32[]{:S(2)}) collective-permute-start(bf16[1,1344,128]{2,1,0:T(8,128)(2,1)S(1)} %get-tuple-element.273), channel_id=1, source_target_pairs={{8,0},{16,8},{24,16},{28,24},{20,28},{12,20},{4,12},{0,4},{9,1},{1... | collective-permute-start | bytes 1032200 | tf_op jit(solution)/shard_map/ppermute | solution.py:687
  149.3 9.6 %collective-permute-start.31 = (bf16[2,672,128]{2,1,0:T(8,128)(2,1)S(1)}, bf16[2,672,128]{2,1,0:T(8,128)(2,1)S(1)}, u32[]{:S(2)}, u32[]{:S(2)}) collective-permute-start(bf16[2,672,128]{2,1,0:T(8,128)(2,1)S(1)} %slice_bitcast_fusion.2), channel_id=1, source_target_pairs={{0,2},{1,3},{2,0},{3,1},{4,6},{5,7},{6,4},{7,5},{8,10},{9,11},{10,... | collective-permute-start | bytes 1032200 | tf_op jit(solution)/shard_map/ppermute | solution.py:636
  158.9 12.5 %collective-permute-start.38 = (bf16[3,672,128]{2,1,0:T(8,128)(2,1)S(1)}, bf16[3,672,128]{2,1,0:T(8,128)(2,1)S(1)}, u32[]{:S(2)}, u32[]{:S(2)}) collective-permute-start(bf16[3,672,128]{2,1,0:T(8,128)(2,1)S(1)} %slice_bitcast_fusion), channel_id=1, source_target_pairs={{0,2},{1,3},{2,0},{3,1},{4,6},{5,7},{6,4},{7,5},{8,10},{9,11},{10,... | collective-permute-start | bytes 1548296 | tf_op jit(solution)/shard_map/ppermute | solution.py:636
  159.6 13.3 %collective-permute-start.36 = (bf16[336,128]{1,0:T(8,128)(2,1)S(1)}, bf16[336,128]{1,0:T(8,128)(2,1)S(1)}, u32[]{:S(2)}, u32[]{:S(2)}) collective-permute-start(bf16[336,128]{1,0:T(8,128)(2,1)S(1)} %get-tuple-element.272), channel_id=1, source_target_pairs={{0,8},{8,16},{16,24},{24,28},{28,20},{20,12},{12,4},{4,0},{1,9},{9... | collective-permute-start | bytes 258056 | tf_op jit(solution)/shard_map/ppermute | solution.py:684
  161.2 11.7 %collective-permute-start.37 = (bf16[336,128]{1,0:T(8,128)(2,1)S(1)}, bf16[336,128]{1,0:T(8,128)(2,1)S(1)}, u32[]{:S(2)}, u32[]{:S(2)}) collective-permute-start(bf16[336,128]{1,0:T(8,128)(2,1)S(1)} %get-tuple-element.271), channel_id=1, source_target_pairs={{8,0},{16,8},{24,16},{28,24},{20,28},{12,20},{4,12},{0,4},{9,1},{1... | collective-permute-start | bytes 258056 | tf_op jit(solution)/shard_map/ppermute | solution.py:687
  161.8 16.2 %collective-permute-start.34 = (bf16[2,1344,128]{2,1,0:T(8,128)(2,1)S(1)}, bf16[2,1344,128]{2,1,0:T(8,128)(2,1)S(1)}, u32[]{:S(2)}, u32[]{:S(2)}) collective-permute-start(bf16[2,1344,128]{2,1,0:T(8,128)(2,1)S(1)} %get-tuple-element.270), channel_id=1, source_target_pairs={{0,8},{8,16},{16,24},{24,28},{28,20},{20,12},{12,4},{4,0},{1,9},{9... | collective-permute-start | bytes 2064392 | tf_op jit(solution)/shard_map/ppermute | solution.py:684
  163.5 15.9 %collective-permute-start.35 = (bf16[2,1344,128]{2,1,0:T(8,128)(2,1)S(1)}, bf16[2,1344,128]{2,1,0:T(8,128)(2,1)S(1)}, u32[]{:S(2)}, u32[]{:S(2)}) collective-permute-start(bf16[2,1344,128]{2,1,0:T(8,128)(2,1)S(1)} %get-tuple-element.269), channel_id=1, source_target_pairs={{8,0},{16,8},{24,16},{28,24},{20,28},{12,20},{4,12},{0,4},{9,1},{1... | collective-permute-start | bytes 2064392 | tf_op jit(solution)/shard_map/ppermute | solution.py:687
  180.1 11.6 %collective-permute-start.44 = (bf16[3,672,128]{2,1,0:T(8,128)(2,1)}, bf16[3,672,128]{2,1,0:T(8,128)(2,1)}, u32[]{:S(2)}, u32[]{:S(2)}) collective-permute-start(bf16[3,672,128]{2,1,0:T(8,128)(2,1)} %slice_bitcast_fusion.1), channel_id=1, source_target_pairs={{0,2},{1,3},{2,0},{3,1},{4,6},{5,7},{6,4},{7,5},{8,10},{9,11},{10,... | collective-permute-start | bytes 1548296 | tf_op jit(solution)/shard_map/ppermute | solution.py:636
  182.4 10.0 %collective-permute-start.43 = (bf16[672,128]{1,0:T(8,128)(2,1)}, bf16[672,128]{1,0:T(8,128)(2,1)}, u32[]{:S(2)}, u32[]{:S(2)}) collective-permute-start(bf16[672,128]{1,0:T(8,128)(2,1)} %fusion.21), channel_id=1, source_target_pairs={{8,0},{16,8},{24,16},{28,24},{20,28},{12,20},{4,12},{0,4},{9,1},{1... | collective-permute-start | bytes 516104 | tf_op jit(solution)/shard_map/ppermute | solution.py:687
  184.3 19.4 %collective-permute-start.40 = (bf16[2,1344,128]{2,1,0:T(8,128)(2,1)}, bf16[2,1344,128]{2,1,0:T(8,128)(2,1)}, u32[]{:S(2)}, u32[]{:S(2)}) collective-permute-start(bf16[2,1344,128]{2,1,0:T(8,128)(2,1)} %get-tuple-element.264), channel_id=1, source_target_pairs={{0,8},{8,16},{16,24},{24,28},{28,20},{20,12},{12,4},{4,0},{1,9},{9... | collective-permute-start | bytes 2064392 | tf_op jit(solution)/shard_map/ppermute | solution.py:684
  185.8 17.9 %collective-permute-start.41 = (bf16[2,1344,128]{2,1,0:T(8,128)(2,1)}, bf16[2,1344,128]{2,1,0:T(8,128)(2,1)}, u32[]{:S(2)}, u32[]{:S(2)}) collective-permute-start(bf16[2,1344,128]{2,1,0:T(8,128)(2,1)} %get-tuple-element.263), channel_id=1, source_target_pairs={{8,0},{16,8},{24,16},{28,24},{20,28},{12,20},{4,12},{0,4},{9,1},{1... | collective-permute-start | bytes 2064392 | tf_op jit(solution)/shard_map/ppermute | solution.py:687
  187.0 16.2 %collective-permute-start.42 = (bf16[672,128]{1,0:T(8,128)(2,1)}, bf16[672,128]{1,0:T(8,128)(2,1)}, u32[]{:S(2)}, u32[]{:S(2)}) collective-permute-start(bf16[672,128]{1,0:T(8,128)(2,1)} %fusion.23), channel_id=1, source_target_pairs={{0,8},{8,16},{16,24},{24,28},{28,20},{20,12},{12,4},{4,0},{1,9},{9... | collective-permute-start | bytes 516104 | tf_op jit(solution)/shard_map/ppermute | solution.py:684
  191.8 11.9 %collective-permute-start.45 = (f32[4,24,96]{2,1,0:T(8,128)S(1)}, f32[4,24,96]{2,1,0:T(8,128)S(1)}, u32[]{:S(2)}, u32[]{:S(2)}) collective-permute-start(f32[4,24,96]{2,1,0:T(8,128)S(1)} %get-tuple-element.277), channel_id=1, source_target_pairs={{0,4},{1,5},{2,6},{3,7},{4,0},{5,1},{6,2},{7,3},{8,12},{9,13},{10,... | collective-permute-start | bytes 110600 | tf_op jit(solution)/shard_map/ppermute | solution.py:641
  205.4 18.9 %collective-permute-start.46 = (bf16[2,1344,128]{2,1,0:T(8,128)(2,1)S(1)}, bf16[2,1344,128]{2,1,0:T(8,128)(2,1)S(1)}, u32[]{:S(2)}, u32[]{:S(2)}) collective-permute-start(bf16[2,1344,128]{2,1,0:T(8,128)(2,1)S(1)} %get-tuple-element.262), channel_id=1, source_target_pairs={{0,8},{8,16},{16,24},{24,28},{28,20},{20,12},{12,4},{4,0},{1,9},{9... | collective-permute-start | bytes 2064392 | tf_op jit(solution)/shard_map/ppermute | solution.py:684
  206.1 18.2 %collective-permute-start.47 = (bf16[2,1344,128]{2,1,0:T(8,128)(2,1)S(1)}, bf16[2,1344,128]{2,1,0:T(8,128)(2,1)S(1)}, u32[]{:S(2)}, u32[]{:S(2)}) collective-permute-start(bf16[2,1344,128]{2,1,0:T(8,128)(2,1)S(1)} %get-tuple-element.261), channel_id=1, source_target_pairs={{8,0},{16,8},{24,16},{28,24},{20,28},{12,20},{4,12},{0,4},{9,1},{1... | collective-permute-start | bytes 2064392 | tf_op jit(solution)/shard_map/ppermute | solution.py:687
  208.9 15.5 %collective-permute-start.48 = (bf16[672,128]{1,0:T(8,128)(2,1)S(1)}, bf16[672,128]{1,0:T(8,128)(2,1)S(1)}, u32[]{:S(2)}, u32[]{:S(2)}) collective-permute-start(bf16[672,128]{1,0:T(8,128)(2,1)S(1)} %get-tuple-element.268), channel_id=1, source_target_pairs={{0,8},{8,16},{16,24},{24,28},{28,20},{20,12},{12,4},{4,0},{1,9},{9... | collective-permute-start | bytes 516104 | tf_op jit(solution)/shard_map/ppermute | solution.py:684
  209.5 14.8 %collective-permute-start.49 = (bf16[672,128]{1,0:T(8,128)(2,1)S(1)}, bf16[672,128]{1,0:T(8,128)(2,1)S(1)}, u32[]{:S(2)}, u32[]{:S(2)}) collective-permute-start(bf16[672,128]{1,0:T(8,128)(2,1)S(1)} %get-tuple-element.267), channel_id=1, source_target_pairs={{8,0},{16,8},{24,16},{28,24},{20,28},{12,20},{4,12},{0,4},{9,1},{1... | collective-permute-start | bytes 516104 | tf_op jit(solution)/shard_map/ppermute | solution.py:687
  210.9 13.4 %collective-permute-start.50 = (f32[2,24,96]{2,1,0:T(8,128)S(1)}, f32[2,24,96]{2,1,0:T(8,128)S(1)}, u32[]{:S(2)}, u32[]{:S(2)}) collective-permute-start(f32[2,24,96]{2,1,0:T(8,128)S(1)} %get-tuple-element.279), channel_id=1, source_target_pairs={{0,8},{1,9},{2,10},{3,11},{4,12},{5,13},{6,14},{7,15},{8,0},{9,1},... | collective-permute-start | bytes 55304 | tf_op jit(solution)/shard_map/ppermute | solution.py:641
  224.6 13.2 %collective-permute-start.51 = (bf16[2,1344,128]{2,1,0:T(8,128)(2,1)S(1)}, bf16[2,1344,128]{2,1,0:T(8,128)(2,1)S(1)}, u32[]{:S(2)}, u32[]{:S(2)}) collective-permute-start(bf16[2,1344,128]{2,1,0:T(8,128)(2,1)S(1)} %fusion.3), channel_id=1, source_target_pairs={{0,2},{1,3},{2,0},{3,1},{4,6},{5,7},{6,4},{7,5},{8,10},{9,11},{10,... | collective-permute-start | bytes 2064392 | tf_op jit(solution)/shard_map/ppermute | solution.py:636
  226.5 7.7 %collective-permute-start.52 = (bf16[672,128]{1,0:T(8,128)(2,1)S(1)}, bf16[672,128]{1,0:T(8,128)(2,1)S(1)}, u32[]{:S(2)}, u32[]{:S(2)}) collective-permute-start(bf16[672,128]{1,0:T(8,128)(2,1)S(1)} %get-tuple-element.266), channel_id=1, source_target_pairs={{0,8},{8,16},{16,24},{24,28},{28,20},{20,12},{12,4},{4,0},{1,9},{9... | collective-permute-start | bytes 516104 | tf_op jit(solution)/shard_map/ppermute | solution.py:684
  226.9 7.4 %collective-permute-start.53 = (bf16[672,128]{1,0:T(8,128)(2,1)S(1)}, bf16[672,128]{1,0:T(8,128)(2,1)S(1)}, u32[]{:S(2)}, u32[]{:S(2)}) collective-permute-start(bf16[672,128]{1,0:T(8,128)(2,1)S(1)} %get-tuple-element.265), channel_id=1, source_target_pairs={{8,0},{16,8},{24,16},{28,24},{20,28},{12,20},{4,12},{0,4},{9,1},{1... | collective-permute-start | bytes 516104 | tf_op jit(solution)/shard_map/ppermute | solution.py:687
  228.6 5.6 %collective-permute-start.54 = (f32[24,96]{1,0:T(8,128)S(1)}, f32[24,96]{1,0:T(8,128)S(1)}, u32[]{:S(2)}, u32[]{:S(2)}) collective-permute-start(f32[24,96]{1,0:T(8,128)S(1)} %get-tuple-element.281), channel_id=1, source_target_pairs={{0,16},{1,17},{2,18},{3,19},{4,20},{5,21},{6,22},{7,23},{8,24},{9,... | collective-permute-start | bytes 27656 | tf_op jit(solution)/shard_map/ppermute | solution.py:641
  239.9 6.8 %collective-permute-start.56 = (bf16[2,1344,128]{2,1,0:T(8,128)(2,1)S(1)}, bf16[2,1344,128]{2,1,0:T(8,128)(2,1)S(1)}, u32[]{:S(2)}, u32[]{:S(2)}) collective-permute-start(bf16[2,1344,128]{2,1,0:T(8,128)(2,1)S(1)} %get-tuple-element.236.own), channel_id=1, source_target_pairs={{0,1},{1,0},{2,3},{3,2},{4,5},{5,4},{6,7},{7,6},{8,9},{9,8},{10,11... | collective-permute-start | bytes 2064392 | tf_op jit(solution)/shard_map/ppermute | solution.py:636
  239.9 6.8 %collective-permute-start.55 = (bf16[672,128]{1,0:T(8,128)(2,1)S(1)}, bf16[672,128]{1,0:T(8,128)(2,1)S(1)}, u32[]{:S(2)}, u32[]{:S(2)}) collective-permute-start(bf16[672,128]{1,0:T(8,128)(2,1)S(1)} %fusion.19), channel_id=1, source_target_pairs={{0,2},{1,3},{2,0},{3,1},{4,6},{5,7},{6,4},{7,5},{8,10},{9,11},{10,... | collective-permute-start | bytes 516104 | tf_op jit(solution)/shard_map/ppermute | solution.py:636
  250.2 10.8 %collective-permute-start.63 = (bf16[1344,128]{1,0:T(8,128)(2,1)S(1)}, bf16[1344,128]{1,0:T(8,128)(2,1)S(1)}, u32[]{:S(2)}, u32[]{:S(2)}) collective-permute-start(bf16[1344,128]{1,0:T(8,128)(2,1)S(1)} %get-tuple-element.256.split_own), channel_id=1, source_target_pairs={{0,1},{1,0},{2,3},{3,2},{4,5},{5,4},{6,7},{7,6},{8,9},{9,8},{10,11... | collective-permute-start | bytes 1032200 | tf_op jit(solution)/shard_map/ppermute | solution.py:636
  (54 other events, 347.6 us)
